TPU v7x, 32 devices: a whole 2x2x4 slice. The times are simulated.
32 devices in a mesh: dp: 8 (over z, core), seq: 4 (over y, x).
Axes of the slice: x: 2, y: 2, z: 4, core: 2. Of those that a mesh axis runs over, the one named last changes fastest.
Arguments:
- enc_final: bfloat16 [8, 96, 4096], P('dp', 'seq'), may hold values from -6 to 6
- norm_gain: float32 [4096], replicated, may hold values from 0.1 to 1.9
- dec_queries: bfloat16 [2, 8, 512, 2048], P(None, 'dp', 'seq'), may hold values from -48 to 48
- out_grad: bfloat16 [2, 8, 512, 2048], P(None, 'dp', 'seq'), may hold values from -6 to 6
- enc_keys: bfloat16 [2, 8, 96, 2048], P(None, 'dp', 'seq'), may hold values from -6 to 6
- enc_values: bfloat16 [2, 8, 96, 2048], P(None, 'dp', 'seq'), may hold values from -6 to 6
- key_weight: bfloat16 [2, 4096, 2048], P(None, None, 'seq'), may hold values from -0.09375 to 0.09375
- value_weight: bfloat16 [2, 4096, 2048], P(None, None, 'seq'), may hold values from -0.09375 to 0.09375
Outputs:
- enc_grad: bfloat16 [8, 96, 4096], P('dp', 'seq')
- gain_grad: float32 [4096], replicated
All inputs are finite; a program needn't handle non-finite values.
Results may differ from a plain program's by a relative error of at most 0.007.
Values may be sent and summed in bfloat16 or wider, within the bound.
No kernel may reach another device: no remote copies, remote signals or barrier semaphores. Data moves between devices by JAX's collectives and lax.ppermute only.
A program may use at most 128 MiB of HBM per device.

v0:
```python
import jax
import jax.numpy as jnp
from jax import lax
from jax.experimental import pallas as pl
from jax.experimental.pallas import tpu as pltpu
from jax.sharding import PartitionSpec as P


HEAD_DIM = 64
LANES = 128
PROJ_BLOCK = 1024
ATTN_ROWS = 512
PACK_VMEM = 8 << 20
LAYER_VMEM = 24 << 20
LOAD_VMEM = 8 << 20
SMALL_VMEM = 2 << 20
F32 = jnp.float32
BF16 = jnp.bfloat16


def xor_pairs(size, step):
    return [(i, i ^ step) for i in range(size)]


def exchange(value, axis, size, step):
    return lax.ppermute(value, axis, xor_pairs(size, step))


def plan_chunks(layers, cols):
    chunks = [(layer, 0, cols) for layer in range(layers)]
    if cols > LANES:
        chunks[-1:] = [(layers - 1, 0, cols - LANES), (layers - 1, cols - LANES, LANES)]
    return chunks


def in_hbm(arrays):
    return [pltpu.with_memory_space_constraint(a, pltpu.HBM) for a in arrays]


def pack_chunk(chunk, arrays, seq_size):
    layer, first, width = chunk
    rows = [a.shape[2] for a in arrays]
    cols = arrays[0].shape[3] // seq_size

    def kernel(q_ref, g_ref, k_ref, v_ref, *rest):
        outs, sems = rest[:seq_size], rest[seq_size]
        me = lax.axis_index("seq")
        copies = []
        for j in list(range(1, seq_size)) + [0]:
            start = pl.multiple_of((me ^ j) * cols + first, LANES)
            base = 0
            for i, ref in enumerate((q_ref, g_ref, k_ref, v_ref)):
                copies.append(
                    pltpu.make_async_copy(
                        ref.at[layer, 0, :, pl.ds(start, width)],
                        outs[j].at[pl.ds(base, rows[i]), :],
                        sems.at[j, i],
                    )
                )
                base += rows[i]
        for c in copies:
            c.start()
        for c in copies:
            c.wait()

    return pl.pallas_call(
        kernel,
        out_shape=[jax.ShapeDtypeStruct((sum(rows), width), BF16)] * seq_size,
        in_specs=[pl.BlockSpec(memory_space=pltpu.HBM)] * 4,
        out_specs=[pl.BlockSpec(memory_space=pltpu.VMEM)] * seq_size,
        scratch_shapes=[pltpu.SemaphoreType.DMA((seq_size, 4))],
        compiler_params=pltpu.CompilerParams(vmem_limit_bytes=PACK_VMEM),
    )(*in_hbm(arrays))


def load_weights(chunks, key_weight, value_weight, after):
    width = key_weight.shape[1]

    def kernel(kw, vw, after_ref, *rest):
        outs, sems = rest[: len(chunks)], rest[len(chunks)]
        copies = []
        for n, (layer, first, cols) in enumerate(chunks):
            for i, src in enumerate((kw, vw)):
                copies.append(
                    pltpu.make_async_copy(
                        src.at[layer, :, pl.ds(first, cols)],
                        outs[n].at[:, pl.ds(i * cols, cols)],
                        sems.at[n, i],
                    )
                )
        for c in copies:
            c.start()
        for c in copies:
            c.wait()

    total = 4 * key_weight.size
    return pl.pallas_call(
        kernel,
        out_shape=[jax.ShapeDtypeStruct((width, 2 * cols), BF16) for _, _, cols in chunks],
        in_specs=[pl.BlockSpec(memory_space=pltpu.HBM)] * 2 + [pl.BlockSpec(memory_space=pl.ANY)],
        out_specs=[pl.BlockSpec(memory_space=pltpu.VMEM)] * len(chunks),
        scratch_shapes=[pltpu.SemaphoreType.DMA((len(chunks), 2))],
        compiler_params=pltpu.CompilerParams(vmem_limit_bytes=LOAD_VMEM),
        cost_estimate=pl.CostEstimate(flops=0, transcendentals=0, bytes_accessed=total),
        name="load_weights",
    )(*in_hbm([key_weight, value_weight]), after)


def attention_into(bufs, dec, enc, kv_ref):
    cols = bufs[0].shape[1]
    count = len(bufs)
    per = LANES // HEAD_DIM
    group = max(1, ATTN_ROWS // dec)
    lane_head = lax.broadcasted_iota(jnp.int32, (1, LANES), 1) // HEAD_DIM
    rows = enc * count

    def stacked(base, ls):
        whole = jnp.concatenate([b[base : base + enc, ls].astype(F32) for b in bufs], axis=0)
        parts = [jnp.where(lane_head == h, whole, 0.0) for h in range(per)]
        return jnp.concatenate(parts, axis=0).astype(BF16)

    def chosen(stack):
        out = stack[:rows]
        for h in range(1, per):
            out = jnp.where(lane_head == h, stack[h * rows : (h + 1) * rows], out)
        return out.astype(BF16)

    nt = (((1,), (1,)), ((), ()))
    nn = (((1,), (0,)), ((), ()))
    for p in range(cols // LANES):
        ls = slice(p * LANES, (p + 1) * LANES)
        keys = stacked(2 * dec, ls)
        values = stacked(2 * dec + enc, ls)
        key_sum = value_sum = None
        for first in range(0, count, group):
            some = bufs[first : first + group]
            q = jnp.concatenate([b[0:dec, ls] for b in some], axis=0)
            g = jnp.concatenate([b[dec : 2 * dec, ls] for b in some], axis=0)
            width = q.shape[0]
            s = lax.dot_general(keys, q, nt, preferred_element_type=F32).reshape(per, rows, width)
            d = lax.dot_general(values, g, nt, preferred_element_type=F32).reshape(per, rows, width)
            e = jnp.exp(s - jnp.max(s, axis=1, keepdims=True))
            w = e * (1.0 / jnp.sum(e, axis=1, keepdims=True))
            delta = jnp.sum(w * d, axis=1, keepdims=True)
            ds = (w * (d - delta)).astype(BF16).reshape(per * rows, width)
            wl = w.astype(BF16).reshape(per * rows, width)
            vg = lax.dot_general(wl, g, nn, preferred_element_type=F32)
            kg = lax.dot_general(ds, q, nn, preferred_element_type=F32)
            key_sum = kg if key_sum is None else key_sum + kg
            value_sum = vg if value_sum is None else value_sum + vg
        kv_ref[:, ls] = chosen(key_sum)
        kv_ref[:, cols + p * LANES : cols + (p + 1) * LANES] = chosen(value_sum)


def chunk_terms(bufs, weight, prior, dec, enc, last):
    count = len(bufs)
    width = weight.shape[0]
    rows = enc * count
    block = PROJ_BLOCK

    def kernel(*refs):
        buf_refs, w_ref = refs[:count], refs[count]
        pos = count + 1
        if prior is not None:
            prior_ref = refs[pos]
            pos += 1
        outs, kv_ref = refs[pos:-1], refs[-1]
        attention_into(buf_refs, dec, enc, kv_ref)
        nt = (((1,), (1,)), ((), ()))
        for b in range(width // block):
            bs = slice(b * block, (b + 1) * block)
            acc = lax.dot_general(kv_ref[...], w_ref[bs, :], nt, preferred_element_type=F32)
            if prior is not None:
                acc += prior_ref[:, bs]
            if last:
                for j in range(count):
                    outs[j][:, bs] = acc[j * enc : (j + 1) * enc].astype(outs[j].dtype)
            else:
                outs[0][:, bs] = acc

    if last:
        out_shape = [jax.ShapeDtypeStruct((enc, width), F32 if j == 0 else BF16) for j in range(count)]
    else:
        out_shape = [jax.ShapeDtypeStruct((rows, width), F32)]
    vmem = pl.BlockSpec(memory_space=pltpu.VMEM)
    operands = list(bufs) + [weight] + ([] if prior is None else [prior])
    return pl.pallas_call(
        kernel,
        out_shape=out_shape,
        in_specs=[vmem] * len(operands),
        out_specs=[vmem] * len(out_shape),
        scratch_shapes=[pltpu.VMEM((rows, weight.shape[1]), BF16)],
        compiler_params=pltpu.CompilerParams(vmem_limit_bytes=LAYER_VMEM),
    )(*operands)


def split_final(enc_final, after):
    enc, half = enc_final.shape[1], enc_final.shape[2] // 2

    def kernel(src, after_ref, *rest):
        outs, sems = rest[:2], rest[2]
        copies = [
            pltpu.make_async_copy(src.at[0, :, pl.ds(h * half, half)], outs[h], sems.at[h])
            for h in range(2)
        ]
        for c in copies:
            c.start()
        for c in copies:
            c.wait()

    return pl.pallas_call(
        kernel,
        out_shape=[jax.ShapeDtypeStruct((enc, half), BF16)] * 2,
        in_specs=[pl.BlockSpec(memory_space=pltpu.HBM), pl.BlockSpec(memory_space=pl.ANY)],
        out_specs=[pl.BlockSpec(memory_space=pltpu.VMEM)] * 2,
        scratch_shapes=[pltpu.SemaphoreType.DMA((2,))],
        compiler_params=pltpu.CompilerParams(vmem_limit_bytes=SMALL_VMEM),
        name="split_final",
    )(*in_hbm([enc_final]), after)


def gather_rows(mine, seq_size, steps):
    have = [(0, mine)]
    for n, step in enumerate(steps):
        whole = have[0][1] if n == 0 else jnp.concatenate([a for _, a in have], axis=0)
        have = have + [(step, exchange(whole, "seq", seq_size, step))]
    return have


def row_order(steps):
    order = [0]
    for step in steps:
        order = order + [j ^ step for j in order]
    return order


def gain_terms(pieces, halves, orders):
    count = len(pieces)
    enc, width = pieces[0].shape
    half = width // 2
    sizes = [len(parts) for parts in halves]

    def kernel(*refs):
        piece_refs = refs[:count]
        part_refs = [refs[count : count + sizes[0]], refs[count + sizes[0] : count + sum(sizes)]]
        out_ref = refs[-1]
        blocks = [[None] * count, [None] * count]
        for h in range(2):
            place = 0
            for ref in part_refs[h]:
                for k in range(ref.shape[0] // enc):
                    blocks[h][orders[h][place]] = (ref, k * enc)
                    place += 1
        inv = []
        for j in range(count):
            square = None
            for h in range(2):
                ref, base = blocks[h][j]
                x = ref[pl.ds(base, enc), :].astype(F32)
                total = jnp.sum(x * x, axis=-1, keepdims=True)
                square = total if square is None else square + total
            inv.append(lax.rsqrt(square * (1.0 / width) + 1e-06))
        for h in range(2):
            hs = slice(h * half, (h + 1) * half)
            terms = None
            for j in range(count):
                ref, base = blocks[h][j]
                normed = ref[pl.ds(base, enc), :].astype(F32) * inv[j]
                product = piece_refs[j][:, hs].astype(F32) * normed
                terms = product if terms is None else terms + product
            out_ref[:, hs] = jnp.sum(terms, axis=0, keepdims=True)

    return pl.pallas_call(
        kernel,
        out_shape=jax.ShapeDtypeStruct((1, width), F32),
        compiler_params=pltpu.CompilerParams(vmem_limit_bytes=PACK_VMEM),
        name="gain_terms",
    )(*pieces, *[a for parts in halves for a in parts])


def finish(own, received, enc_final, norm_gain):
    enc, width = own.shape

    def kernel(own_ref, *refs):
        recv_refs = refs[: len(received)]
        final_ref, gain_ref, grad_ref = refs[len(received) :]
        state = own_ref[...]
        for r in recv_refs:
            state = state + r[...].astype(F32)
        final = final_ref[0].astype(F32)
        inv_rms = lax.rsqrt(jnp.mean(final * final, axis=-1, keepdims=True) + 1e-06)
        normed = final * inv_rms
        scaled = gain_ref[...] * state
        mean = jnp.mean(scaled * normed, axis=-1, keepdims=True)
        grad_ref[0] = (inv_rms * (scaled - normed * mean)).astype(BF16)

    return pl.pallas_call(
        kernel,
        out_shape=jax.ShapeDtypeStruct((1, enc, width), BF16),
        compiler_params=pltpu.CompilerParams(vmem_limit_bytes=PACK_VMEM),
        name="finish",
    )(own, *received, enc_final, norm_gain.reshape(1, width))


def body(
    enc_final, norm_gain, dec_queries, out_grad, enc_keys, enc_values, key_weight, value_weight
):
    seq = lax.axis_size("seq")
    docs = lax.axis_size("dp")
    layers = dec_queries.shape[0]
    dec, enc = dec_queries.shape[2], enc_keys.shape[2]
    arrays = (dec_queries, out_grad, enc_keys, enc_values)
    chunks = plan_chunks(layers, key_weight.shape[2])
    gathered = []
    for index, chunk in enumerate(chunks):
        bufs = pack_chunk(chunk, arrays, seq)
        gathered.append([bufs[0]] + [exchange(bufs[j], "seq", seq, j) for j in range(1, seq)])
        if index == 0:
            steps = [1 << b for b in range(seq.bit_length() - 1)]
            orders = [steps, steps[::-1]]
            finals = split_final(enc_final, bufs[0])
            halves = [gather_rows(f, seq, o) for f, o in zip(finals, orders)]
    weights = load_weights(chunks, key_weight, value_weight, gathered[-1][0])
    prior = None
    for index in range(len(chunks)):
        outs = chunk_terms(
            gathered[index], weights[index], prior, dec, enc, index == len(chunks) - 1
        )
        prior = outs[0]
    received = [exchange(outs[j], "seq", seq, j) for j in range(1, seq)]
    gain = gain_terms(
        outs, [[a for _, a in parts] for parts in halves], [row_order(o) for o in orders]
    )
    enc_grad = finish(outs[0], received, enc_final, norm_gain)
    stages = [
        (axis, size, 1 << b)
        for axis, size in (("dp", docs), ("seq", seq))
        for b in range(size.bit_length() - 1)
    ]
    for axis, size, step in stages:
        gain = gain + exchange(gain, axis, size, step)
    return (enc_grad, gain[0] / docs)


def solution(mesh):
    placed = (
        P("dp", "seq", None),
        P(),
        P(None, "dp", "seq", None),
        P(None, "dp", "seq", None),
        P(None, "dp", "seq", None),
        P(None, "dp", "seq", None),
        P(None, None, "seq"),
        P(None, None, "seq"),
    )

    def whole(*args):
        step = jax.shard_map(
            body, mesh=mesh, in_specs=placed, out_specs=(P("dp", "seq", None), P()), check_vma=False
        )
        return step(*args)

    return whole
```

profile of v0, /device:TPU:0, one launch (start us, length us, event | category | flops | bytes accessed | tf_op | source)
XLA Modules:
  0.0 83.3 jit_solution(1641822558351862784)
XLA Ops:
  0.6 1.5 %shard_map.97 = (bf16[304,512]{1,0:T(8,128)(2,1)S(1)}, bf16[304,512]{1,0:T(8,128)(2,1)S(1)}, bf16[304,512]{1,0:T(8,128)(2,1)S(1)}, bf16[304,512]{1,0:T(8,128)(2,1)S(1)}) custom-call(bf16[2,1,128,2048]{3,2,1,0:T(8,128)(2,1)} %q_ref.5, bf16[2,1,128,2048]{3,2,1,0:T(8,128)(2,1)} %g_ref.5, bf16[2,1,24,2048]{3,2,1,0:T(8,128)(2,1)} %k_ref.5, ...), custom_call_target="tpu_custom_call" | custom-call | tf_op jit(solution)/shard_map/pallas_call | solution.py:66
  2.2 1.0 %split_final.1 = (bf16[24,2048]{1,0:T(8,128)(2,1)S(1)}, bf16[24,2048]{1,0:T(8,128)(2,1)S(1)}) custom-call(bf16[1,24,4096]{2,1,0:T(8,128)(2,1)} %src.1, bf16[304,512]{1,0:T(8,128)(2,1)S(1)} %get-tuple-element.33.refs_0_.after_ref), custom_call_target="tpu_custom_call" | custom-call | tf_op jit(solution)/shard_map/split_final/pallas_call | solution.py:211
  3.1 3.0 %collective-permute-start.12 = (bf16[24,2048]{1,0:T(8,128)(2,1)S(1)}, bf16[24,2048]{1,0:T(8,128)(2,1)S(1)}, u32[]{:S(2)}, u32[]{:S(2)}) collective-permute-start(bf16[24,2048]{1,0:T(8,128)(2,1)S(1)} %get-tuple-element.42.refs_4_), channel_id=1, source_target_pairs={{0,1},{1,0},{2,3},{3,2},{4,5},{5,4},{6,7},{7,6},{8,9},{9,8},{10,11... | collective-permute-start | bytes 294920 | tf_op jit(solution)/shard_map/ppermute | solution.py:26
  6.2 1.4 %shard_map.96 = (bf16[304,384]{1,0:T(8,128)(2,1)S(1)}, bf16[304,384]{1,0:T(8,128)(2,1)S(1)}, bf16[304,384]{1,0:T(8,128)(2,1)S(1)}, bf16[304,384]{1,0:T(8,128)(2,1)S(1)}) custom-call(bf16[2,1,128,2048]{3,2,1,0:T(8,128)(2,1)} %q_ref.5, bf16[2,1,128,2048]{3,2,1,0:T(8,128)(2,1)} %g_ref.5, bf16[2,1,24,2048]{3,2,1,0:T(8,128)(2,1)} %k_ref.5, ...), custom_call_target="tpu_custom_call" | custom-call | tf_op jit(solution)/shard_map/pallas_call | solution.py:66
  7.6 0.1 collective-permute-start.3
  7.7 2.0 %collective-permute-start.6 = (bf16[304,512]{1,0:T(8,128)(2,1)S(1)}, bf16[304,512]{1,0:T(8,128)(2,1)S(1)}, u32[]{:S(2)}, u32[]{:S(2)}) collective-permute-start(bf16[304,512]{1,0:T(8,128)(2,1)S(1)} %get-tuple-element.34), channel_id=1, source_target_pairs={{0,1},{1,0},{2,3},{3,2},{4,5},{5,4},{6,7},{7,6},{8,9},{9,8},{10,11... | collective-permute-start | bytes 933896 | tf_op jit(solution)/shard_map/ppermute | solution.py:26
  9.7 1.5 %collective-permute-start.4 = (bf16[304,384]{1,0:T(8,128)(2,1)S(1)}, bf16[304,384]{1,0:T(8,128)(2,1)S(1)}, u32[]{:S(2)}, u32[]{:S(2)}) collective-permute-start(bf16[304,384]{1,0:T(8,128)(2,1)S(1)} %get-tuple-element.30), channel_id=1, source_target_pairs={{0,2},{1,3},{2,0},{3,1},{4,6},{5,7},{6,4},{7,5},{8,10},{9,11},{10,... | collective-permute-start | bytes 700424 | tf_op jit(solution)/shard_map/ppermute | solution.py:26
  11.2 0.0 collective-permute-start.5
  11.2 0.0 collective-permute-done.12.refs_5_
  11.2 2.0 %collective-permute-start.14 = (bf16[24,2048]{1,0:T(8,128)(2,1)S(1)}, bf16[24,2048]{1,0:T(8,128)(2,1)S(1)}, u32[]{:S(2)}, u32[]{:S(2)}) collective-permute-start(bf16[24,2048]{1,0:T(8,128)(2,1)S(1)} %get-tuple-element.43.refs_7_), channel_id=1, source_target_pairs={{0,2},{1,3},{2,0},{3,1},{4,6},{5,7},{6,4},{7,5},{8,10},{9,11},{10,... | collective-permute-start | bytes 294920 | tf_op jit(solution)/shard_map/ppermute | solution.py:26
  13.2 5.2 %collective-permute-done.14.refs_8_ = bf16[24,2048]{1,0:T(8,128)(2,1)S(1)} collective-permute-done((bf16[24,2048]{1,0:T(8,128)(2,1)S(1)}, bf16[24,2048]{1,0:T(8,128)(2,1)S(1)}, u32[]{:S(2)}, u32[]{:S(2)}) %collective-permute-start.14) | collective-permute-done | bytes 98336 | tf_op jit(solution)/shard_map/ppermute | solution.py:26
  18.4 1.5 %collective-permute-start.7 = (bf16[304,512]{1,0:T(8,128)(2,1)S(1)}, bf16[304,512]{1,0:T(8,128)(2,1)S(1)}, u32[]{:S(2)}, u32[]{:S(2)}) collective-permute-start(bf16[304,512]{1,0:T(8,128)(2,1)S(1)} %get-tuple-element.35), channel_id=1, source_target_pairs={{0,2},{1,3},{2,0},{3,1},{4,6},{5,7},{6,4},{7,5},{8,10},{9,11},{10,... | collective-permute-start | bytes 933896 | tf_op jit(solution)/shard_map/ppermute | solution.py:26
  19.9 0.0 collective-permute-done.3.refs_1_
  19.9 0.3 collective-permute-start.8
  20.2 1.8 %collective-permute-start.13 = (bf16[48,2048]{1,0:T(8,128)(2,1)S(1)}, bf16[48,2048]{1,0:T(8,128)(2,1)S(1)}, u32[]{:S(2)}, u32[]{:S(2)}) collective-permute-start(bf16[48,2048]{1,0:T(8,128)(2,1)S(1)} %pad_maximum_fusion), channel_id=1, source_target_pairs={{0,2},{1,3},{2,0},{3,1},{4,6},{5,7},{6,4},{7,5},{8,10},{9,11},{10,... | collective-permute-start | bytes 589832 | tf_op jit(solution)/shard_map/ppermute | solution.py:26
  22.0 7.0 %collective-permute-done.5.refs_3_ = bf16[304,384]{1,0:T(8,128)(2,1)S(1)} collective-permute-done((bf16[304,384]{1,0:T(8,128)(2,1)S(1)}, bf16[304,384]{1,0:T(8,128)(2,1)S(1)}, u32[]{:S(2)}, u32[]{:S(2)}) %collective-permute-start.5) | collective-permute-done | bytes 233504 | tf_op jit(solution)/shard_map/ppermute | solution.py:26
  29.0 0.5 collective-permute-start.15
  29.5 1.1 %shard_map.95 = (bf16[304,128]{1,0:T(8,128)(2,1)S(1)}, bf16[304,128]{1,0:T(8,128)(2,1)S(1)}, bf16[304,128]{1,0:T(8,128)(2,1)S(1)}, bf16[304,128]{1,0:T(8,128)(2,1)S(1)}) custom-call(bf16[2,1,128,2048]{3,2,1,0:T(8,128)(2,1)} %q_ref.5, bf16[2,1,128,2048]{3,2,1,0:T(8,128)(2,1)} %g_ref.5, bf16[2,1,24,2048]{3,2,1,0:T(8,128)(2,1)} %k_ref.5, ...), custom_call_target="tpu_custom_call" | custom-call | tf_op jit(solution)/shard_map/pallas_call | solution.py:66
  30.6 1.6 %collective-permute-start = (bf16[304,128]{1,0:T(8,128)(2,1)S(1)}, bf16[304,128]{1,0:T(8,128)(2,1)S(1)}, u32[]{:S(2)}, u32[]{:S(2)}) collective-permute-start(bf16[304,128]{1,0:T(8,128)(2,1)S(1)} %get-tuple-element.24), channel_id=1, source_target_pairs={{0,1},{1,0},{2,3},{3,2},{4,5},{5,4},{6,7},{7,6},{8,9},{9,8},{10,11... | collective-permute-start | bytes 233480 | tf_op jit(solution)/shard_map/ppermute | solution.py:26
  32.2 7.7 %collective-permute-done.7.refs_2_ = bf16[304,512]{1,0:T(8,128)(2,1)S(1)} collective-permute-done((bf16[304,512]{1,0:T(8,128)(2,1)S(1)}, bf16[304,512]{1,0:T(8,128)(2,1)S(1)}, u32[]{:S(2)}, u32[]{:S(2)}) %collective-permute-start.7) | collective-permute-done | bytes 311328 | tf_op jit(solution)/shard_map/ppermute | solution.py:26
  39.8 1.8 %collective-permute-start.1 = (bf16[304,128]{1,0:T(8,128)(2,1)S(1)}, bf16[304,128]{1,0:T(8,128)(2,1)S(1)}, u32[]{:S(2)}, u32[]{:S(2)}) collective-permute-start(bf16[304,128]{1,0:T(8,128)(2,1)S(1)} %get-tuple-element.25), channel_id=1, source_target_pairs={{0,2},{1,3},{2,0},{3,1},{4,6},{5,7},{6,4},{7,5},{8,10},{9,11},{10,... | collective-permute-start | bytes 233480 | tf_op jit(solution)/shard_map/ppermute | solution.py:26
  41.7 0.7 collective-permute-start.2
  42.4 5.8 %load_weights.1 = (bf16[4096,1024]{1,0:T(8,128)(2,1)S(1)}, bf16[4096,768]{1,0:T(8,128)(2,1)S(1)}, bf16[4096,256]{1,0:T(8,128)(2,1)S(1)}) custom-call(bf16[2,4096,512]{2,1,0:T(8,128)(2,1)} %kw.1, bf16[2,4096,512]{2,1,0:T(8,128)(2,1)} %vw.1, bf16[304,128]{1,0:T(8,128)(2,1)S(1)} %get-tuple-element.23.after_ref.refs_0_), custom_call_target="tpu_custom_call" | custom-call | bytes 16777216 | tf_op jit(solution)/shard_map/load_weights/pallas_call | solution.py:97
  48.2 4.2 %shard_map.98.refs_5_ = f32[96,4096]{1,0:T(8,128)S(1)} custom-call(bf16[304,512]{1,0:T(8,128)(2,1)S(1)} %get-tuple-element.33.refs_0_.after_ref, bf16[304,512]{1,0:T(8,128)(2,1)S(1)} %collective-permute-done.6.refs_1_, bf16[304,512]{1,0:T(8,128)(2,1)S(1)} %collective-permute-done.7.refs_2_, bf16[304,512]{1,0:T(8,128)(2,1)S(1)} %collective-permute-done.8.refs_3_, ...), custom_call_target="tpu_custom_call" | custom-call | tf_op jit(solution)/shard_map/pallas_call | solution.py:187
  52.5 0.0 copy-start
  52.5 0.0 copy-start.1
  52.5 3.2 %shard_map.99.refs_5_ = f32[96,4096]{1,0:T(8,128)S(1)} custom-call(bf16[304,384]{1,0:T(8,128)(2,1)S(1)} %get-tuple-element.28.refs_0_, bf16[304,384]{1,0:T(8,128)(2,1)S(1)} %collective-permute-done.3.refs_1_, bf16[304,384]{1,0:T(8,128)(2,1)S(1)} %collective-permute-done.4.refs_2_, bf16[304,384]{1,0:T(8,128)(2,1)S(1)} %collective-permute-done.5.refs_3_, ...), custom_call_target="tpu_custom_call" | custom-call | tf_op jit(solution)/shard_map/pallas_call | solution.py:187
  55.7 0.0 collective-permute-done.refs_1_
  55.7 1.3 %shard_map.100 = (f32[24,4096]{1,0:T(8,128)S(1)}, bf16[24,4096]{1,0:T(8,128)(2,1)S(1)}, bf16[24,4096]{1,0:T(8,128)(2,1)S(1)}, bf16[24,4096]{1,0:T(8,128)(2,1)S(1)}) custom-call(bf16[304,128]{1,0:T(8,128)(2,1)S(1)} %get-tuple-element.23.after_ref.refs_0_, bf16[304,128]{1,0:T(8,128)(2,1)S(1)} %collective-permute-done.refs_1_, ...), custom_call_target="tpu_custom_call" | custom-call | tf_op jit(solution)/shard_map/pallas_call | solution.py:187
  57.0 0.0 collective-permute-done.15.refs_9_
  57.0 0.5 gain_terms.1
  57.5 0.1 collective-permute-start.16
  57.6 1.2 %collective-permute-done.16 = f32[1,4096]{1,0:T(1,128)S(1)} collective-permute-done((f32[1,4096]{1,0:T(1,128)S(1)}, f32[1,4096]{1,0:T(1,128)S(1)}, u32[]{:S(2)}, u32[]{:S(2)}) %collective-permute-start.16) | collective-permute-done | bytes 16416 | tf_op jit(solution)/shard_map/ppermute | solution.py:26
  58.7 1.8 %collective-permute-start.17 = (f32[1,4096]{1,0:T(1,128)S(1)}, f32[1,4096]{1,0:T(1,128)S(1)}, u32[]{:S(2)}, u32[]{:S(2)}) collective-permute-start(f32[1,4096]{1,0:T(1,128)S(1)} %add.15), channel_id=1, source_target_pairs={{0,8},{4,12},{8,0},{12,4},{16,24},{20,28},{24,16},{28,20},{1,9},{5... | collective-permute-start | bytes 49160 | tf_op jit(solution)/shard_map/ppermute | solution.py:26
  60.5 2.0 %collective-permute-done.17 = f32[1,4096]{1,0:T(1,128)S(1)} collective-permute-done((f32[1,4096]{1,0:T(1,128)S(1)}, f32[1,4096]{1,0:T(1,128)S(1)}, u32[]{:S(2)}, u32[]{:S(2)}) %collective-permute-start.17) | collective-permute-done | bytes 16416 | tf_op jit(solution)/shard_map/ppermute | solution.py:26
  62.6 2.8 %collective-permute-start.18 = (f32[1,4096]{1,0:T(1,128)S(1)}, f32[1,4096]{1,0:T(1,128)S(1)}, u32[]{:S(2)}, u32[]{:S(2)}) collective-permute-start(f32[1,4096]{1,0:T(1,128)S(1)} %add.16), channel_id=1, source_target_pairs={{0,16},{4,20},{8,24},{12,28},{16,0},{20,4},{24,8},{28,12},{1,17},{... | collective-permute-start | bytes 49160 | tf_op jit(solution)/shard_map/ppermute | solution.py:26
  65.4 1.9 %collective-permute-done.18 = f32[1,4096]{1,0:T(1,128)S(1)} collective-permute-done((f32[1,4096]{1,0:T(1,128)S(1)}, f32[1,4096]{1,0:T(1,128)S(1)}, u32[]{:S(2)}, u32[]{:S(2)}) %collective-permute-start.18) | collective-permute-done | bytes 16416 | tf_op jit(solution)/shard_map/ppermute | solution.py:26
  67.3 1.0 %collective-permute-start.19 = (f32[1,4096]{1,0:T(1,128)S(1)}, f32[1,4096]{1,0:T(1,128)S(1)}, u32[]{:S(2)}, u32[]{:S(2)}) collective-permute-start(f32[1,4096]{1,0:T(1,128)S(1)} %add.17), channel_id=1, source_target_pairs={{0,1},{1,0},{2,3},{3,2},{4,5},{5,4},{6,7},{7,6},{8,9},{9,8},{10,11... | collective-permute-start | bytes 49160 | tf_op jit(solution)/shard_map/ppermute | solution.py:26
  68.3 2.8 %collective-permute-done.19 = f32[1,4096]{1,0:T(1,128)S(1)} collective-permute-done((f32[1,4096]{1,0:T(1,128)S(1)}, f32[1,4096]{1,0:T(1,128)S(1)}, u32[]{:S(2)}, u32[]{:S(2)}) %collective-permute-start.19) | collective-permute-done | bytes 16416 | tf_op jit(solution)/shard_map/ppermute | solution.py:26
  71.1 2.0 %collective-permute-start.20 = (f32[1,4096]{1,0:T(1,128)S(1)}, f32[1,4096]{1,0:T(1,128)S(1)}, u32[]{:S(2)}, u32[]{:S(2)}) collective-permute-start(f32[1,4096]{1,0:T(1,128)S(1)} %add.18), channel_id=1, source_target_pairs={{0,2},{1,3},{2,0},{3,1},{4,6},{5,7},{6,4},{7,5},{8,10},{9,11},{10,... | collective-permute-start | bytes 49160 | tf_op jit(solution)/shard_map/ppermute | solution.py:26
  73.1 0.1 collective-permute-start.10
  73.2 2.2 %collective-permute-start.11 = (bf16[24,4096]{1,0:T(8,128)(2,1)S(1)}, bf16[24,4096]{1,0:T(8,128)(2,1)S(1)}, u32[]{:S(2)}, u32[]{:S(2)}) collective-permute-start(bf16[24,4096]{1,0:T(8,128)(2,1)S(1)} %get-tuple-element.41.refs_3_), channel_id=1, source_target_pairs={{0,3},{1,2},{2,1},{3,0},{4,7},{5,6},{6,5},{7,4},{8,11},{9,10},{10,... | collective-permute-start | bytes 589832 | tf_op jit(solution)/shard_map/ppermute | solution.py:26
  75.4 1.1 %collective-permute-start.9 = (bf16[24,4096]{1,0:T(8,128)(2,1)S(1)}, bf16[24,4096]{1,0:T(8,128)(2,1)S(1)}, u32[]{:S(2)}, u32[]{:S(2)}) collective-permute-start(bf16[24,4096]{1,0:T(8,128)(2,1)S(1)} %get-tuple-element.39.refs_1_), channel_id=1, source_target_pairs={{0,1},{1,0},{2,3},{3,2},{4,5},{5,4},{6,7},{7,6},{8,9},{9,8},{10,11... | collective-permute-start | bytes 589832 | tf_op jit(solution)/shard_map/ppermute | solution.py:26
  76.6 0.6 add_multiply_fusion
  77.2 3.7 %collective-permute-done.10.refs_1_ = bf16[24,4096]{1,0:T(8,128)(2,1)S(1)} collective-permute-done((bf16[24,4096]{1,0:T(8,128)(2,1)S(1)}, bf16[24,4096]{1,0:T(8,128)(2,1)S(1)}, u32[]{:S(2)}, u32[]{:S(2)}) %collective-permute-start.10) | collective-permute-done | bytes 196640 | tf_op jit(solution)/shard_map/ppermute | solution.py:26
  80.9 0.0 collective-permute-done.11.refs_2_
  80.9 1.5 %collective-permute-done.9.refs_0_ = bf16[24,4096]{1,0:T(8,128)(2,1)S(1)} collective-permute-done((bf16[24,4096]{1,0:T(8,128)(2,1)S(1)}, bf16[24,4096]{1,0:T(8,128)(2,1)S(1)}, u32[]{:S(2)}, u32[]{:S(2)}) %collective-permute-start.9) | collective-permute-done | bytes 196640 | tf_op jit(solution)/shard_map/ppermute | solution.py:26
  82.3 1.0 %finish.1 = bf16[1,24,4096]{2,1,0:T(8,128)(2,1)} custom-call(f32[24,4096]{1,0:T(8,128)S(1)} %get-tuple-element.38.own_ref.refs_0_, bf16[24,4096]{1,0:T(8,128)(2,1)S(1)} %collective-permute-done.9.refs_0_, bf16[24,4096]{1,0:T(8,128)(2,1)S(1)} %collective-permute-done.10.refs_1_, bf16[24,4096]{1,0:T(8,128)(2,1)S(1)} %collective-permute-done.11.refs_2_, ...), custom_call_target="tpu_custom_call" | custom-call | tf_op jit(solution)/shard_map/finish/pallas_call | solution.py:297
  (15 shorter events, 0.1 us)
Async XLA Ops:
  3.1 8.1 %collective-permute-start.12 = (bf16[24,2048]{1,0:T(8,128)(2,1)S(1)}, bf16[24,2048]{1,0:T(8,128)(2,1)S(1)}, u32[]{:S(2)}, u32[]{:S(2)}) collective-permute-start(bf16[24,2048]{1,0:T(8,128)(2,1)S(1)} %get-tuple-element.42.refs_4_), channel_id=1, source_target_pairs={{0,1},{1,0},{2,3},{3,2},{4,5},{5,4},{6,7},{7,6},{8,9},{9,8},{10,11... | collective-permute-start | bytes 294920 | tf_op jit(solution)/shard_map/ppermute | solution.py:26
  7.6 12.3 %collective-permute-start.3 = (bf16[304,384]{1,0:T(8,128)(2,1)S(1)}, bf16[304,384]{1,0:T(8,128)(2,1)S(1)}, u32[]{:S(2)}, u32[]{:S(2)}) collective-permute-start(bf16[304,384]{1,0:T(8,128)(2,1)S(1)} %get-tuple-element.29), channel_id=1, source_target_pairs={{0,1},{1,0},{2,3},{3,2},{4,5},{5,4},{6,7},{7,6},{8,9},{9,8},{10,11... | collective-permute-start | bytes 700424 | tf_op jit(solution)/shard_map/ppermute | solution.py:26
  7.7 22.9 %collective-permute-start.6 = (bf16[304,512]{1,0:T(8,128)(2,1)S(1)}, bf16[304,512]{1,0:T(8,128)(2,1)S(1)}, u32[]{:S(2)}, u32[]{:S(2)}) collective-permute-start(bf16[304,512]{1,0:T(8,128)(2,1)S(1)} %get-tuple-element.34), channel_id=1, source_target_pairs={{0,1},{1,0},{2,3},{3,2},{4,5},{5,4},{6,7},{7,6},{8,9},{9,8},{10,11... | collective-permute-start | bytes 933896 | tf_op jit(solution)/shard_map/ppermute | solution.py:26
  9.7 10.5 %collective-permute-start.4 = (bf16[304,384]{1,0:T(8,128)(2,1)S(1)}, bf16[304,384]{1,0:T(8,128)(2,1)S(1)}, u32[]{:S(2)}, u32[]{:S(2)}) collective-permute-start(bf16[304,384]{1,0:T(8,128)(2,1)S(1)} %get-tuple-element.30), channel_id=1, source_target_pairs={{0,2},{1,3},{2,0},{3,1},{4,6},{5,7},{6,4},{7,5},{8,10},{9,11},{10,... | collective-permute-start | bytes 700424 | tf_op jit(solution)/shard_map/ppermute | solution.py:26
  11.2 17.7 %collective-permute-start.5 = (bf16[304,384]{1,0:T(8,128)(2,1)S(1)}, bf16[304,384]{1,0:T(8,128)(2,1)S(1)}, u32[]{:S(2)}, u32[]{:S(2)}) collective-permute-start(bf16[304,384]{1,0:T(8,128)(2,1)S(1)} %get-tuple-element.31), channel_id=1, source_target_pairs={{0,3},{1,2},{2,1},{3,0},{4,7},{5,6},{6,5},{7,4},{8,11},{9,10},{10,... | collective-permute-start | bytes 700424 | tf_op jit(solution)/shard_map/ppermute | solution.py:26
  11.2 7.2 %collective-permute-start.14 = (bf16[24,2048]{1,0:T(8,128)(2,1)S(1)}, bf16[24,2048]{1,0:T(8,128)(2,1)S(1)}, u32[]{:S(2)}, u32[]{:S(2)}) collective-permute-start(bf16[24,2048]{1,0:T(8,128)(2,1)S(1)} %get-tuple-element.43.refs_7_), channel_id=1, source_target_pairs={{0,2},{1,3},{2,0},{3,1},{4,6},{5,7},{6,4},{7,5},{8,10},{9,11},{10,... | collective-permute-start | bytes 294920 | tf_op jit(solution)/shard_map/ppermute | solution.py:26
  18.4 21.4 %collective-permute-start.7 = (bf16[304,512]{1,0:T(8,128)(2,1)S(1)}, bf16[304,512]{1,0:T(8,128)(2,1)S(1)}, u32[]{:S(2)}, u32[]{:S(2)}) collective-permute-start(bf16[304,512]{1,0:T(8,128)(2,1)S(1)} %get-tuple-element.35), channel_id=1, source_target_pairs={{0,2},{1,3},{2,0},{3,1},{4,6},{5,7},{6,4},{7,5},{8,10},{9,11},{10,... | collective-permute-start | bytes 933896 | tf_op jit(solution)/shard_map/ppermute | solution.py:26
  19.9 21.8 %collective-permute-start.8 = (bf16[304,512]{1,0:T(8,128)(2,1)S(1)}, bf16[304,512]{1,0:T(8,128)(2,1)S(1)}, u32[]{:S(2)}, u32[]{:S(2)}) collective-permute-start(bf16[304,512]{1,0:T(8,128)(2,1)S(1)} %get-tuple-element.36), channel_id=1, source_target_pairs={{0,3},{1,2},{2,1},{3,0},{4,7},{5,6},{6,5},{7,4},{8,11},{9,10},{10,... | collective-permute-start | bytes 933896 | tf_op jit(solution)/shard_map/ppermute | solution.py:26
  20.2 36.7 %collective-permute-start.13 = (bf16[48,2048]{1,0:T(8,128)(2,1)S(1)}, bf16[48,2048]{1,0:T(8,128)(2,1)S(1)}, u32[]{:S(2)}, u32[]{:S(2)}) collective-permute-start(bf16[48,2048]{1,0:T(8,128)(2,1)S(1)} %pad_maximum_fusion), channel_id=1, source_target_pairs={{0,2},{1,3},{2,0},{3,1},{4,6},{5,7},{6,4},{7,5},{8,10},{9,11},{10,... | collective-permute-start | bytes 589832 | tf_op jit(solution)/shard_map/ppermute | solution.py:26
  29.0 28.0 %collective-permute-start.15 = (bf16[48,2048]{1,0:T(8,128)(2,1)S(1)}, bf16[48,2048]{1,0:T(8,128)(2,1)S(1)}, u32[]{:S(2)}, u32[]{:S(2)}) collective-permute-start(bf16[48,2048]{1,0:T(8,128)(2,1)S(1)} %pad_maximum_fusion.1), channel_id=1, source_target_pairs={{0,1},{1,0},{2,3},{3,2},{4,5},{5,4},{6,7},{7,6},{8,9},{9,8},{10,11... | collective-permute-start | bytes 589832 | tf_op jit(solution)/shard_map/ppermute | solution.py:26
  30.6 25.1 %collective-permute-start = (bf16[304,128]{1,0:T(8,128)(2,1)S(1)}, bf16[304,128]{1,0:T(8,128)(2,1)S(1)}, u32[]{:S(2)}, u32[]{:S(2)}) collective-permute-start(bf16[304,128]{1,0:T(8,128)(2,1)S(1)} %get-tuple-element.24), channel_id=1, source_target_pairs={{0,1},{1,0},{2,3},{3,2},{4,5},{5,4},{6,7},{7,6},{8,9},{9,8},{10,11... | collective-permute-start | bytes 233480 | tf_op jit(solution)/shard_map/ppermute | solution.py:26
  39.8 15.9 %collective-permute-start.1 = (bf16[304,128]{1,0:T(8,128)(2,1)S(1)}, bf16[304,128]{1,0:T(8,128)(2,1)S(1)}, u32[]{:S(2)}, u32[]{:S(2)}) collective-permute-start(bf16[304,128]{1,0:T(8,128)(2,1)S(1)} %get-tuple-element.25), channel_id=1, source_target_pairs={{0,2},{1,3},{2,0},{3,1},{4,6},{5,7},{6,4},{7,5},{8,10},{9,11},{10,... | collective-permute-start | bytes 233480 | tf_op jit(solution)/shard_map/ppermute | solution.py:26
  41.7 14.0 %collective-permute-start.2 = (bf16[304,128]{1,0:T(8,128)(2,1)S(1)}, bf16[304,128]{1,0:T(8,128)(2,1)S(1)}, u32[]{:S(2)}, u32[]{:S(2)}) collective-permute-start(bf16[304,128]{1,0:T(8,128)(2,1)S(1)} %get-tuple-element.26), channel_id=1, source_target_pairs={{0,3},{1,2},{2,1},{3,0},{4,7},{5,6},{6,5},{7,4},{8,11},{9,10},{10,... | collective-permute-start | bytes 233480 | tf_op jit(solution)/shard_map/ppermute | solution.py:26
  52.5 29.9 %copy-start = (bf16[1,24,4096]{2,1,0:T(8,128)(2,1)S(1)}, bf16[1,24,4096]{2,1,0:T(8,128)(2,1)}, u32[]{:S(2)}) copy-start(bf16[1,24,4096]{2,1,0:T(8,128)(2,1)} %src.1) | copy-start | bytes 589828
  52.5 29.9 %copy-start.1 = (f32[4096]{0:T(1024)S(1)}, f32[4096]{0:T(1024)}, u32[]{:S(2)}) copy-start(f32[4096]{0:T(1024)} %param.9) | copy-start | bytes 49156
  57.5 1.2 %collective-permute-start.16 = (f32[1,4096]{1,0:T(1,128)S(1)}, f32[1,4096]{1,0:T(1,128)S(1)}, u32[]{:S(2)}, u32[]{:S(2)}) collective-permute-start(f32[1,4096]{1,0:T(1,128)S(1)} %gain_terms.1), channel_id=1, source_target_pairs={{0,4},{4,0},{8,12},{12,8},{16,20},{20,16},{24,28},{28,24},{1,5},{5... | collective-permute-start | bytes 49160 | tf_op jit(solution)/shard_map/ppermute | solution.py:26
  58.7 3.8 %collective-permute-start.17 = (f32[1,4096]{1,0:T(1,128)S(1)}, f32[1,4096]{1,0:T(1,128)S(1)}, u32[]{:S(2)}, u32[]{:S(2)}) collective-permute-start(f32[1,4096]{1,0:T(1,128)S(1)} %add.15), channel_id=1, source_target_pairs={{0,8},{4,12},{8,0},{12,4},{16,24},{20,28},{24,16},{28,20},{1,9},{5... | collective-permute-start | bytes 49160 | tf_op jit(solution)/shard_map/ppermute | solution.py:26
  62.6 4.7 %collective-permute-start.18 = (f32[1,4096]{1,0:T(1,128)S(1)}, f32[1,4096]{1,0:T(1,128)S(1)}, u32[]{:S(2)}, u32[]{:S(2)}) collective-permute-start(f32[1,4096]{1,0:T(1,128)S(1)} %add.16), channel_id=1, source_target_pairs={{0,16},{4,20},{8,24},{12,28},{16,0},{20,4},{24,8},{28,12},{1,17},{... | collective-permute-start | bytes 49160 | tf_op jit(solution)/shard_map/ppermute | solution.py:26
  67.3 3.8 %collective-permute-start.19 = (f32[1,4096]{1,0:T(1,128)S(1)}, f32[1,4096]{1,0:T(1,128)S(1)}, u32[]{:S(2)}, u32[]{:S(2)}) collective-permute-start(f32[1,4096]{1,0:T(1,128)S(1)} %add.17), channel_id=1, source_target_pairs={{0,1},{1,0},{2,3},{3,2},{4,5},{5,4},{6,7},{7,6},{8,9},{9,8},{10,11... | collective-permute-start | bytes 49160 | tf_op jit(solution)/shard_map/ppermute | solution.py:26
  71.1 5.5 %collective-permute-start.20 = (f32[1,4096]{1,0:T(1,128)S(1)}, f32[1,4096]{1,0:T(1,128)S(1)}, u32[]{:S(2)}, u32[]{:S(2)}) collective-permute-start(f32[1,4096]{1,0:T(1,128)S(1)} %add.18), channel_id=1, source_target_pairs={{0,2},{1,3},{2,0},{3,1},{4,6},{5,7},{6,4},{7,5},{8,10},{9,11},{10,... | collective-permute-start | bytes 49160 | tf_op jit(solution)/shard_map/ppermute | solution.py:26
  73.1 7.8 %collective-permute-start.10 = (bf16[24,4096]{1,0:T(8,128)(2,1)S(1)}, bf16[24,4096]{1,0:T(8,128)(2,1)S(1)}, u32[]{:S(2)}, u32[]{:S(2)}) collective-permute-start(bf16[24,4096]{1,0:T(8,128)(2,1)S(1)} %get-tuple-element.40.refs_2_), channel_id=1, source_target_pairs={{0,2},{1,3},{2,0},{3,1},{4,6},{5,7},{6,4},{7,5},{8,10},{9,11},{10,... | collective-permute-start | bytes 589832 | tf_op jit(solution)/shard_map/ppermute | solution.py:26
  73.2 7.7 %collective-permute-start.11 = (bf16[24,4096]{1,0:T(8,128)(2,1)S(1)}, bf16[24,4096]{1,0:T(8,128)(2,1)S(1)}, u32[]{:S(2)}, u32[]{:S(2)}) collective-permute-start(bf16[24,4096]{1,0:T(8,128)(2,1)S(1)} %get-tuple-element.41.refs_3_), channel_id=1, source_target_pairs={{0,3},{1,2},{2,1},{3,0},{4,7},{5,6},{6,5},{7,4},{8,11},{9,10},{10,... | collective-permute-start | bytes 589832 | tf_op jit(solution)/shard_map/ppermute | solution.py:26
  75.4 6.9 %collective-permute-start.9 = (bf16[24,4096]{1,0:T(8,128)(2,1)S(1)}, bf16[24,4096]{1,0:T(8,128)(2,1)S(1)}, u32[]{:S(2)}, u32[]{:S(2)}) collective-permute-start(bf16[24,4096]{1,0:T(8,128)(2,1)S(1)} %get-tuple-element.39.refs_1_), channel_id=1, source_target_pairs={{0,1},{1,0},{2,3},{3,2},{4,5},{5,4},{6,7},{7,6},{8,9},{9,8},{10,11... | collective-permute-start | bytes 589832 | tf_op jit(solution)/shard_map/ppermute | solution.py:26
where the time goes:
time: 83.6 us; the launch traced here: 83.3 us
  waiting for transfers between devices  32.8 us (39%)
  starting transfers between devices  28 us (33%)
  Pallas kernels  21 us (25%)
    ppermute x21, waiting for transfers between devices, exchange(): return lax.ppermute(value, axis, xor_pairs(size, step))  32.8 us
    ppermute x21, starting transfers between devices, exchange(): return lax.ppermute(value, axis, xor_pairs(size, step))  28 us
    pallas_call x3, Pallas kernels, chunk_terms(): pl.pallas_call(kernel, out_shape=out_shape, in_specs=[vmem] * len(operand...  8.69 us
    pallas_call x1, Pallas kernels, load_weights(): pl.pallas_call(kernel, out_shape=[jax.ShapeDtypeStruct((width, 2 * cols),...  5.84 us
    pallas_call x3, Pallas kernels, pack_chunk(): pl.pallas_call(kernel, out_shape=[jax.ShapeDtypeStruct((sum(rows), width)...  4.04 us
  transfers between devices with their start and end apart: 21, of which 9 were waited for; matrix products, arithmetic and copies ran while one was open for 1% of the time, Pallas kernels for 20%

commit v1 on v0

--- a/solution.py
+++ b/solution.py
@@ -12,7 +12,6 @@
 ATTN_ROWS = 512
 PACK_VMEM = 8 << 20
 LAYER_VMEM = 24 << 20
-LOAD_VMEM = 8 << 20
 SMALL_VMEM = 2 << 20
 F32 = jnp.float32
 BF16 = jnp.bfloat16
@@ -71,39 +70,6 @@
         scratch_shapes=[pltpu.SemaphoreType.DMA((seq_size, 4))],
         compiler_params=pltpu.CompilerParams(vmem_limit_bytes=PACK_VMEM),
     )(*in_hbm(arrays))
-
-
-def load_weights(chunks, key_weight, value_weight, after):
-    width = key_weight.shape[1]
-
-    def kernel(kw, vw, after_ref, *rest):
-        outs, sems = rest[: len(chunks)], rest[len(chunks)]
-        copies = []
-        for n, (layer, first, cols) in enumerate(chunks):
-            for i, src in enumerate((kw, vw)):
-                copies.append(
-                    pltpu.make_async_copy(
-                        src.at[layer, :, pl.ds(first, cols)],
-                        outs[n].at[:, pl.ds(i * cols, cols)],
-                        sems.at[n, i],
-                    )
-                )
-        for c in copies:
-            c.start()
-        for c in copies:
-            c.wait()
-
-    total = 4 * key_weight.size
-    return pl.pallas_call(
-        kernel,
-        out_shape=[jax.ShapeDtypeStruct((width, 2 * cols), BF16) for _, _, cols in chunks],
-        in_specs=[pl.BlockSpec(memory_space=pltpu.HBM)] * 2 + [pl.BlockSpec(memory_space=pl.ANY)],
-        out_specs=[pl.BlockSpec(memory_space=pltpu.VMEM)] * len(chunks),
-        scratch_shapes=[pltpu.SemaphoreType.DMA((len(chunks), 2))],
-        compiler_params=pltpu.CompilerParams(vmem_limit_bytes=LOAD_VMEM),
-        cost_estimate=pl.CostEstimate(flops=0, transcendentals=0, bytes_accessed=total),
-        name="load_weights",
-    )(*in_hbm([key_weight, value_weight]), after)
 
 
 def attention_into(bufs, dec, enc, kv_ref):
@@ -152,23 +118,62 @@
         kv_ref[:, cols + p * LANES : cols + (p + 1) * LANES] = chosen(value_sum)
 
 
-def chunk_terms(bufs, weight, prior, dec, enc, last):
+def weight_copies(chunk, key_weight, value_weight, dest, sems):
+    layer, first, cols = chunk
+    copies = []
+    for b in range(dest.shape[0] // PROJ_BLOCK):
+        rows = pl.ds(b * PROJ_BLOCK, PROJ_BLOCK)
+        copies.append(
+            [
+                pltpu.make_async_copy(
+                    src.at[layer, rows, pl.ds(first, cols)],
+                    dest.at[rows, pl.ds(i * cols, cols)],
+                    sems.at[b, i],
+                )
+                for i, src in enumerate((key_weight, value_weight))
+            ]
+        )
+    return copies
+
+
+def chunk_terms(index, chunks, bufs, key_weight, value_weight, ready, prior, dec, enc):
     count = len(bufs)
-    width = weight.shape[0]
+    width = key_weight.shape[1]
     rows = enc * count
-    block = PROJ_BLOCK
+    nblocks = width // PROJ_BLOCK
+    cols = chunks[index][2]
+    last = index == len(chunks) - 1
+    fetch = index == 0 and not last
 
     def kernel(*refs):
-        buf_refs, w_ref = refs[:count], refs[count]
-        pos = count + 1
-        if prior is not None:
-            prior_ref = refs[pos]
-            pos += 1
-        outs, kv_ref = refs[pos:-1], refs[-1]
+        refs = list(refs)
+        buf_refs = [refs.pop(0) for _ in range(count)]
+        if ready is None:
+            kw, vw = refs.pop(0), refs.pop(0)
+        else:
+            w_ref = refs.pop(0)
+        prior_ref = None if prior is None else refs.pop(0)
+        outs = [refs.pop(0) for _ in range(count if last else 1)]
+        next_ref = refs.pop(0) if fetch else None
+        kv_ref = refs.pop(0)
+        if ready is None:
+            w_ref, sems = refs.pop(0), refs.pop(0)
+            copies = weight_copies(chunks[index], kw, vw, w_ref, sems)
+            for pair in copies:
+                for c in pair:
+                    c.start()
+        if fetch:
+            next_copies = weight_copies(chunks[-1], kw, vw, next_ref, refs.pop(0))
+            for pair in next_copies:
+                for c in pair:
+                    c.start()
         attention_into(buf_refs, dec, enc, kv_ref)
         nt = (((1,), (1,)), ((), ()))
-        for b in range(width // block):
-            bs = slice(b * block, (b + 1) * block)
+        for b in range(nblocks):
+            bs = slice(b * PROJ_BLOCK, (b + 1) * PROJ_BLOCK)
+            if ready is None:
+                for c in copies[b]:
+                    c.wait()
             acc = lax.dot_general(kv_ref[...], w_ref[bs, :], nt, preferred_element_type=F32)
             if prior is not None:
                 acc += prior_ref[:, bs]
@@ -177,21 +182,35 @@
                     outs[j][:, bs] = acc[j * enc : (j + 1) * enc].astype(outs[j].dtype)
             else:
                 outs[0][:, bs] = acc
+        if fetch:
+            for pair in next_copies:
+                for c in pair:
+                    c.wait()
 
     if last:
         out_shape = [jax.ShapeDtypeStruct((enc, width), F32 if j == 0 else BF16) for j in range(count)]
     else:
         out_shape = [jax.ShapeDtypeStruct((rows, width), F32)]
+    scratch = [pltpu.VMEM((rows, 2 * cols), BF16)]
+    if ready is None:
+        scratch += [pltpu.VMEM((width, 2 * cols), BF16), pltpu.SemaphoreType.DMA((nblocks, 2))]
+    if fetch:
+        out_shape.append(jax.ShapeDtypeStruct((width, 2 * chunks[-1][2]), BF16))
+        scratch.append(pltpu.SemaphoreType.DMA((nblocks, 2)))
     vmem = pl.BlockSpec(memory_space=pltpu.VMEM)
-    operands = list(bufs) + [weight] + ([] if prior is None else [prior])
+    if ready is None:
+        weights, specs = in_hbm([key_weight, value_weight]), [pl.BlockSpec(memory_space=pltpu.HBM)] * 2
+    else:
+        weights, specs = [ready], [vmem]
+    tail = [] if prior is None else [prior]
     return pl.pallas_call(
         kernel,
         out_shape=out_shape,
-        in_specs=[vmem] * len(operands),
+        in_specs=[vmem] * count + specs + [vmem] * len(tail),
         out_specs=[vmem] * len(out_shape),
-        scratch_shapes=[pltpu.VMEM((rows, weight.shape[1]), BF16)],
+        scratch_shapes=scratch,
         compiler_params=pltpu.CompilerParams(vmem_limit_bytes=LAYER_VMEM),
-    )(*operands)
+    )(*bufs, *weights, *tail)
 
 
 def split_final(enc_final, after):
@@ -320,13 +339,16 @@
             orders = [steps, steps[::-1]]
             finals = split_final(enc_final, bufs[0])
             halves = [gather_rows(f, seq, o) for f, o in zip(finals, orders)]
-    weights = load_weights(chunks, key_weight, value_weight, gathered[-1][0])
-    prior = None
+    prior = ready = None
     for index in range(len(chunks)):
+        last = index == len(chunks) - 1
         outs = chunk_terms(
-            gathered[index], weights[index], prior, dec, enc, index == len(chunks) - 1
+            index, chunks, gathered[index], key_weight, value_weight,
+            ready if last else None, prior, dec, enc,
         )
         prior = outs[0]
+        if index == 0:
+            ready = outs[-1]
     received = [exchange(outs[j], "seq", seq, j) for j in range(1, seq)]
     gain = gain_terms(
         outs, [[a for _, a in parts] for parts in halves], [row_order(o) for o in orders]
@@ -355,9 +377,7 @@
     )
 
     def whole(*args):
-        step = jax.shard_map(
-            body, mesh=mesh, in_specs=placed, out_specs=(P("dp", "seq", None), P()), check_vma=False
-        )
+        step = jax.shard_map(body, mesh=mesh, in_specs=placed, out_specs=(P("dp", "seq", None), P()), check_vma=False)
         return step(*args)
 
     return whole

time: 83.6 us -> 80.9 us (0.968)
  Pallas kernels: 21 us -> 18.3 us
    pallas_call x4 -> x3, Pallas kernels: 14.5 us -> 11.8 us  [chunk_terms(): pl.pallas_call(kernel, out_shape=out_shape, in_specs=[vmem] * count + spe...]
  transfers between devices with their start and end apart: 21 -> 21, of which waited for: 9 -> 9; matrix products, arithmetic and copies ran while one was open for 1% -> 1% of each run, Pallas kernels for 20% -> 18%
where the time goes in v1:
time: 80.9 us; the launch traced here: 80.6 us
  waiting for transfers between devices  32.8 us (41%)
  starting transfers between devices  28 us (35%)
  Pallas kernels  18.3 us (23%)
  between operations  0.81 us (1%)
    ppermute x21, waiting for transfers between devices, exchange(): return lax.ppermute(value, axis, xor_pairs(size, step))  32.8 us
    ppermute x21, starting transfers between devices, exchange(): return lax.ppermute(value, axis, xor_pairs(size, step))  28 us
    pallas_call x3, Pallas kernels, chunk_terms(): pl.pallas_call(kernel, out_shape=out_shape, in_specs=[vmem] * count + spe...  11.8 us
    pallas_call x3, Pallas kernels, pack_chunk(): pl.pallas_call(kernel, out_shape=[jax.ShapeDtypeStruct((sum(rows), width)...  4.04 us
  transfers between devices with their start and end apart: 21, of which 9 were waited for; matrix products, arithmetic and copies ran while one was open for 1% of the time, Pallas kernels for 18%

profile of v1, /device:TPU:0, one launch (start us, length us, event | category | flops | bytes accessed | tf_op | source)
XLA Modules:
  0.0 80.6 jit_solution(557467419278549660)
XLA Ops:
  0.6 1.5 %shard_map.96 = (bf16[304,512]{1,0:T(8,128)(2,1)S(1)}, bf16[304,512]{1,0:T(8,128)(2,1)S(1)}, bf16[304,512]{1,0:T(8,128)(2,1)S(1)}, bf16[304,512]{1,0:T(8,128)(2,1)S(1)}) custom-call(bf16[2,1,128,2048]{3,2,1,0:T(8,128)(2,1)} %q_ref.5, bf16[2,1,128,2048]{3,2,1,0:T(8,128)(2,1)} %g_ref.5, bf16[2,1,24,2048]{3,2,1,0:T(8,128)(2,1)} %k_ref.5, ...), custom_call_target="tpu_custom_call" | custom-call | tf_op jit(solution)/shard_map/pallas_call | solution.py:65
  2.2 1.0 %split_final.1 = (bf16[24,2048]{1,0:T(8,128)(2,1)S(1)}, bf16[24,2048]{1,0:T(8,128)(2,1)S(1)}) custom-call(bf16[1,24,4096]{2,1,0:T(8,128)(2,1)} %src.1, bf16[304,512]{1,0:T(8,128)(2,1)S(1)} %get-tuple-element.26.refs_0_.after_ref), custom_call_target="tpu_custom_call" | custom-call | tf_op jit(solution)/shard_map/split_final/pallas_call | solution.py:230
  3.1 3.0 %collective-permute-start.12 = (bf16[24,2048]{1,0:T(8,128)(2,1)S(1)}, bf16[24,2048]{1,0:T(8,128)(2,1)S(1)}, u32[]{:S(2)}, u32[]{:S(2)}) collective-permute-start(bf16[24,2048]{1,0:T(8,128)(2,1)S(1)} %get-tuple-element.40.refs_4_), channel_id=1, source_target_pairs={{0,1},{1,0},{2,3},{3,2},{4,5},{5,4},{6,7},{7,6},{8,9},{9,8},{10,11... | collective-permute-start | bytes 294920 | tf_op jit(solution)/shard_map/ppermute | solution.py:25
  6.2 1.4 %shard_map.98 = (bf16[304,384]{1,0:T(8,128)(2,1)S(1)}, bf16[304,384]{1,0:T(8,128)(2,1)S(1)}, bf16[304,384]{1,0:T(8,128)(2,1)S(1)}, bf16[304,384]{1,0:T(8,128)(2,1)S(1)}) custom-call(bf16[2,1,128,2048]{3,2,1,0:T(8,128)(2,1)} %q_ref.5, bf16[2,1,128,2048]{3,2,1,0:T(8,128)(2,1)} %g_ref.5, bf16[2,1,24,2048]{3,2,1,0:T(8,128)(2,1)} %k_ref.5, ...), custom_call_target="tpu_custom_call" | custom-call | tf_op jit(solution)/shard_map/pallas_call | solution.py:65
  7.6 0.1 collective-permute-start.6
  7.7 2.0 %collective-permute-start.3 = (bf16[304,512]{1,0:T(8,128)(2,1)S(1)}, bf16[304,512]{1,0:T(8,128)(2,1)S(1)}, u32[]{:S(2)}, u32[]{:S(2)}) collective-permute-start(bf16[304,512]{1,0:T(8,128)(2,1)S(1)} %get-tuple-element.27), channel_id=1, source_target_pairs={{0,1},{1,0},{2,3},{3,2},{4,5},{5,4},{6,7},{7,6},{8,9},{9,8},{10,11... | collective-permute-start | bytes 933896 | tf_op jit(solution)/shard_map/ppermute | solution.py:25
  9.7 1.5 %collective-permute-start.7 = (bf16[304,384]{1,0:T(8,128)(2,1)S(1)}, bf16[304,384]{1,0:T(8,128)(2,1)S(1)}, u32[]{:S(2)}, u32[]{:S(2)}) collective-permute-start(bf16[304,384]{1,0:T(8,128)(2,1)S(1)} %get-tuple-element.33), channel_id=1, source_target_pairs={{0,2},{1,3},{2,0},{3,1},{4,6},{5,7},{6,4},{7,5},{8,10},{9,11},{10,... | collective-permute-start | bytes 700424 | tf_op jit(solution)/shard_map/ppermute | solution.py:25
  11.2 0.0 collective-permute-start.8
  11.2 0.0 collective-permute-done.12.refs_5_
  11.2 2.0 %collective-permute-start.14 = (bf16[24,2048]{1,0:T(8,128)(2,1)S(1)}, bf16[24,2048]{1,0:T(8,128)(2,1)S(1)}, u32[]{:S(2)}, u32[]{:S(2)}) collective-permute-start(bf16[24,2048]{1,0:T(8,128)(2,1)S(1)} %get-tuple-element.41.refs_7_), channel_id=1, source_target_pairs={{0,2},{1,3},{2,0},{3,1},{4,6},{5,7},{6,4},{7,5},{8,10},{9,11},{10,... | collective-permute-start | bytes 294920 | tf_op jit(solution)/shard_map/ppermute | solution.py:25
  13.2 5.2 %collective-permute-done.14.refs_8_ = bf16[24,2048]{1,0:T(8,128)(2,1)S(1)} collective-permute-done((bf16[24,2048]{1,0:T(8,128)(2,1)S(1)}, bf16[24,2048]{1,0:T(8,128)(2,1)S(1)}, u32[]{:S(2)}, u32[]{:S(2)}) %collective-permute-start.14) | collective-permute-done | bytes 98336 | tf_op jit(solution)/shard_map/ppermute | solution.py:25
  18.4 1.5 %collective-permute-start.4 = (bf16[304,512]{1,0:T(8,128)(2,1)S(1)}, bf16[304,512]{1,0:T(8,128)(2,1)S(1)}, u32[]{:S(2)}, u32[]{:S(2)}) collective-permute-start(bf16[304,512]{1,0:T(8,128)(2,1)S(1)} %get-tuple-element.28), channel_id=1, source_target_pairs={{0,2},{1,3},{2,0},{3,1},{4,6},{5,7},{6,4},{7,5},{8,10},{9,11},{10,... | collective-permute-start | bytes 933896 | tf_op jit(solution)/shard_map/ppermute | solution.py:25
  19.9 0.0 collective-permute-done.6.refs_1_
  19.9 0.3 collective-permute-start.5
  20.2 1.8 %collective-permute-start.13 = (bf16[48,2048]{1,0:T(8,128)(2,1)S(1)}, bf16[48,2048]{1,0:T(8,128)(2,1)S(1)}, u32[]{:S(2)}, u32[]{:S(2)}) collective-permute-start(bf16[48,2048]{1,0:T(8,128)(2,1)S(1)} %pad_maximum_fusion), channel_id=1, source_target_pairs={{0,2},{1,3},{2,0},{3,1},{4,6},{5,7},{6,4},{7,5},{8,10},{9,11},{10,... | collective-permute-start | bytes 589832 | tf_op jit(solution)/shard_map/ppermute | solution.py:25
  22.0 7.0 %collective-permute-done.8.refs_3_ = bf16[304,384]{1,0:T(8,128)(2,1)S(1)} collective-permute-done((bf16[304,384]{1,0:T(8,128)(2,1)S(1)}, bf16[304,384]{1,0:T(8,128)(2,1)S(1)}, u32[]{:S(2)}, u32[]{:S(2)}) %collective-permute-start.8) | collective-permute-done | bytes 233504 | tf_op jit(solution)/shard_map/ppermute | solution.py:25
  29.0 0.5 collective-permute-start.15
  29.5 1.1 %shard_map.95 = (bf16[304,128]{1,0:T(8,128)(2,1)S(1)}, bf16[304,128]{1,0:T(8,128)(2,1)S(1)}, bf16[304,128]{1,0:T(8,128)(2,1)S(1)}, bf16[304,128]{1,0:T(8,128)(2,1)S(1)}) custom-call(bf16[2,1,128,2048]{3,2,1,0:T(8,128)(2,1)} %q_ref.5, bf16[2,1,128,2048]{3,2,1,0:T(8,128)(2,1)} %g_ref.5, bf16[2,1,24,2048]{3,2,1,0:T(8,128)(2,1)} %k_ref.5, ...), custom_call_target="tpu_custom_call" | custom-call | tf_op jit(solution)/shard_map/pallas_call | solution.py:65
  30.6 1.6 %collective-permute-start = (bf16[304,128]{1,0:T(8,128)(2,1)S(1)}, bf16[304,128]{1,0:T(8,128)(2,1)S(1)}, u32[]{:S(2)}, u32[]{:S(2)}) collective-permute-start(bf16[304,128]{1,0:T(8,128)(2,1)S(1)} %get-tuple-element.23), channel_id=1, source_target_pairs={{0,1},{1,0},{2,3},{3,2},{4,5},{5,4},{6,7},{7,6},{8,9},{9,8},{10,11... | collective-permute-start | bytes 233480 | tf_op jit(solution)/shard_map/ppermute | solution.py:25
  32.2 7.7 %collective-permute-done.4.refs_2_ = bf16[304,512]{1,0:T(8,128)(2,1)S(1)} collective-permute-done((bf16[304,512]{1,0:T(8,128)(2,1)S(1)}, bf16[304,512]{1,0:T(8,128)(2,1)S(1)}, u32[]{:S(2)}, u32[]{:S(2)}) %collective-permute-start.4) | collective-permute-done | bytes 311328 | tf_op jit(solution)/shard_map/ppermute | solution.py:25
  39.8 1.8 %collective-permute-start.1 = (bf16[304,128]{1,0:T(8,128)(2,1)S(1)}, bf16[304,128]{1,0:T(8,128)(2,1)S(1)}, u32[]{:S(2)}, u32[]{:S(2)}) collective-permute-start(bf16[304,128]{1,0:T(8,128)(2,1)S(1)} %get-tuple-element.24), channel_id=1, source_target_pairs={{0,2},{1,3},{2,0},{3,1},{4,6},{5,7},{6,4},{7,5},{8,10},{9,11},{10,... | collective-permute-start | bytes 233480 | tf_op jit(solution)/shard_map/ppermute | solution.py:25
  41.7 0.7 collective-permute-start.2
  42.4 6.4 %shard_map.97 = (f32[96,4096]{1,0:T(8,128)S(1)}, bf16[4096,256]{1,0:T(8,128)(2,1)S(1)}) custom-call(bf16[304,512]{1,0:T(8,128)(2,1)S(1)} %get-tuple-element.26.refs_0_.after_ref, bf16[304,512]{1,0:T(8,128)(2,1)S(1)} %collective-permute-done.3.refs_1_, bf16[304,512]{1,0:T(8,128)(2,1)S(1)} %collective-permute-done.4.refs_2_, ...), custom_call_target="tpu_custom_call" | custom-call | tf_op jit(solution)/shard_map/pallas_call | solution.py:206
  48.7 4.2 %shard_map.99.refs_5_ = f32[96,4096]{1,0:T(8,128)S(1)} custom-call(bf16[304,384]{1,0:T(8,128)(2,1)S(1)} %get-tuple-element.31.refs_0_, bf16[304,384]{1,0:T(8,128)(2,1)S(1)} %collective-permute-done.6.refs_1_, bf16[304,384]{1,0:T(8,128)(2,1)S(1)} %collective-permute-done.7.refs_2_, bf16[304,384]{1,0:T(8,128)(2,1)S(1)} %collective-permute-done.8.refs_3_, ...), custom_call_target="tpu_custom_call" | custom-call | tf_op jit(solution)/shard_map/pallas_call | solution.py:206
  53.0 0.0 collective-permute-done.refs_1_
  53.0 0.0 collective-permute-done.2.refs_3_
  53.0 0.0 copy-start
  53.0 0.0 copy-start.1
  53.0 1.2 %shard_map.100 = (f32[24,4096]{1,0:T(8,128)S(1)}, bf16[24,4096]{1,0:T(8,128)(2,1)S(1)}, bf16[24,4096]{1,0:T(8,128)(2,1)S(1)}, bf16[24,4096]{1,0:T(8,128)(2,1)S(1)}) custom-call(bf16[304,128]{1,0:T(8,128)(2,1)S(1)} %get-tuple-element.22.refs_0_, bf16[304,128]{1,0:T(8,128)(2,1)S(1)} %collective-permute-done.refs_1_, ...), custom_call_target="tpu_custom_call" | custom-call | tf_op jit(solution)/shard_map/pallas_call | solution.py:206
  54.3 0.0 collective-permute-done.15.refs_9_
  54.3 0.5 gain_terms.1
  54.8 0.1 collective-permute-start.16
  54.8 1.2 %collective-permute-done.16 = f32[1,4096]{1,0:T(1,128)S(1)} collective-permute-done((f32[1,4096]{1,0:T(1,128)S(1)}, f32[1,4096]{1,0:T(1,128)S(1)}, u32[]{:S(2)}, u32[]{:S(2)}) %collective-permute-start.16) | collective-permute-done | bytes 16416 | tf_op jit(solution)/shard_map/ppermute | solution.py:25
  56.0 1.8 %collective-permute-start.17 = (f32[1,4096]{1,0:T(1,128)S(1)}, f32[1,4096]{1,0:T(1,128)S(1)}, u32[]{:S(2)}, u32[]{:S(2)}) collective-permute-start(f32[1,4096]{1,0:T(1,128)S(1)} %add.15), channel_id=1, source_target_pairs={{0,8},{4,12},{8,0},{12,4},{16,24},{20,28},{24,16},{28,20},{1,9},{5... | collective-permute-start | bytes 49160 | tf_op jit(solution)/shard_map/ppermute | solution.py:25
  57.8 2.0 %collective-permute-done.17 = f32[1,4096]{1,0:T(1,128)S(1)} collective-permute-done((f32[1,4096]{1,0:T(1,128)S(1)}, f32[1,4096]{1,0:T(1,128)S(1)}, u32[]{:S(2)}, u32[]{:S(2)}) %collective-permute-start.17) | collective-permute-done | bytes 16416 | tf_op jit(solution)/shard_map/ppermute | solution.py:25
  59.9 2.8 %collective-permute-start.18 = (f32[1,4096]{1,0:T(1,128)S(1)}, f32[1,4096]{1,0:T(1,128)S(1)}, u32[]{:S(2)}, u32[]{:S(2)}) collective-permute-start(f32[1,4096]{1,0:T(1,128)S(1)} %add.16), channel_id=1, source_target_pairs={{0,16},{4,20},{8,24},{12,28},{16,0},{20,4},{24,8},{28,12},{1,17},{... | collective-permute-start | bytes 49160 | tf_op jit(solution)/shard_map/ppermute | solution.py:25
  62.7 1.9 %collective-permute-done.18 = f32[1,4096]{1,0:T(1,128)S(1)} collective-permute-done((f32[1,4096]{1,0:T(1,128)S(1)}, f32[1,4096]{1,0:T(1,128)S(1)}, u32[]{:S(2)}, u32[]{:S(2)}) %collective-permute-start.18) | collective-permute-done | bytes 16416 | tf_op jit(solution)/shard_map/ppermute | solution.py:25
  64.6 1.0 %collective-permute-start.19 = (f32[1,4096]{1,0:T(1,128)S(1)}, f32[1,4096]{1,0:T(1,128)S(1)}, u32[]{:S(2)}, u32[]{:S(2)}) collective-permute-start(f32[1,4096]{1,0:T(1,128)S(1)} %add.17), channel_id=1, source_target_pairs={{0,1},{1,0},{2,3},{3,2},{4,5},{5,4},{6,7},{7,6},{8,9},{9,8},{10,11... | collective-permute-start | bytes 49160 | tf_op jit(solution)/shard_map/ppermute | solution.py:25
  65.6 2.8 %collective-permute-done.19 = f32[1,4096]{1,0:T(1,128)S(1)} collective-permute-done((f32[1,4096]{1,0:T(1,128)S(1)}, f32[1,4096]{1,0:T(1,128)S(1)}, u32[]{:S(2)}, u32[]{:S(2)}) %collective-permute-start.19) | collective-permute-done | bytes 16416 | tf_op jit(solution)/shard_map/ppermute | solution.py:25
  68.4 2.0 %collective-permute-start.20 = (f32[1,4096]{1,0:T(1,128)S(1)}, f32[1,4096]{1,0:T(1,128)S(1)}, u32[]{:S(2)}, u32[]{:S(2)}) collective-permute-start(f32[1,4096]{1,0:T(1,128)S(1)} %add.18), channel_id=1, source_target_pairs={{0,2},{1,3},{2,0},{3,1},{4,6},{5,7},{6,4},{7,5},{8,10},{9,11},{10,... | collective-permute-start | bytes 49160 | tf_op jit(solution)/shard_map/ppermute | solution.py:25
  70.4 0.1 collective-permute-start.10
  70.5 2.2 %collective-permute-start.11 = (bf16[24,4096]{1,0:T(8,128)(2,1)S(1)}, bf16[24,4096]{1,0:T(8,128)(2,1)S(1)}, u32[]{:S(2)}, u32[]{:S(2)}) collective-permute-start(bf16[24,4096]{1,0:T(8,128)(2,1)S(1)} %get-tuple-element.39.refs_3_), channel_id=1, source_target_pairs={{0,3},{1,2},{2,1},{3,0},{4,7},{5,6},{6,5},{7,4},{8,11},{9,10},{10,... | collective-permute-start | bytes 589832 | tf_op jit(solution)/shard_map/ppermute | solution.py:25
  72.7 1.1 %collective-permute-start.9 = (bf16[24,4096]{1,0:T(8,128)(2,1)S(1)}, bf16[24,4096]{1,0:T(8,128)(2,1)S(1)}, u32[]{:S(2)}, u32[]{:S(2)}) collective-permute-start(bf16[24,4096]{1,0:T(8,128)(2,1)S(1)} %get-tuple-element.37.refs_1_), channel_id=1, source_target_pairs={{0,1},{1,0},{2,3},{3,2},{4,5},{5,4},{6,7},{7,6},{8,9},{9,8},{10,11... | collective-permute-start | bytes 589832 | tf_op jit(solution)/shard_map/ppermute | solution.py:25
  73.9 0.6 add_multiply_fusion
  74.5 3.7 %collective-permute-done.10.refs_1_ = bf16[24,4096]{1,0:T(8,128)(2,1)S(1)} collective-permute-done((bf16[24,4096]{1,0:T(8,128)(2,1)S(1)}, bf16[24,4096]{1,0:T(8,128)(2,1)S(1)}, u32[]{:S(2)}, u32[]{:S(2)}) %collective-permute-start.10) | collective-permute-done | bytes 196640 | tf_op jit(solution)/shard_map/ppermute | solution.py:25
  78.1 0.0 collective-permute-done.11.refs_2_
  78.1 1.5 %collective-permute-done.9.refs_0_ = bf16[24,4096]{1,0:T(8,128)(2,1)S(1)} collective-permute-done((bf16[24,4096]{1,0:T(8,128)(2,1)S(1)}, bf16[24,4096]{1,0:T(8,128)(2,1)S(1)}, u32[]{:S(2)}, u32[]{:S(2)}) %collective-permute-start.9) | collective-permute-done | bytes 196640 | tf_op jit(solution)/shard_map/ppermute | solution.py:25
  79.6 1.0 %finish.1 = bf16[1,24,4096]{2,1,0:T(8,128)(2,1)} custom-call(f32[24,4096]{1,0:T(8,128)S(1)} %get-tuple-element.36.own_ref.refs_0_, bf16[24,4096]{1,0:T(8,128)(2,1)S(1)} %collective-permute-done.9.refs_0_, bf16[24,4096]{1,0:T(8,128)(2,1)S(1)} %collective-permute-done.10.refs_1_, bf16[24,4096]{1,0:T(8,128)(2,1)S(1)} %collective-permute-done.11.refs_2_, ...), custom_call_target="tpu_custom_call" | custom-call | tf_op jit(solution)/shard_map/finish/pallas_call | solution.py:316
  (14 shorter events, 0.1 us)
Async XLA Ops:
  3.1 8.1 %collective-permute-start.12 = (bf16[24,2048]{1,0:T(8,128)(2,1)S(1)}, bf16[24,2048]{1,0:T(8,128)(2,1)S(1)}, u32[]{:S(2)}, u32[]{:S(2)}) collective-permute-start(bf16[24,2048]{1,0:T(8,128)(2,1)S(1)} %get-tuple-element.40.refs_4_), channel_id=1, source_target_pairs={{0,1},{1,0},{2,3},{3,2},{4,5},{5,4},{6,7},{7,6},{8,9},{9,8},{10,11... | collective-permute-start | bytes 294920 | tf_op jit(solution)/shard_map/ppermute | solution.py:25
  7.6 12.3 %collective-permute-start.6 = (bf16[304,384]{1,0:T(8,128)(2,1)S(1)}, bf16[304,384]{1,0:T(8,128)(2,1)S(1)}, u32[]{:S(2)}, u32[]{:S(2)}) collective-permute-start(bf16[304,384]{1,0:T(8,128)(2,1)S(1)} %get-tuple-element.32), channel_id=1, source_target_pairs={{0,1},{1,0},{2,3},{3,2},{4,5},{5,4},{6,7},{7,6},{8,9},{9,8},{10,11... | collective-permute-start | bytes 700424 | tf_op jit(solution)/shard_map/ppermute | solution.py:25
  7.7 22.9 %collective-permute-start.3 = (bf16[304,512]{1,0:T(8,128)(2,1)S(1)}, bf16[304,512]{1,0:T(8,128)(2,1)S(1)}, u32[]{:S(2)}, u32[]{:S(2)}) collective-permute-start(bf16[304,512]{1,0:T(8,128)(2,1)S(1)} %get-tuple-element.27), channel_id=1, source_target_pairs={{0,1},{1,0},{2,3},{3,2},{4,5},{5,4},{6,7},{7,6},{8,9},{9,8},{10,11... | collective-permute-start | bytes 933896 | tf_op jit(solution)/shard_map/ppermute | solution.py:25
  9.7 10.5 %collective-permute-start.7 = (bf16[304,384]{1,0:T(8,128)(2,1)S(1)}, bf16[304,384]{1,0:T(8,128)(2,1)S(1)}, u32[]{:S(2)}, u32[]{:S(2)}) collective-permute-start(bf16[304,384]{1,0:T(8,128)(2,1)S(1)} %get-tuple-element.33), channel_id=1, source_target_pairs={{0,2},{1,3},{2,0},{3,1},{4,6},{5,7},{6,4},{7,5},{8,10},{9,11},{10,... | collective-permute-start | bytes 700424 | tf_op jit(solution)/shard_map/ppermute | solution.py:25
  11.2 17.7 %collective-permute-start.8 = (bf16[304,384]{1,0:T(8,128)(2,1)S(1)}, bf16[304,384]{1,0:T(8,128)(2,1)S(1)}, u32[]{:S(2)}, u32[]{:S(2)}) collective-permute-start(bf16[304,384]{1,0:T(8,128)(2,1)S(1)} %get-tuple-element.34), channel_id=1, source_target_pairs={{0,3},{1,2},{2,1},{3,0},{4,7},{5,6},{6,5},{7,4},{8,11},{9,10},{10,... | collective-permute-start | bytes 700424 | tf_op jit(solution)/shard_map/ppermute | solution.py:25
  11.2 7.2 %collective-permute-start.14 = (bf16[24,2048]{1,0:T(8,128)(2,1)S(1)}, bf16[24,2048]{1,0:T(8,128)(2,1)S(1)}, u32[]{:S(2)}, u32[]{:S(2)}) collective-permute-start(bf16[24,2048]{1,0:T(8,128)(2,1)S(1)} %get-tuple-element.41.refs_7_), channel_id=1, source_target_pairs={{0,2},{1,3},{2,0},{3,1},{4,6},{5,7},{6,4},{7,5},{8,10},{9,11},{10,... | collective-permute-start | bytes 294920 | tf_op jit(solution)/shard_map/ppermute | solution.py:25
  18.4 21.4 %collective-permute-start.4 = (bf16[304,512]{1,0:T(8,128)(2,1)S(1)}, bf16[304,512]{1,0:T(8,128)(2,1)S(1)}, u32[]{:S(2)}, u32[]{:S(2)}) collective-permute-start(bf16[304,512]{1,0:T(8,128)(2,1)S(1)} %get-tuple-element.28), channel_id=1, source_target_pairs={{0,2},{1,3},{2,0},{3,1},{4,6},{5,7},{6,4},{7,5},{8,10},{9,11},{10,... | collective-permute-start | bytes 933896 | tf_op jit(solution)/shard_map/ppermute | solution.py:25
  19.9 21.8 %collective-permute-start.5 = (bf16[304,512]{1,0:T(8,128)(2,1)S(1)}, bf16[304,512]{1,0:T(8,128)(2,1)S(1)}, u32[]{:S(2)}, u32[]{:S(2)}) collective-permute-start(bf16[304,512]{1,0:T(8,128)(2,1)S(1)} %get-tuple-element.29), channel_id=1, source_target_pairs={{0,3},{1,2},{2,1},{3,0},{4,7},{5,6},{6,5},{7,4},{8,11},{9,10},{10,... | collective-permute-start | bytes 933896 | tf_op jit(solution)/shard_map/ppermute | solution.py:25
  20.2 34.0 %collective-permute-start.13 = (bf16[48,2048]{1,0:T(8,128)(2,1)S(1)}, bf16[48,2048]{1,0:T(8,128)(2,1)S(1)}, u32[]{:S(2)}, u32[]{:S(2)}) collective-permute-start(bf16[48,2048]{1,0:T(8,128)(2,1)S(1)} %pad_maximum_fusion), channel_id=1, source_target_pairs={{0,2},{1,3},{2,0},{3,1},{4,6},{5,7},{6,4},{7,5},{8,10},{9,11},{10,... | collective-permute-start | bytes 589832 | tf_op jit(solution)/shard_map/ppermute | solution.py:25
  29.0 25.3 %collective-permute-start.15 = (bf16[48,2048]{1,0:T(8,128)(2,1)S(1)}, bf16[48,2048]{1,0:T(8,128)(2,1)S(1)}, u32[]{:S(2)}, u32[]{:S(2)}) collective-permute-start(bf16[48,2048]{1,0:T(8,128)(2,1)S(1)} %pad_maximum_fusion.1), channel_id=1, source_target_pairs={{0,1},{1,0},{2,3},{3,2},{4,5},{5,4},{6,7},{7,6},{8,9},{9,8},{10,11... | collective-permute-start | bytes 589832 | tf_op jit(solution)/shard_map/ppermute | solution.py:25
  30.6 22.4 %collective-permute-start = (bf16[304,128]{1,0:T(8,128)(2,1)S(1)}, bf16[304,128]{1,0:T(8,128)(2,1)S(1)}, u32[]{:S(2)}, u32[]{:S(2)}) collective-permute-start(bf16[304,128]{1,0:T(8,128)(2,1)S(1)} %get-tuple-element.23), channel_id=1, source_target_pairs={{0,1},{1,0},{2,3},{3,2},{4,5},{5,4},{6,7},{7,6},{8,9},{9,8},{10,11... | collective-permute-start | bytes 233480 | tf_op jit(solution)/shard_map/ppermute | solution.py:25
  39.8 13.2 %collective-permute-start.1 = (bf16[304,128]{1,0:T(8,128)(2,1)S(1)}, bf16[304,128]{1,0:T(8,128)(2,1)S(1)}, u32[]{:S(2)}, u32[]{:S(2)}) collective-permute-start(bf16[304,128]{1,0:T(8,128)(2,1)S(1)} %get-tuple-element.24), channel_id=1, source_target_pairs={{0,2},{1,3},{2,0},{3,1},{4,6},{5,7},{6,4},{7,5},{8,10},{9,11},{10,... | collective-permute-start | bytes 233480 | tf_op jit(solution)/shard_map/ppermute | solution.py:25
  41.7 11.3 %collective-permute-start.2 = (bf16[304,128]{1,0:T(8,128)(2,1)S(1)}, bf16[304,128]{1,0:T(8,128)(2,1)S(1)}, u32[]{:S(2)}, u32[]{:S(2)}) collective-permute-start(bf16[304,128]{1,0:T(8,128)(2,1)S(1)} %get-tuple-element.25), channel_id=1, source_target_pairs={{0,3},{1,2},{2,1},{3,0},{4,7},{5,6},{6,5},{7,4},{8,11},{9,10},{10,... | collective-permute-start | bytes 233480 | tf_op jit(solution)/shard_map/ppermute | solution.py:25
  53.0 26.6 %copy-start = (bf16[1,24,4096]{2,1,0:T(8,128)(2,1)S(1)}, bf16[1,24,4096]{2,1,0:T(8,128)(2,1)}, u32[]{:S(2)}) copy-start(bf16[1,24,4096]{2,1,0:T(8,128)(2,1)} %src.1) | copy-start | bytes 589828
  53.0 26.6 %copy-start.1 = (f32[4096]{0:T(1024)S(1)}, f32[4096]{0:T(1024)}, u32[]{:S(2)}) copy-start(f32[4096]{0:T(1024)} %param.9) | copy-start | bytes 49156
  54.8 1.2 %collective-permute-start.16 = (f32[1,4096]{1,0:T(1,128)S(1)}, f32[1,4096]{1,0:T(1,128)S(1)}, u32[]{:S(2)}, u32[]{:S(2)}) collective-permute-start(f32[1,4096]{1,0:T(1,128)S(1)} %gain_terms.1), channel_id=1, source_target_pairs={{0,4},{4,0},{8,12},{12,8},{16,20},{20,16},{24,28},{28,24},{1,5},{5... | collective-permute-start | bytes 49160 | tf_op jit(solution)/shard_map/ppermute | solution.py:25
  56.0 3.8 %collective-permute-start.17 = (f32[1,4096]{1,0:T(1,128)S(1)}, f32[1,4096]{1,0:T(1,128)S(1)}, u32[]{:S(2)}, u32[]{:S(2)}) collective-permute-start(f32[1,4096]{1,0:T(1,128)S(1)} %add.15), channel_id=1, source_target_pairs={{0,8},{4,12},{8,0},{12,4},{16,24},{20,28},{24,16},{28,20},{1,9},{5... | collective-permute-start | bytes 49160 | tf_op jit(solution)/shard_map/ppermute | solution.py:25
  59.9 4.7 %collective-permute-start.18 = (f32[1,4096]{1,0:T(1,128)S(1)}, f32[1,4096]{1,0:T(1,128)S(1)}, u32[]{:S(2)}, u32[]{:S(2)}) collective-permute-start(f32[1,4096]{1,0:T(1,128)S(1)} %add.16), channel_id=1, source_target_pairs={{0,16},{4,20},{8,24},{12,28},{16,0},{20,4},{24,8},{28,12},{1,17},{... | collective-permute-start | bytes 49160 | tf_op jit(solution)/shard_map/ppermute | solution.py:25
  64.6 3.8 %collective-permute-start.19 = (f32[1,4096]{1,0:T(1,128)S(1)}, f32[1,4096]{1,0:T(1,128)S(1)}, u32[]{:S(2)}, u32[]{:S(2)}) collective-permute-start(f32[1,4096]{1,0:T(1,128)S(1)} %add.17), channel_id=1, source_target_pairs={{0,1},{1,0},{2,3},{3,2},{4,5},{5,4},{6,7},{7,6},{8,9},{9,8},{10,11... | collective-permute-start | bytes 49160 | tf_op jit(solution)/shard_map/ppermute | solution.py:25
  68.4 5.4 %collective-permute-start.20 = (f32[1,4096]{1,0:T(1,128)S(1)}, f32[1,4096]{1,0:T(1,128)S(1)}, u32[]{:S(2)}, u32[]{:S(2)}) collective-permute-start(f32[1,4096]{1,0:T(1,128)S(1)} %add.18), channel_id=1, source_target_pairs={{0,2},{1,3},{2,0},{3,1},{4,6},{5,7},{6,4},{7,5},{8,10},{9,11},{10,... | collective-permute-start | bytes 49160 | tf_op jit(solution)/shard_map/ppermute | solution.py:25
  70.4 7.8 %collective-permute-start.10 = (bf16[24,4096]{1,0:T(8,128)(2,1)S(1)}, bf16[24,4096]{1,0:T(8,128)(2,1)S(1)}, u32[]{:S(2)}, u32[]{:S(2)}) collective-permute-start(bf16[24,4096]{1,0:T(8,128)(2,1)S(1)} %get-tuple-element.38.refs_2_), channel_id=1, source_target_pairs={{0,2},{1,3},{2,0},{3,1},{4,6},{5,7},{6,4},{7,5},{8,10},{9,11},{10,... | collective-permute-start | bytes 589832 | tf_op jit(solution)/shard_map/ppermute | solution.py:25
  70.5 7.6 %collective-permute-start.11 = (bf16[24,4096]{1,0:T(8,128)(2,1)S(1)}, bf16[24,4096]{1,0:T(8,128)(2,1)S(1)}, u32[]{:S(2)}, u32[]{:S(2)}) collective-permute-start(bf16[24,4096]{1,0:T(8,128)(2,1)S(1)} %get-tuple-element.39.refs_3_), channel_id=1, source_target_pairs={{0,3},{1,2},{2,1},{3,0},{4,7},{5,6},{6,5},{7,4},{8,11},{9,10},{10,... | collective-permute-start | bytes 589832 | tf_op jit(solution)/shard_map/ppermute | solution.py:25
  72.7 6.9 %collective-permute-start.9 = (bf16[24,4096]{1,0:T(8,128)(2,1)S(1)}, bf16[24,4096]{1,0:T(8,128)(2,1)S(1)}, u32[]{:S(2)}, u32[]{:S(2)}) collective-permute-start(bf16[24,4096]{1,0:T(8,128)(2,1)S(1)} %get-tuple-element.37.refs_1_), channel_id=1, source_target_pairs={{0,1},{1,0},{2,3},{3,2},{4,5},{5,4},{6,7},{7,6},{8,9},{9,8},{10,11... | collective-permute-start | bytes 589832 | tf_op jit(solution)/shard_map/ppermute | solution.py:25

commit v2 on v1

--- a/solution.py
+++ b/solution.py
@@ -136,6 +136,30 @@
     return copies
 
 
+def load_weights(chunks, key_weight, value_weight, after):
+    width = key_weight.shape[1]
+
+    def kernel(kw, vw, after_ref, *rest):
+        outs, sems = rest[: len(chunks)], rest[len(chunks) :]
+        copies = []
+        for chunk, out, sem in zip(chunks, outs, sems):
+            copies += sum(weight_copies(chunk, kw, vw, out, sem), [])
+        for c in copies:
+            c.start()
+        for c in copies:
+            c.wait()
+
+    return pl.pallas_call(
+        kernel,
+        out_shape=[jax.ShapeDtypeStruct((width, 2 * cols), BF16) for _, _, cols in chunks],
+        in_specs=[pl.BlockSpec(memory_space=pltpu.HBM)] * 2 + [pl.BlockSpec(memory_space=pl.ANY)],
+        out_specs=[pl.BlockSpec(memory_space=pltpu.VMEM)] * len(chunks),
+        scratch_shapes=[pltpu.SemaphoreType.DMA((width // PROJ_BLOCK, 2)) for _ in chunks],
+        compiler_params=pltpu.CompilerParams(vmem_limit_bytes=PACK_VMEM),
+        name="load_weights",
+    )(*in_hbm([key_weight, value_weight]), after)
+
+
 def chunk_terms(index, chunks, bufs, key_weight, value_weight, ready, prior, dec, enc):
     count = len(bufs)
     width = key_weight.shape[1]
@@ -143,7 +167,6 @@
     nblocks = width // PROJ_BLOCK
     cols = chunks[index][2]
     last = index == len(chunks) - 1
-    fetch = index == 0 and not last
 
     def kernel(*refs):
         refs = list(refs)
@@ -154,17 +177,11 @@
             w_ref = refs.pop(0)
         prior_ref = None if prior is None else refs.pop(0)
         outs = [refs.pop(0) for _ in range(count if last else 1)]
-        next_ref = refs.pop(0) if fetch else None
         kv_ref = refs.pop(0)
         if ready is None:
             w_ref, sems = refs.pop(0), refs.pop(0)
             copies = weight_copies(chunks[index], kw, vw, w_ref, sems)
             for pair in copies:
-                for c in pair:
-                    c.start()
-        if fetch:
-            next_copies = weight_copies(chunks[-1], kw, vw, next_ref, refs.pop(0))
-            for pair in next_copies:
                 for c in pair:
                     c.start()
         attention_into(buf_refs, dec, enc, kv_ref)
@@ -182,10 +199,6 @@
                     outs[j][:, bs] = acc[j * enc : (j + 1) * enc].astype(outs[j].dtype)
             else:
                 outs[0][:, bs] = acc
-        if fetch:
-            for pair in next_copies:
-                for c in pair:
-                    c.wait()
 
     if last:
         out_shape = [jax.ShapeDtypeStruct((enc, width), F32 if j == 0 else BF16) for j in range(count)]
@@ -194,9 +207,6 @@
     scratch = [pltpu.VMEM((rows, 2 * cols), BF16)]
     if ready is None:
         scratch += [pltpu.VMEM((width, 2 * cols), BF16), pltpu.SemaphoreType.DMA((nblocks, 2))]
-    if fetch:
-        out_shape.append(jax.ShapeDtypeStruct((width, 2 * chunks[-1][2]), BF16))
-        scratch.append(pltpu.SemaphoreType.DMA((nblocks, 2)))
     vmem = pl.BlockSpec(memory_space=pltpu.VMEM)
     if ready is None:
         weights, specs = in_hbm([key_weight, value_weight]), [pl.BlockSpec(memory_space=pltpu.HBM)] * 2
@@ -339,16 +349,14 @@
             orders = [steps, steps[::-1]]
             finals = split_final(enc_final, bufs[0])
             halves = [gather_rows(f, seq, o) for f, o in zip(finals, orders)]
-    prior = ready = None
+    ready = load_weights(chunks[1:], key_weight, value_weight, gathered[-1][0])
+    prior = None
     for index in range(len(chunks)):
-        last = index == len(chunks) - 1
         outs = chunk_terms(
             index, chunks, gathered[index], key_weight, value_weight,
-            ready if last else None, prior, dec, enc,
+            ready[index - 1] if index else None, prior, dec, enc,
         )
         prior = outs[0]
-        if index == 0:
-            ready = outs[-1]
     received = [exchange(outs[j], "seq", seq, j) for j in range(1, seq)]
     gain = gain_terms(
         outs, [[a for _, a in parts] for parts in halves], [row_order(o) for o in orders]

time: 80.9 us -> 82.3 us (1.017)
  waiting for transfers between devices: 32.8 us -> 30 us
  Pallas kernels: 18.3 us -> 20.6 us
  starting transfers between devices: 28 us -> 29.8 us
    pallas_call x0 -> x1, Pallas kernels: none -> 3.55 us  [load_weights(): pl.pallas_call(kernel, out_shape=[jax.ShapeDtypeStruct((width, 2 * cols),...]
    ppermute x21, waiting for transfers between devices: 32.8 us -> 30 us  [exchange(): return lax.ppermute(value, axis, xor_pairs(size, step))]
    ppermute x21, starting transfers between devices: 28 us -> 29.8 us  [exchange(): return lax.ppermute(value, axis, xor_pairs(size, step))]
    pallas_call x3, Pallas kernels: 11.8 us -> 10.6 us  [chunk_terms(): pl.pallas_call(kernel, out_shape=out_shape, in_specs=[vmem] * count + spe...]
  transfers between devices with their start and end apart: 21 -> 21, of which waited for: 9 -> 8; matrix products, arithmetic and copies ran while one was open for 1% -> 1% of each run, Pallas kernels for 18% -> 20%
where the time goes in v2:
time: 82.3 us; the launch traced here: 82 us
  waiting for transfers between devices  30 us (36%)
  starting transfers between devices  29.8 us (36%)
  Pallas kernels  20.6 us (25%)
    ppermute x21, waiting for transfers between devices, exchange(): return lax.ppermute(value, axis, xor_pairs(size, step))  30 us
    ppermute x21, starting transfers between devices, exchange(): return lax.ppermute(value, axis, xor_pairs(size, step))  29.8 us
    pallas_call x3, Pallas kernels, chunk_terms(): pl.pallas_call(kernel, out_shape=out_shape, in_specs=[vmem] * count + spe...  10.6 us
    pallas_call x3, Pallas kernels, pack_chunk(): pl.pallas_call(kernel, out_shape=[jax.ShapeDtypeStruct((sum(rows), width)...  4.04 us
    pallas_call x1, Pallas kernels, load_weights(): pl.pallas_call(kernel, out_shape=[jax.ShapeDtypeStruct((width, 2 * cols),...  3.55 us
  transfers between devices with their start and end apart: 21, of which 8 were waited for; matrix products, arithmetic and copies ran while one was open for 1% of the time, Pallas kernels for 20%

profile of v2, /device:TPU:0, one launch (start us, length us, event | category | flops | bytes accessed | tf_op | source)
XLA Modules:
  0.0 82.0 jit_solution(9154730368023018570)
XLA Ops:
  0.6 1.5 %shard_map.97 = (bf16[304,512]{1,0:T(8,128)(2,1)S(1)}, bf16[304,512]{1,0:T(8,128)(2,1)S(1)}, bf16[304,512]{1,0:T(8,128)(2,1)S(1)}, bf16[304,512]{1,0:T(8,128)(2,1)S(1)}) custom-call(bf16[2,1,128,2048]{3,2,1,0:T(8,128)(2,1)} %q_ref.5, bf16[2,1,128,2048]{3,2,1,0:T(8,128)(2,1)} %g_ref.5, bf16[2,1,24,2048]{3,2,1,0:T(8,128)(2,1)} %k_ref.5, ...), custom_call_target="tpu_custom_call" | custom-call | tf_op jit(solution)/shard_map/pallas_call | solution.py:65
  2.2 1.0 %split_final.1 = (bf16[24,2048]{1,0:T(8,128)(2,1)S(1)}, bf16[24,2048]{1,0:T(8,128)(2,1)S(1)}) custom-call(bf16[1,24,4096]{2,1,0:T(8,128)(2,1)} %src.1, bf16[304,512]{1,0:T(8,128)(2,1)S(1)} %get-tuple-element.32.refs_0_.after_ref), custom_call_target="tpu_custom_call" | custom-call | tf_op jit(solution)/shard_map/split_final/pallas_call | solution.py:240
  3.1 3.0 %collective-permute-start.12 = (bf16[24,2048]{1,0:T(8,128)(2,1)S(1)}, bf16[24,2048]{1,0:T(8,128)(2,1)S(1)}, u32[]{:S(2)}, u32[]{:S(2)}) collective-permute-start(bf16[24,2048]{1,0:T(8,128)(2,1)S(1)} %get-tuple-element.40.refs_4_), channel_id=1, source_target_pairs={{0,1},{1,0},{2,3},{3,2},{4,5},{5,4},{6,7},{7,6},{8,9},{9,8},{10,11... | collective-permute-start | bytes 294920 | tf_op jit(solution)/shard_map/ppermute | solution.py:25
  6.2 1.4 %shard_map.96 = (bf16[304,384]{1,0:T(8,128)(2,1)S(1)}, bf16[304,384]{1,0:T(8,128)(2,1)S(1)}, bf16[304,384]{1,0:T(8,128)(2,1)S(1)}, bf16[304,384]{1,0:T(8,128)(2,1)S(1)}) custom-call(bf16[2,1,128,2048]{3,2,1,0:T(8,128)(2,1)} %q_ref.5, bf16[2,1,128,2048]{3,2,1,0:T(8,128)(2,1)} %g_ref.5, bf16[2,1,24,2048]{3,2,1,0:T(8,128)(2,1)} %k_ref.5, ...), custom_call_target="tpu_custom_call" | custom-call | tf_op jit(solution)/shard_map/pallas_call | solution.py:65
  7.6 0.1 collective-permute-start.3
  7.7 2.0 %collective-permute-start.4 = (bf16[304,384]{1,0:T(8,128)(2,1)S(1)}, bf16[304,384]{1,0:T(8,128)(2,1)S(1)}, u32[]{:S(2)}, u32[]{:S(2)}) collective-permute-start(bf16[304,384]{1,0:T(8,128)(2,1)S(1)} %get-tuple-element.29), channel_id=1, source_target_pairs={{0,2},{1,3},{2,0},{3,1},{4,6},{5,7},{6,4},{7,5},{8,10},{9,11},{10,... | collective-permute-start | bytes 700424 | tf_op jit(solution)/shard_map/ppermute | solution.py:25
  9.7 1.4 %collective-permute-start.5 = (bf16[304,384]{1,0:T(8,128)(2,1)S(1)}, bf16[304,384]{1,0:T(8,128)(2,1)S(1)}, u32[]{:S(2)}, u32[]{:S(2)}) collective-permute-start(bf16[304,384]{1,0:T(8,128)(2,1)S(1)} %get-tuple-element.30), channel_id=1, source_target_pairs={{0,3},{1,2},{2,1},{3,0},{4,7},{5,6},{6,5},{7,4},{8,11},{9,10},{10,... | collective-permute-start | bytes 700424 | tf_op jit(solution)/shard_map/ppermute | solution.py:25
  11.2 0.1 collective-permute-start.6
  11.2 2.0 %collective-permute-start.14 = (bf16[24,2048]{1,0:T(8,128)(2,1)S(1)}, bf16[24,2048]{1,0:T(8,128)(2,1)S(1)}, u32[]{:S(2)}, u32[]{:S(2)}) collective-permute-start(bf16[24,2048]{1,0:T(8,128)(2,1)S(1)} %get-tuple-element.41.refs_7_), channel_id=1, source_target_pairs={{0,2},{1,3},{2,0},{3,1},{4,6},{5,7},{6,4},{7,5},{8,10},{9,11},{10,... | collective-permute-start | bytes 294920 | tf_op jit(solution)/shard_map/ppermute | solution.py:25
  13.2 8.5 %collective-permute-done.14.refs_8_ = bf16[24,2048]{1,0:T(8,128)(2,1)S(1)} collective-permute-done((bf16[24,2048]{1,0:T(8,128)(2,1)S(1)}, bf16[24,2048]{1,0:T(8,128)(2,1)S(1)}, u32[]{:S(2)}, u32[]{:S(2)}) %collective-permute-start.14) | collective-permute-done | bytes 98336 | tf_op jit(solution)/shard_map/ppermute | solution.py:25
  21.8 1.9 %collective-permute-start.7 = (bf16[304,512]{1,0:T(8,128)(2,1)S(1)}, bf16[304,512]{1,0:T(8,128)(2,1)S(1)}, u32[]{:S(2)}, u32[]{:S(2)}) collective-permute-start(bf16[304,512]{1,0:T(8,128)(2,1)S(1)} %get-tuple-element.34), channel_id=1, source_target_pairs={{0,2},{1,3},{2,0},{3,1},{4,6},{5,7},{6,4},{7,5},{8,10},{9,11},{10,... | collective-permute-start | bytes 933896 | tf_op jit(solution)/shard_map/ppermute | solution.py:25
  23.7 1.4 %collective-permute-start.8 = (bf16[304,512]{1,0:T(8,128)(2,1)S(1)}, bf16[304,512]{1,0:T(8,128)(2,1)S(1)}, u32[]{:S(2)}, u32[]{:S(2)}) collective-permute-start(bf16[304,512]{1,0:T(8,128)(2,1)S(1)} %get-tuple-element.35), channel_id=1, source_target_pairs={{0,3},{1,2},{2,1},{3,0},{4,7},{5,6},{6,5},{7,4},{8,11},{9,10},{10,... | collective-permute-start | bytes 933896 | tf_op jit(solution)/shard_map/ppermute | solution.py:25
  25.2 0.0 collective-permute-done.4.refs_2_
  25.2 1.6 %collective-permute-start.13 = (bf16[48,2048]{1,0:T(8,128)(2,1)S(1)}, bf16[48,2048]{1,0:T(8,128)(2,1)S(1)}, u32[]{:S(2)}, u32[]{:S(2)}) collective-permute-start(bf16[48,2048]{1,0:T(8,128)(2,1)S(1)} %pad_maximum_fusion), channel_id=1, source_target_pairs={{0,2},{1,3},{2,0},{3,1},{4,6},{5,7},{6,4},{7,5},{8,10},{9,11},{10,... | collective-permute-start | bytes 589832 | tf_op jit(solution)/shard_map/ppermute | solution.py:25
  26.8 0.5 collective-permute-start.15
  27.3 1.1 %shard_map.95 = (bf16[304,128]{1,0:T(8,128)(2,1)S(1)}, bf16[304,128]{1,0:T(8,128)(2,1)S(1)}, bf16[304,128]{1,0:T(8,128)(2,1)S(1)}, bf16[304,128]{1,0:T(8,128)(2,1)S(1)}) custom-call(bf16[2,1,128,2048]{3,2,1,0:T(8,128)(2,1)} %q_ref.5, bf16[2,1,128,2048]{3,2,1,0:T(8,128)(2,1)} %g_ref.5, bf16[2,1,24,2048]{3,2,1,0:T(8,128)(2,1)} %k_ref.5, ...), custom_call_target="tpu_custom_call" | custom-call | tf_op jit(solution)/shard_map/pallas_call | solution.py:65
  28.4 0.0 collective-permute-done.6.refs_1_
  28.4 1.6 %collective-permute-start = (bf16[304,128]{1,0:T(8,128)(2,1)S(1)}, bf16[304,128]{1,0:T(8,128)(2,1)S(1)}, u32[]{:S(2)}, u32[]{:S(2)}) collective-permute-start(bf16[304,128]{1,0:T(8,128)(2,1)S(1)} %get-tuple-element.23), channel_id=1, source_target_pairs={{0,1},{1,0},{2,3},{3,2},{4,5},{5,4},{6,7},{7,6},{8,9},{9,8},{10,11... | collective-permute-start | bytes 233480 | tf_op jit(solution)/shard_map/ppermute | solution.py:25
  30.0 8.6 %collective-permute-done.7.refs_2_ = bf16[304,512]{1,0:T(8,128)(2,1)S(1)} collective-permute-done((bf16[304,512]{1,0:T(8,128)(2,1)S(1)}, bf16[304,512]{1,0:T(8,128)(2,1)S(1)}, u32[]{:S(2)}, u32[]{:S(2)}) %collective-permute-start.7) | collective-permute-done | bytes 311328 | tf_op jit(solution)/shard_map/ppermute | solution.py:25
  38.5 2.6 %collective-permute-start.1 = (bf16[304,128]{1,0:T(8,128)(2,1)S(1)}, bf16[304,128]{1,0:T(8,128)(2,1)S(1)}, u32[]{:S(2)}, u32[]{:S(2)}) collective-permute-start(bf16[304,128]{1,0:T(8,128)(2,1)S(1)} %get-tuple-element.24), channel_id=1, source_target_pairs={{0,2},{1,3},{2,0},{3,1},{4,6},{5,7},{6,4},{7,5},{8,10},{9,11},{10,... | collective-permute-start | bytes 233480 | tf_op jit(solution)/shard_map/ppermute | solution.py:25
  41.1 0.0 collective-permute-done.8.refs_3_
  41.1 1.1 %collective-permute-start.2 = (bf16[304,128]{1,0:T(8,128)(2,1)S(1)}, bf16[304,128]{1,0:T(8,128)(2,1)S(1)}, u32[]{:S(2)}, u32[]{:S(2)}) collective-permute-start(bf16[304,128]{1,0:T(8,128)(2,1)S(1)} %get-tuple-element.25), channel_id=1, source_target_pairs={{0,3},{1,2},{2,1},{3,0},{4,7},{5,6},{6,5},{7,4},{8,11},{9,10},{10,... | collective-permute-start | bytes 233480 | tf_op jit(solution)/shard_map/ppermute | solution.py:25
  42.1 3.5 %load_weights.1 = (bf16[4096,768]{1,0:T(8,128)(2,1)S(1)}, bf16[4096,256]{1,0:T(8,128)(2,1)S(1)}) custom-call(bf16[2,4096,512]{2,1,0:T(8,128)(2,1)} %refs_4_.1, bf16[2,4096,512]{2,1,0:T(8,128)(2,1)} %refs_5_.1, bf16[304,128]{1,0:T(8,128)(2,1)S(1)} %get-tuple-element.22.after_ref.refs_0_), custom_call_target="tpu_custom_call" | custom-call | tf_op jit(solution)/shard_map/load_weights/pallas_call | solution.py:152
  45.7 6.2 %shard_map.98.refs_5_ = f32[96,4096]{1,0:T(8,128)S(1)} custom-call(bf16[304,512]{1,0:T(8,128)(2,1)S(1)} %get-tuple-element.32.refs_0_.after_ref, bf16[304,512]{1,0:T(8,128)(2,1)S(1)} %collective-permute-done.6.refs_1_, bf16[304,512]{1,0:T(8,128)(2,1)S(1)} %collective-permute-done.7.refs_2_, bf16[304,512]{1,0:T(8,128)(2,1)S(1)} %collective-permute-done.8.refs_3_, ...), custom_call_target="tpu_custom_call" | custom-call | tf_op jit(solution)/shard_map/pallas_call | solution.py:216
  51.9 0.0 copy-start
  51.9 0.0 copy-start.1
  51.9 3.2 %shard_map.99.refs_5_ = f32[96,4096]{1,0:T(8,128)S(1)} custom-call(bf16[304,384]{1,0:T(8,128)(2,1)S(1)} %get-tuple-element.27.refs_0_, bf16[304,384]{1,0:T(8,128)(2,1)S(1)} %collective-permute-done.3.refs_1_, bf16[304,384]{1,0:T(8,128)(2,1)S(1)} %collective-permute-done.4.refs_2_, bf16[304,384]{1,0:T(8,128)(2,1)S(1)} %collective-permute-done.5.refs_3_, ...), custom_call_target="tpu_custom_call" | custom-call | tf_op jit(solution)/shard_map/pallas_call | solution.py:216
  55.1 0.0 collective-permute-done.refs_1_
  55.1 0.0 collective-permute-done.1.refs_2_
  55.1 1.3 %shard_map.100 = (f32[24,4096]{1,0:T(8,128)S(1)}, bf16[24,4096]{1,0:T(8,128)(2,1)S(1)}, bf16[24,4096]{1,0:T(8,128)(2,1)S(1)}, bf16[24,4096]{1,0:T(8,128)(2,1)S(1)}) custom-call(bf16[304,128]{1,0:T(8,128)(2,1)S(1)} %get-tuple-element.22.after_ref.refs_0_, bf16[304,128]{1,0:T(8,128)(2,1)S(1)} %collective-permute-done.refs_1_, ...), custom_call_target="tpu_custom_call" | custom-call | tf_op jit(solution)/shard_map/pallas_call | solution.py:216
  56.4 0.5 gain_terms.1
  56.9 0.1 collective-permute-start.16
  57.0 1.2 %collective-permute-done.16 = f32[1,4096]{1,0:T(1,128)S(1)} collective-permute-done((f32[1,4096]{1,0:T(1,128)S(1)}, f32[1,4096]{1,0:T(1,128)S(1)}, u32[]{:S(2)}, u32[]{:S(2)}) %collective-permute-start.16) | collective-permute-done | bytes 16416 | tf_op jit(solution)/shard_map/ppermute | solution.py:25
  58.2 1.5 %collective-permute-start.17 = (f32[1,4096]{1,0:T(1,128)S(1)}, f32[1,4096]{1,0:T(1,128)S(1)}, u32[]{:S(2)}, u32[]{:S(2)}) collective-permute-start(f32[1,4096]{1,0:T(1,128)S(1)} %add.15), channel_id=1, source_target_pairs={{0,8},{4,12},{8,0},{12,4},{16,24},{20,28},{24,16},{28,20},{1,9},{5... | collective-permute-start | bytes 49160 | tf_op jit(solution)/shard_map/ppermute | solution.py:25
  59.7 2.3 %collective-permute-done.17 = f32[1,4096]{1,0:T(1,128)S(1)} collective-permute-done((f32[1,4096]{1,0:T(1,128)S(1)}, f32[1,4096]{1,0:T(1,128)S(1)}, u32[]{:S(2)}, u32[]{:S(2)}) %collective-permute-start.17) | collective-permute-done | bytes 16416 | tf_op jit(solution)/shard_map/ppermute | solution.py:25
  62.0 2.6 %collective-permute-start.18 = (f32[1,4096]{1,0:T(1,128)S(1)}, f32[1,4096]{1,0:T(1,128)S(1)}, u32[]{:S(2)}, u32[]{:S(2)}) collective-permute-start(f32[1,4096]{1,0:T(1,128)S(1)} %add.16), channel_id=1, source_target_pairs={{0,16},{4,20},{8,24},{12,28},{16,0},{20,4},{24,8},{28,12},{1,17},{... | collective-permute-start | bytes 49160 | tf_op jit(solution)/shard_map/ppermute | solution.py:25
  64.5 2.1 %collective-permute-done.18 = f32[1,4096]{1,0:T(1,128)S(1)} collective-permute-done((f32[1,4096]{1,0:T(1,128)S(1)}, f32[1,4096]{1,0:T(1,128)S(1)}, u32[]{:S(2)}, u32[]{:S(2)}) %collective-permute-start.18) | collective-permute-done | bytes 16416 | tf_op jit(solution)/shard_map/ppermute | solution.py:25
  66.7 0.6 collective-permute-start.19
  67.3 3.2 %collective-permute-done.19 = f32[1,4096]{1,0:T(1,128)S(1)} collective-permute-done((f32[1,4096]{1,0:T(1,128)S(1)}, f32[1,4096]{1,0:T(1,128)S(1)}, u32[]{:S(2)}, u32[]{:S(2)}) %collective-permute-start.19) | collective-permute-done | bytes 16416 | tf_op jit(solution)/shard_map/ppermute | solution.py:25
  70.5 2.3 %collective-permute-start.20 = (f32[1,4096]{1,0:T(1,128)S(1)}, f32[1,4096]{1,0:T(1,128)S(1)}, u32[]{:S(2)}, u32[]{:S(2)}) collective-permute-start(f32[1,4096]{1,0:T(1,128)S(1)} %add.18), channel_id=1, source_target_pairs={{0,2},{1,3},{2,0},{3,1},{4,6},{5,7},{6,4},{7,5},{8,10},{9,11},{10,... | collective-permute-start | bytes 49160 | tf_op jit(solution)/shard_map/ppermute | solution.py:25
  72.8 0.4 collective-permute-start.9
  73.2 0.1 collective-permute-start.10
  73.3 3.0 %collective-permute-start.11 = (bf16[24,4096]{1,0:T(8,128)(2,1)S(1)}, bf16[24,4096]{1,0:T(8,128)(2,1)S(1)}, u32[]{:S(2)}, u32[]{:S(2)}) collective-permute-start(bf16[24,4096]{1,0:T(8,128)(2,1)S(1)} %get-tuple-element.39.refs_3_), channel_id=1, source_target_pairs={{0,3},{1,2},{2,1},{3,0},{4,7},{5,6},{6,5},{7,4},{8,11},{9,10},{10,... | collective-permute-start | bytes 589832 | tf_op jit(solution)/shard_map/ppermute | solution.py:25
  76.3 0.0 collective-permute-done.20
  76.3 0.6 add_multiply_fusion
  76.9 1.5 %collective-permute-done.9.refs_0_ = bf16[24,4096]{1,0:T(8,128)(2,1)S(1)} collective-permute-done((bf16[24,4096]{1,0:T(8,128)(2,1)S(1)}, bf16[24,4096]{1,0:T(8,128)(2,1)S(1)}, u32[]{:S(2)}, u32[]{:S(2)}) %collective-permute-start.9) | collective-permute-done | bytes 196640 | tf_op jit(solution)/shard_map/ppermute | solution.py:25
  78.5 2.5 %collective-permute-done.10.refs_1_ = bf16[24,4096]{1,0:T(8,128)(2,1)S(1)} collective-permute-done((bf16[24,4096]{1,0:T(8,128)(2,1)S(1)}, bf16[24,4096]{1,0:T(8,128)(2,1)S(1)}, u32[]{:S(2)}, u32[]{:S(2)}) %collective-permute-start.10) | collective-permute-done | bytes 196640 | tf_op jit(solution)/shard_map/ppermute | solution.py:25
  81.0 1.0 %finish.1 = bf16[1,24,4096]{2,1,0:T(8,128)(2,1)} custom-call(f32[24,4096]{1,0:T(8,128)S(1)} %get-tuple-element.36.own_ref.refs_0_, bf16[24,4096]{1,0:T(8,128)(2,1)S(1)} %collective-permute-done.9.refs_0_, bf16[24,4096]{1,0:T(8,128)(2,1)S(1)} %collective-permute-done.10.refs_1_, bf16[24,4096]{1,0:T(8,128)(2,1)S(1)} %collective-permute-done.11.refs_2_, ...), custom_call_target="tpu_custom_call" | custom-call | tf_op jit(solution)/shard_map/finish/pallas_call | solution.py:326
  (15 shorter events, 0.1 us)
Async XLA Ops:
  3.1 8.1 %collective-permute-start.12 = (bf16[24,2048]{1,0:T(8,128)(2,1)S(1)}, bf16[24,2048]{1,0:T(8,128)(2,1)S(1)}, u32[]{:S(2)}, u32[]{:S(2)}) collective-permute-start(bf16[24,2048]{1,0:T(8,128)(2,1)S(1)} %get-tuple-element.40.refs_4_), channel_id=1, source_target_pairs={{0,1},{1,0},{2,3},{3,2},{4,5},{5,4},{6,7},{7,6},{8,9},{9,8},{10,11... | collective-permute-start | bytes 294920 | tf_op jit(solution)/shard_map/ppermute | solution.py:25
  7.6 16.1 %collective-permute-start.3 = (bf16[304,384]{1,0:T(8,128)(2,1)S(1)}, bf16[304,384]{1,0:T(8,128)(2,1)S(1)}, u32[]{:S(2)}, u32[]{:S(2)}) collective-permute-start(bf16[304,384]{1,0:T(8,128)(2,1)S(1)} %get-tuple-element.28), channel_id=1, source_target_pairs={{0,1},{1,0},{2,3},{3,2},{4,5},{5,4},{6,7},{7,6},{8,9},{9,8},{10,11... | collective-permute-start | bytes 700424 | tf_op jit(solution)/shard_map/ppermute | solution.py:25
  7.7 17.5 %collective-permute-start.4 = (bf16[304,384]{1,0:T(8,128)(2,1)S(1)}, bf16[304,384]{1,0:T(8,128)(2,1)S(1)}, u32[]{:S(2)}, u32[]{:S(2)}) collective-permute-start(bf16[304,384]{1,0:T(8,128)(2,1)S(1)} %get-tuple-element.29), channel_id=1, source_target_pairs={{0,2},{1,3},{2,0},{3,1},{4,6},{5,7},{6,4},{7,5},{8,10},{9,11},{10,... | collective-permute-start | bytes 700424 | tf_op jit(solution)/shard_map/ppermute | solution.py:25
  9.7 17.0 %collective-permute-start.5 = (bf16[304,384]{1,0:T(8,128)(2,1)S(1)}, bf16[304,384]{1,0:T(8,128)(2,1)S(1)}, u32[]{:S(2)}, u32[]{:S(2)}) collective-permute-start(bf16[304,384]{1,0:T(8,128)(2,1)S(1)} %get-tuple-element.30), channel_id=1, source_target_pairs={{0,3},{1,2},{2,1},{3,0},{4,7},{5,6},{6,5},{7,4},{8,11},{9,10},{10,... | collective-permute-start | bytes 700424 | tf_op jit(solution)/shard_map/ppermute | solution.py:25
  11.2 17.2 %collective-permute-start.6 = (bf16[304,512]{1,0:T(8,128)(2,1)S(1)}, bf16[304,512]{1,0:T(8,128)(2,1)S(1)}, u32[]{:S(2)}, u32[]{:S(2)}) collective-permute-start(bf16[304,512]{1,0:T(8,128)(2,1)S(1)} %get-tuple-element.33), channel_id=1, source_target_pairs={{0,1},{1,0},{2,3},{3,2},{4,5},{5,4},{6,7},{7,6},{8,9},{9,8},{10,11... | collective-permute-start | bytes 933896 | tf_op jit(solution)/shard_map/ppermute | solution.py:25
  11.2 10.5 %collective-permute-start.14 = (bf16[24,2048]{1,0:T(8,128)(2,1)S(1)}, bf16[24,2048]{1,0:T(8,128)(2,1)S(1)}, u32[]{:S(2)}, u32[]{:S(2)}) collective-permute-start(bf16[24,2048]{1,0:T(8,128)(2,1)S(1)} %get-tuple-element.41.refs_7_), channel_id=1, source_target_pairs={{0,2},{1,3},{2,0},{3,1},{4,6},{5,7},{6,4},{7,5},{8,10},{9,11},{10,... | collective-permute-start | bytes 294920 | tf_op jit(solution)/shard_map/ppermute | solution.py:25
  21.8 16.7 %collective-permute-start.7 = (bf16[304,512]{1,0:T(8,128)(2,1)S(1)}, bf16[304,512]{1,0:T(8,128)(2,1)S(1)}, u32[]{:S(2)}, u32[]{:S(2)}) collective-permute-start(bf16[304,512]{1,0:T(8,128)(2,1)S(1)} %get-tuple-element.34), channel_id=1, source_target_pairs={{0,2},{1,3},{2,0},{3,1},{4,6},{5,7},{6,4},{7,5},{8,10},{9,11},{10,... | collective-permute-start | bytes 933896 | tf_op jit(solution)/shard_map/ppermute | solution.py:25
  23.7 17.4 %collective-permute-start.8 = (bf16[304,512]{1,0:T(8,128)(2,1)S(1)}, bf16[304,512]{1,0:T(8,128)(2,1)S(1)}, u32[]{:S(2)}, u32[]{:S(2)}) collective-permute-start(bf16[304,512]{1,0:T(8,128)(2,1)S(1)} %get-tuple-element.35), channel_id=1, source_target_pairs={{0,3},{1,2},{2,1},{3,0},{4,7},{5,6},{6,5},{7,4},{8,11},{9,10},{10,... | collective-permute-start | bytes 933896 | tf_op jit(solution)/shard_map/ppermute | solution.py:25
  25.2 31.2 %collective-permute-start.13 = (bf16[48,2048]{1,0:T(8,128)(2,1)S(1)}, bf16[48,2048]{1,0:T(8,128)(2,1)S(1)}, u32[]{:S(2)}, u32[]{:S(2)}) collective-permute-start(bf16[48,2048]{1,0:T(8,128)(2,1)S(1)} %pad_maximum_fusion), channel_id=1, source_target_pairs={{0,2},{1,3},{2,0},{3,1},{4,6},{5,7},{6,4},{7,5},{8,10},{9,11},{10,... | collective-permute-start | bytes 589832 | tf_op jit(solution)/shard_map/ppermute | solution.py:25
  26.8 29.6 %collective-permute-start.15 = (bf16[48,2048]{1,0:T(8,128)(2,1)S(1)}, bf16[48,2048]{1,0:T(8,128)(2,1)S(1)}, u32[]{:S(2)}, u32[]{:S(2)}) collective-permute-start(bf16[48,2048]{1,0:T(8,128)(2,1)S(1)} %pad_maximum_fusion.1), channel_id=1, source_target_pairs={{0,1},{1,0},{2,3},{3,2},{4,5},{5,4},{6,7},{7,6},{8,9},{9,8},{10,11... | collective-permute-start | bytes 589832 | tf_op jit(solution)/shard_map/ppermute | solution.py:25
  28.4 26.7 %collective-permute-start = (bf16[304,128]{1,0:T(8,128)(2,1)S(1)}, bf16[304,128]{1,0:T(8,128)(2,1)S(1)}, u32[]{:S(2)}, u32[]{:S(2)}) collective-permute-start(bf16[304,128]{1,0:T(8,128)(2,1)S(1)} %get-tuple-element.23), channel_id=1, source_target_pairs={{0,1},{1,0},{2,3},{3,2},{4,5},{5,4},{6,7},{7,6},{8,9},{9,8},{10,11... | collective-permute-start | bytes 233480 | tf_op jit(solution)/shard_map/ppermute | solution.py:25
  38.5 16.6 %collective-permute-start.1 = (bf16[304,128]{1,0:T(8,128)(2,1)S(1)}, bf16[304,128]{1,0:T(8,128)(2,1)S(1)}, u32[]{:S(2)}, u32[]{:S(2)}) collective-permute-start(bf16[304,128]{1,0:T(8,128)(2,1)S(1)} %get-tuple-element.24), channel_id=1, source_target_pairs={{0,2},{1,3},{2,0},{3,1},{4,6},{5,7},{6,4},{7,5},{8,10},{9,11},{10,... | collective-permute-start | bytes 233480 | tf_op jit(solution)/shard_map/ppermute | solution.py:25
  41.1 14.0 %collective-permute-start.2 = (bf16[304,128]{1,0:T(8,128)(2,1)S(1)}, bf16[304,128]{1,0:T(8,128)(2,1)S(1)}, u32[]{:S(2)}, u32[]{:S(2)}) collective-permute-start(bf16[304,128]{1,0:T(8,128)(2,1)S(1)} %get-tuple-element.25), channel_id=1, source_target_pairs={{0,3},{1,2},{2,1},{3,0},{4,7},{5,6},{6,5},{7,4},{8,11},{9,10},{10,... | collective-permute-start | bytes 233480 | tf_op jit(solution)/shard_map/ppermute | solution.py:25
  51.9 29.1 %copy-start = (bf16[1,24,4096]{2,1,0:T(8,128)(2,1)S(1)}, bf16[1,24,4096]{2,1,0:T(8,128)(2,1)}, u32[]{:S(2)}) copy-start(bf16[1,24,4096]{2,1,0:T(8,128)(2,1)} %src.1) | copy-start | bytes 589828
  51.9 29.1 %copy-start.1 = (f32[4096]{0:T(1024)S(1)}, f32[4096]{0:T(1024)}, u32[]{:S(2)}) copy-start(f32[4096]{0:T(1024)} %param.9) | copy-start | bytes 49156
  56.9 1.2 %collective-permute-start.16 = (f32[1,4096]{1,0:T(1,128)S(1)}, f32[1,4096]{1,0:T(1,128)S(1)}, u32[]{:S(2)}, u32[]{:S(2)}) collective-permute-start(f32[1,4096]{1,0:T(1,128)S(1)} %gain_terms.1), channel_id=1, source_target_pairs={{0,4},{4,0},{8,12},{12,8},{16,20},{20,16},{24,28},{28,24},{1,5},{5... | collective-permute-start | bytes 49160 | tf_op jit(solution)/shard_map/ppermute | solution.py:25
  58.2 3.8 %collective-permute-start.17 = (f32[1,4096]{1,0:T(1,128)S(1)}, f32[1,4096]{1,0:T(1,128)S(1)}, u32[]{:S(2)}, u32[]{:S(2)}) collective-permute-start(f32[1,4096]{1,0:T(1,128)S(1)} %add.15), channel_id=1, source_target_pairs={{0,8},{4,12},{8,0},{12,4},{16,24},{20,28},{24,16},{28,20},{1,9},{5... | collective-permute-start | bytes 49160 | tf_op jit(solution)/shard_map/ppermute | solution.py:25
  62.0 4.7 %collective-permute-start.18 = (f32[1,4096]{1,0:T(1,128)S(1)}, f32[1,4096]{1,0:T(1,128)S(1)}, u32[]{:S(2)}, u32[]{:S(2)}) collective-permute-start(f32[1,4096]{1,0:T(1,128)S(1)} %add.16), channel_id=1, source_target_pairs={{0,16},{4,20},{8,24},{12,28},{16,0},{20,4},{24,8},{28,12},{1,17},{... | collective-permute-start | bytes 49160 | tf_op jit(solution)/shard_map/ppermute | solution.py:25
  66.7 3.8 %collective-permute-start.19 = (f32[1,4096]{1,0:T(1,128)S(1)}, f32[1,4096]{1,0:T(1,128)S(1)}, u32[]{:S(2)}, u32[]{:S(2)}) collective-permute-start(f32[1,4096]{1,0:T(1,128)S(1)} %add.17), channel_id=1, source_target_pairs={{0,1},{1,0},{2,3},{3,2},{4,5},{5,4},{6,7},{7,6},{8,9},{9,8},{10,11... | collective-permute-start | bytes 49160 | tf_op jit(solution)/shard_map/ppermute | solution.py:25
  70.5 5.8 %collective-permute-start.20 = (f32[1,4096]{1,0:T(1,128)S(1)}, f32[1,4096]{1,0:T(1,128)S(1)}, u32[]{:S(2)}, u32[]{:S(2)}) collective-permute-start(f32[1,4096]{1,0:T(1,128)S(1)} %add.18), channel_id=1, source_target_pairs={{0,2},{1,3},{2,0},{3,1},{4,6},{5,7},{6,4},{7,5},{8,10},{9,11},{10,... | collective-permute-start | bytes 49160 | tf_op jit(solution)/shard_map/ppermute | solution.py:25
  72.8 5.7 %collective-permute-start.9 = (bf16[24,4096]{1,0:T(8,128)(2,1)S(1)}, bf16[24,4096]{1,0:T(8,128)(2,1)S(1)}, u32[]{:S(2)}, u32[]{:S(2)}) collective-permute-start(bf16[24,4096]{1,0:T(8,128)(2,1)S(1)} %get-tuple-element.37.refs_1_), channel_id=1, source_target_pairs={{0,1},{1,0},{2,3},{3,2},{4,5},{5,4},{6,7},{7,6},{8,9},{9,8},{10,11... | collective-permute-start | bytes 589832 | tf_op jit(solution)/shard_map/ppermute | solution.py:25
  73.2 7.8 %collective-permute-start.10 = (bf16[24,4096]{1,0:T(8,128)(2,1)S(1)}, bf16[24,4096]{1,0:T(8,128)(2,1)S(1)}, u32[]{:S(2)}, u32[]{:S(2)}) collective-permute-start(bf16[24,4096]{1,0:T(8,128)(2,1)S(1)} %get-tuple-element.38.refs_2_), channel_id=1, source_target_pairs={{0,2},{1,3},{2,0},{3,1},{4,6},{5,7},{6,4},{7,5},{8,10},{9,11},{10,... | collective-permute-start | bytes 589832 | tf_op jit(solution)/shard_map/ppermute | solution.py:25
  73.3 7.7 %collective-permute-start.11 = (bf16[24,4096]{1,0:T(8,128)(2,1)S(1)}, bf16[24,4096]{1,0:T(8,128)(2,1)S(1)}, u32[]{:S(2)}, u32[]{:S(2)}) collective-permute-start(bf16[24,4096]{1,0:T(8,128)(2,1)S(1)} %get-tuple-element.39.refs_3_), channel_id=1, source_target_pairs={{0,3},{1,2},{2,1},{3,0},{4,7},{5,6},{6,5},{7,4},{8,11},{9,10},{10,... | collective-permute-start | bytes 589832 | tf_op jit(solution)/shard_map/ppermute | solution.py:25

commit v3 on v2

--- a/solution.py
+++ b/solution.py
@@ -12,7 +12,6 @@
 ATTN_ROWS = 512
 PACK_VMEM = 8 << 20
 LAYER_VMEM = 24 << 20
-SMALL_VMEM = 2 << 20
 F32 = jnp.float32
 BF16 = jnp.bfloat16
 
@@ -223,88 +222,72 @@
     )(*bufs, *weights, *tail)
 
 
-def split_final(enc_final, after):
-    enc, half = enc_final.shape[1], enc_final.shape[2] // 2
-
-    def kernel(src, after_ref, *rest):
-        outs, sems = rest[:2], rest[2]
-        copies = [
-            pltpu.make_async_copy(src.at[0, :, pl.ds(h * half, half)], outs[h], sems.at[h])
-            for h in range(2)
-        ]
-        for c in copies:
-            c.start()
-        for c in copies:
-            c.wait()
-
-    return pl.pallas_call(
-        kernel,
-        out_shape=[jax.ShapeDtypeStruct((enc, half), BF16)] * 2,
-        in_specs=[pl.BlockSpec(memory_space=pltpu.HBM), pl.BlockSpec(memory_space=pl.ANY)],
-        out_specs=[pl.BlockSpec(memory_space=pltpu.VMEM)] * 2,
-        scratch_shapes=[pltpu.SemaphoreType.DMA((2,))],
-        compiler_params=pltpu.CompilerParams(vmem_limit_bytes=SMALL_VMEM),
-        name="split_final",
-    )(*in_hbm([enc_final]), after)
-
-
-def gather_rows(mine, seq_size, steps):
-    have = [(0, mine)]
-    for n, step in enumerate(steps):
-        whole = have[0][1] if n == 0 else jnp.concatenate([a for _, a in have], axis=0)
-        have = have + [(step, exchange(whole, "seq", seq_size, step))]
-    return have
-
-
-def row_order(steps):
-    order = [0]
-    for step in steps:
-        order = order + [j ^ step for j in order]
-    return order
-
-
-def gain_terms(pieces, halves, orders):
+def gather_rows(enc_final, seq_size):
+    enc, width = enc_final.shape[1], enc_final.shape[2]
+    rows = {0: [(enc_final, 0, 0, width)]}
+    if seq_size == 4:
+        half = width // 2
+        near = {j: exchange(enc_final, "seq", seq_size, j) for j in (1, 2)}
+        for j in (1, 2):
+            rows[j] = [(near[j], 0, 0, width)]
+        sends = [near[1][:, :, :half], near[2][:, :, half:]]
+        low = exchange(sends[0], "seq", seq_size, 2)
+        high = exchange(sends[1], "seq", seq_size, 1)
+        rows[3] = [(low, 0, 0, half), (high, 0, half, half)]
+        return rows
+    have, order = [enc_final], [0]
+    step = 1
+    while step < seq_size:
+        whole = jnp.concatenate(have, axis=1) if len(have) > 1 else have[0]
+        got = exchange(whole, "seq", seq_size, step)
+        for place, j in enumerate(order):
+            rows[j ^ step] = [(got, place * enc, 0, width)]
+        have, order = have + [got], order + [j ^ step for j in order]
+        step *= 2
+    return rows
+
+
+def gain_terms(pieces, rows):
     count = len(pieces)
     enc, width = pieces[0].shape
-    half = width // 2
-    sizes = [len(parts) for parts in halves]
+    arrays = []
+    places = []
+    for j in range(count):
+        spots = []
+        for array, base, first, cols in rows[j]:
+            known = [n for n, a in enumerate(arrays) if a is array]
+            if not known:
+                arrays.append(array)
+                known = [len(arrays) - 1]
+            spots.append((known[0], base, first, cols))
+        places.append(spots)
+    cuts = sorted({first for spots in places for _, _, first, _ in spots} | {width})
 
     def kernel(*refs):
-        piece_refs = refs[:count]
-        part_refs = [refs[count : count + sizes[0]], refs[count + sizes[0] : count + sum(sizes)]]
-        out_ref = refs[-1]
-        blocks = [[None] * count, [None] * count]
-        for h in range(2):
-            place = 0
-            for ref in part_refs[h]:
-                for k in range(ref.shape[0] // enc):
-                    blocks[h][orders[h][place]] = (ref, k * enc)
-                    place += 1
+        piece_refs, row_refs, out_ref = refs[:count], refs[count:-1], refs[-1]
         inv = []
-        for j in range(count):
-            square = None
-            for h in range(2):
-                ref, base = blocks[h][j]
-                x = ref[pl.ds(base, enc), :].astype(F32)
-                total = jnp.sum(x * x, axis=-1, keepdims=True)
-                square = total if square is None else square + total
+        for spots in places:
+            square = 0.0
+            for n, base, _, cols in spots:
+                x = row_refs[n][0, pl.ds(base, enc), :].astype(F32)
+                square = square + jnp.sum(x * x, axis=-1, keepdims=True)
             inv.append(lax.rsqrt(square * (1.0 / width) + 1e-06))
-        for h in range(2):
-            hs = slice(h * half, (h + 1) * half)
+        for low, high in zip(cuts[:-1], cuts[1:]):
             terms = None
-            for j in range(count):
-                ref, base = blocks[h][j]
-                normed = ref[pl.ds(base, enc), :].astype(F32) * inv[j]
-                product = piece_refs[j][:, hs].astype(F32) * normed
-                terms = product if terms is None else terms + product
-            out_ref[:, hs] = jnp.sum(terms, axis=0, keepdims=True)
+            for j, spots in enumerate(places):
+                for n, base, first, cols in spots:
+                    if first <= low and high <= first + cols:
+                        x = row_refs[n][0, pl.ds(base, enc), pl.ds(low - first, high - low)]
+                        product = piece_refs[j][:, low:high].astype(F32) * (x.astype(F32) * inv[j])
+                        terms = product if terms is None else terms + product
+            out_ref[:, low:high] = jnp.sum(terms, axis=0, keepdims=True)
 
     return pl.pallas_call(
         kernel,
         out_shape=jax.ShapeDtypeStruct((1, width), F32),
         compiler_params=pltpu.CompilerParams(vmem_limit_bytes=PACK_VMEM),
         name="gain_terms",
-    )(*pieces, *[a for parts in halves for a in parts])
+    )(*pieces, *arrays)
 
 
 def finish(own, received, enc_final, norm_gain):
@@ -340,15 +323,14 @@
     dec, enc = dec_queries.shape[2], enc_keys.shape[2]
     arrays = (dec_queries, out_grad, enc_keys, enc_values)
     chunks = plan_chunks(layers, key_weight.shape[2])
+    rows = gather_rows(enc_final, seq)
     gathered = []
-    for index, chunk in enumerate(chunks):
+    for chunk in chunks:
         bufs = pack_chunk(chunk, arrays, seq)
-        gathered.append([bufs[0]] + [exchange(bufs[j], "seq", seq, j) for j in range(1, seq)])
-        if index == 0:
-            steps = [1 << b for b in range(seq.bit_length() - 1)]
-            orders = [steps, steps[::-1]]
-            finals = split_final(enc_final, bufs[0])
-            halves = [gather_rows(f, seq, o) for f, o in zip(finals, orders)]
+        moved = [bufs[0]]
+        for j in range(1, seq):
+            moved.append(exchange(bufs[j], "seq", seq, j))
+        gathered.append(moved)
     ready = load_weights(chunks[1:], key_weight, value_weight, gathered[-1][0])
     prior = None
     for index in range(len(chunks)):
@@ -358,9 +340,7 @@
         )
         prior = outs[0]
     received = [exchange(outs[j], "seq", seq, j) for j in range(1, seq)]
-    gain = gain_terms(
-        outs, [[a for _, a in parts] for parts in halves], [row_order(o) for o in orders]
-    )
+    gain = gain_terms(outs, rows)
     enc_grad = finish(outs[0], received, enc_final, norm_gain)
     stages = [
         (axis, size, 1 << b)

time: 82.3 us -> 82.2 us (level)
  waiting for transfers between devices: 30 us -> 31.1 us
  Pallas kernels: 20.6 us -> 19.7 us
    ppermute x21, waiting for transfers between devices: 30 us -> 31.1 us  [exchange(): return lax.ppermute(value, axis, xor_pairs(size, step))]
    pallas_call x1 -> x0, Pallas kernels: 0.96 us -> none  [split_final(): pl.pallas_call(kernel, out_shape=[jax.ShapeDtypeStruct((enc, half), BF16)...]
  transfers between devices with their start and end apart: 21 -> 21, of which waited for: 8 -> 9; matrix products, arithmetic and copies ran while one was open for 1% -> 1% of each run, Pallas kernels for 20% -> 22%
where the time goes in v3:
time: 82.2 us; the launch traced here: 81.9 us
  waiting for transfers between devices  31.1 us (38%)
  starting transfers between devices  29.6 us (36%)
  Pallas kernels  19.7 us (24%)
    ppermute x21, waiting for transfers between devices, exchange(): return lax.ppermute(value, axis, xor_pairs(size, step))  31.1 us
    ppermute x21, starting transfers between devices, exchange(): return lax.ppermute(value, axis, xor_pairs(size, step))  29.6 us
    pallas_call x3, Pallas kernels, chunk_terms(): pl.pallas_call(kernel, out_shape=out_shape, in_specs=[vmem] * count + spe...  10.6 us
    pallas_call x3, Pallas kernels, pack_chunk(): pl.pallas_call(kernel, out_shape=[jax.ShapeDtypeStruct((sum(rows), width)...  4.02 us
    pallas_call x1, Pallas kernels, load_weights(): pl.pallas_call(kernel, out_shape=[jax.ShapeDtypeStruct((width, 2 * cols),...  3.55 us
  transfers between devices with their start and end apart: 21, of which 9 were waited for; matrix products, arithmetic and copies ran while one was open for 1% of the time, Pallas kernels for 22%

profile of v3, /device:TPU:0, one launch (start us, length us, event | category | flops | bytes accessed | tf_op | source)
XLA Modules:
  0.0 81.9 jit_solution(6986511237922137183)
XLA Ops:
  0.6 3.0 %collective-permute-start.12 = (bf16[1,24,4096]{2,1,0:T(8,128)(2,1)}, bf16[1,24,4096]{2,1,0:T(8,128)(2,1)S(1)}, u32[]{:S(2)}, u32[]{:S(2)}) collective-permute-start(bf16[1,24,4096]{2,1,0:T(8,128)(2,1)} %refs_4_.3), channel_id=1, source_target_pairs={{0,1},{1,0},{2,3},{3,2},{4,5},{5,4},{6,7},{7,6},{8,9},{9,8},{10,11... | collective-permute-start | bytes 589832 | tf_op jit(solution)/shard_map/ppermute | solution.py:24
  3.7 1.4 %shard_map.96 = (bf16[304,384]{1,0:T(8,128)(2,1)S(1)}, bf16[304,384]{1,0:T(8,128)(2,1)S(1)}, bf16[304,384]{1,0:T(8,128)(2,1)S(1)}, bf16[304,384]{1,0:T(8,128)(2,1)S(1)}) custom-call(bf16[2,1,128,2048]{3,2,1,0:T(8,128)(2,1)} %q_ref.5, bf16[2,1,128,2048]{3,2,1,0:T(8,128)(2,1)} %g_ref.5, bf16[2,1,24,2048]{3,2,1,0:T(8,128)(2,1)} %k_ref.5, ...), custom_call_target="tpu_custom_call" | custom-call | tf_op jit(solution)/shard_map/pallas_call | solution.py:64
  5.1 0.1 collective-permute-start.3
  5.2 2.0 %collective-permute-start.13 = (bf16[1,24,4096]{2,1,0:T(8,128)(2,1)}, bf16[1,24,4096]{2,1,0:T(8,128)(2,1)S(1)}, u32[]{:S(2)}, u32[]{:S(2)}) collective-permute-start(bf16[1,24,4096]{2,1,0:T(8,128)(2,1)} %refs_4_.3), channel_id=1, source_target_pairs={{0,2},{1,3},{2,0},{3,1},{4,6},{5,7},{6,4},{7,5},{8,10},{9,11},{10,... | collective-permute-start | bytes 589832 | tf_op jit(solution)/shard_map/ppermute | solution.py:24
  7.2 1.5 %shard_map.97 = (bf16[304,512]{1,0:T(8,128)(2,1)S(1)}, bf16[304,512]{1,0:T(8,128)(2,1)S(1)}, bf16[304,512]{1,0:T(8,128)(2,1)S(1)}, bf16[304,512]{1,0:T(8,128)(2,1)S(1)}) custom-call(bf16[2,1,128,2048]{3,2,1,0:T(8,128)(2,1)} %q_ref.5, bf16[2,1,128,2048]{3,2,1,0:T(8,128)(2,1)} %g_ref.5, bf16[2,1,24,2048]{3,2,1,0:T(8,128)(2,1)} %k_ref.5, ...), custom_call_target="tpu_custom_call" | custom-call | tf_op jit(solution)/shard_map/pallas_call | solution.py:64
  8.7 1.6 %collective-permute-start.6 = (bf16[304,512]{1,0:T(8,128)(2,1)S(1)}, bf16[304,512]{1,0:T(8,128)(2,1)S(1)}, u32[]{:S(2)}, u32[]{:S(2)}) collective-permute-start(bf16[304,512]{1,0:T(8,128)(2,1)S(1)} %get-tuple-element.31), channel_id=1, source_target_pairs={{0,1},{1,0},{2,3},{3,2},{4,5},{5,4},{6,7},{7,6},{8,9},{9,8},{10,11... | collective-permute-start | bytes 933896 | tf_op jit(solution)/shard_map/ppermute | solution.py:24
  10.3 0.5 collective-permute-start.7
  10.8 0.0 collective-permute-done.12.refs_5_
  10.8 1.8 %collective-permute-start.8 = (bf16[304,512]{1,0:T(8,128)(2,1)S(1)}, bf16[304,512]{1,0:T(8,128)(2,1)S(1)}, u32[]{:S(2)}, u32[]{:S(2)}) collective-permute-start(bf16[304,512]{1,0:T(8,128)(2,1)S(1)} %get-tuple-element.33), channel_id=1, source_target_pairs={{0,3},{1,2},{2,1},{3,0},{4,7},{5,6},{6,5},{7,4},{8,11},{9,10},{10,... | collective-permute-start | bytes 933896 | tf_op jit(solution)/shard_map/ppermute | solution.py:24
  12.6 2.3 %collective-permute-start.4 = (bf16[304,384]{1,0:T(8,128)(2,1)S(1)}, bf16[304,384]{1,0:T(8,128)(2,1)S(1)}, u32[]{:S(2)}, u32[]{:S(2)}) collective-permute-start(bf16[304,384]{1,0:T(8,128)(2,1)S(1)} %get-tuple-element.27), channel_id=1, source_target_pairs={{0,2},{1,3},{2,0},{3,1},{4,6},{5,7},{6,4},{7,5},{8,10},{9,11},{10,... | collective-permute-start | bytes 700424 | tf_op jit(solution)/shard_map/ppermute | solution.py:24
  14.9 0.0 collective-permute-done.3.refs_1_
  14.9 2.7 %collective-permute-start.5 = (bf16[304,384]{1,0:T(8,128)(2,1)S(1)}, bf16[304,384]{1,0:T(8,128)(2,1)S(1)}, u32[]{:S(2)}, u32[]{:S(2)}) collective-permute-start(bf16[304,384]{1,0:T(8,128)(2,1)S(1)} %get-tuple-element.28), channel_id=1, source_target_pairs={{0,3},{1,2},{2,1},{3,0},{4,7},{5,6},{6,5},{7,4},{8,11},{9,10},{10,... | collective-permute-start | bytes 700424 | tf_op jit(solution)/shard_map/ppermute | solution.py:24
  17.6 17.5 %collective-permute-done.4.refs_2_ = bf16[304,384]{1,0:T(8,128)(2,1)S(1)} collective-permute-done((bf16[304,384]{1,0:T(8,128)(2,1)S(1)}, bf16[304,384]{1,0:T(8,128)(2,1)S(1)}, u32[]{:S(2)}, u32[]{:S(2)}) %collective-permute-start.4) | collective-permute-done | bytes 233504 | tf_op jit(solution)/shard_map/ppermute | solution.py:24
  35.2 1.7 %collective-permute-start.14 = (bf16[1,24,2048]{2,1,0:T(8,128)(2,1)S(1)}, bf16[1,24,2048]{2,1,0:T(8,128)(2,1)S(1)}, u32[]{:S(2)}, u32[]{:S(2)}) collective-permute-start(bf16[1,24,2048]{2,1,0:T(8,128)(2,1)S(1)} %slice.8), channel_id=1, source_target_pairs={{0,2},{1,3},{2,0},{3,1},{4,6},{5,7},{6,4},{7,5},{8,10},{9,11},{10,... | collective-permute-start | bytes 294920 | tf_op jit(solution)/shard_map/ppermute | solution.py:24
  36.9 0.0 collective-permute-done.5.refs_3_
  36.9 1.5 %collective-permute-start.15 = (bf16[1,24,2048]{2,1,0:T(8,128)(2,1)S(1)}, bf16[1,24,2048]{2,1,0:T(8,128)(2,1)S(1)}, u32[]{:S(2)}, u32[]{:S(2)}) collective-permute-start(bf16[1,24,2048]{2,1,0:T(8,128)(2,1)S(1)} %slice.9), channel_id=1, source_target_pairs={{0,1},{1,0},{2,3},{3,2},{4,5},{5,4},{6,7},{7,6},{8,9},{9,8},{10,11... | collective-permute-start | bytes 294920 | tf_op jit(solution)/shard_map/ppermute | solution.py:24
  38.3 1.1 %shard_map.95 = (bf16[304,128]{1,0:T(8,128)(2,1)S(1)}, bf16[304,128]{1,0:T(8,128)(2,1)S(1)}, bf16[304,128]{1,0:T(8,128)(2,1)S(1)}, bf16[304,128]{1,0:T(8,128)(2,1)S(1)}) custom-call(bf16[2,1,128,2048]{3,2,1,0:T(8,128)(2,1)} %q_ref.5, bf16[2,1,128,2048]{3,2,1,0:T(8,128)(2,1)} %g_ref.5, bf16[2,1,24,2048]{3,2,1,0:T(8,128)(2,1)} %k_ref.5, ...), custom_call_target="tpu_custom_call" | custom-call | tf_op jit(solution)/shard_map/pallas_call | solution.py:64
  39.4 0.0 collective-permute-done.6.refs_1_
  39.5 0.6 collective-permute-start
  40.1 0.3 collective-permute-start.1
  40.4 0.0 collective-permute-done.8.refs_3_
  40.4 2.6 %collective-permute-start.2 = (bf16[304,128]{1,0:T(8,128)(2,1)S(1)}, bf16[304,128]{1,0:T(8,128)(2,1)S(1)}, u32[]{:S(2)}, u32[]{:S(2)}) collective-permute-start(bf16[304,128]{1,0:T(8,128)(2,1)S(1)} %get-tuple-element.23), channel_id=1, source_target_pairs={{0,3},{1,2},{2,1},{3,0},{4,7},{5,6},{6,5},{7,4},{8,11},{9,10},{10,... | collective-permute-start | bytes 233480 | tf_op jit(solution)/shard_map/ppermute | solution.py:24
  43.0 3.5 %load_weights.1 = (bf16[4096,768]{1,0:T(8,128)(2,1)S(1)}, bf16[4096,256]{1,0:T(8,128)(2,1)S(1)}) custom-call(bf16[2,4096,512]{2,1,0:T(8,128)(2,1)} %refs_4_.2, bf16[2,4096,512]{2,1,0:T(8,128)(2,1)} %refs_5_.1, bf16[304,128]{1,0:T(8,128)(2,1)S(1)} %get-tuple-element.20.after_ref.refs_0_), custom_call_target="tpu_custom_call" | custom-call | tf_op jit(solution)/shard_map/load_weights/pallas_call | solution.py:151
  46.6 6.1 %shard_map.98.refs_5_ = f32[96,4096]{1,0:T(8,128)S(1)} custom-call(bf16[304,512]{1,0:T(8,128)(2,1)S(1)} %get-tuple-element.30.refs_0_, bf16[304,512]{1,0:T(8,128)(2,1)S(1)} %collective-permute-done.6.refs_1_, bf16[304,512]{1,0:T(8,128)(2,1)S(1)} %collective-permute-done.7.refs_2_, bf16[304,512]{1,0:T(8,128)(2,1)S(1)} %collective-permute-done.8.refs_3_, ...), custom_call_target="tpu_custom_call" | custom-call | tf_op jit(solution)/shard_map/pallas_call | solution.py:215
  52.7 0.0 copy-start
  52.7 0.0 copy-start.1
  52.7 3.2 %shard_map.99.refs_5_ = f32[96,4096]{1,0:T(8,128)S(1)} custom-call(bf16[304,384]{1,0:T(8,128)(2,1)S(1)} %get-tuple-element.25.refs_0_, bf16[304,384]{1,0:T(8,128)(2,1)S(1)} %collective-permute-done.3.refs_1_, bf16[304,384]{1,0:T(8,128)(2,1)S(1)} %collective-permute-done.4.refs_2_, bf16[304,384]{1,0:T(8,128)(2,1)S(1)} %collective-permute-done.5.refs_3_, ...), custom_call_target="tpu_custom_call" | custom-call | tf_op jit(solution)/shard_map/pallas_call | solution.py:215
  55.9 0.0 collective-permute-done.refs_1_
  56.0 1.3 %shard_map.100 = (f32[24,4096]{1,0:T(8,128)S(1)}, bf16[24,4096]{1,0:T(8,128)(2,1)S(1)}, bf16[24,4096]{1,0:T(8,128)(2,1)S(1)}, bf16[24,4096]{1,0:T(8,128)(2,1)S(1)}) custom-call(bf16[304,128]{1,0:T(8,128)(2,1)S(1)} %get-tuple-element.20.after_ref.refs_0_, bf16[304,128]{1,0:T(8,128)(2,1)S(1)} %collective-permute-done.refs_1_, ...), custom_call_target="tpu_custom_call" | custom-call | tf_op jit(solution)/shard_map/pallas_call | solution.py:215
  57.3 0.5 gain_terms.1
  57.8 0.1 collective-permute-start.16
  57.8 1.2 %collective-permute-done.16 = f32[1,4096]{1,0:T(1,128)S(1)} collective-permute-done((f32[1,4096]{1,0:T(1,128)S(1)}, f32[1,4096]{1,0:T(1,128)S(1)}, u32[]{:S(2)}, u32[]{:S(2)}) %collective-permute-start.16) | collective-permute-done | bytes 16416 | tf_op jit(solution)/shard_map/ppermute | solution.py:24
  59.0 1.7 %collective-permute-start.17 = (f32[1,4096]{1,0:T(1,128)S(1)}, f32[1,4096]{1,0:T(1,128)S(1)}, u32[]{:S(2)}, u32[]{:S(2)}) collective-permute-start(f32[1,4096]{1,0:T(1,128)S(1)} %add.15), channel_id=1, source_target_pairs={{0,8},{4,12},{8,0},{12,4},{16,24},{20,28},{24,16},{28,20},{1,9},{5... | collective-permute-start | bytes 49160 | tf_op jit(solution)/shard_map/ppermute | solution.py:24
  60.7 2.2 %collective-permute-done.17 = f32[1,4096]{1,0:T(1,128)S(1)} collective-permute-done((f32[1,4096]{1,0:T(1,128)S(1)}, f32[1,4096]{1,0:T(1,128)S(1)}, u32[]{:S(2)}, u32[]{:S(2)}) %collective-permute-start.17) | collective-permute-done | bytes 16416 | tf_op jit(solution)/shard_map/ppermute | solution.py:24
  62.9 2.7 %collective-permute-start.18 = (f32[1,4096]{1,0:T(1,128)S(1)}, f32[1,4096]{1,0:T(1,128)S(1)}, u32[]{:S(2)}, u32[]{:S(2)}) collective-permute-start(f32[1,4096]{1,0:T(1,128)S(1)} %add.16), channel_id=1, source_target_pairs={{0,16},{4,20},{8,24},{12,28},{16,0},{20,4},{24,8},{28,12},{1,17},{... | collective-permute-start | bytes 49160 | tf_op jit(solution)/shard_map/ppermute | solution.py:24
  65.5 2.0 %collective-permute-done.18 = f32[1,4096]{1,0:T(1,128)S(1)} collective-permute-done((f32[1,4096]{1,0:T(1,128)S(1)}, f32[1,4096]{1,0:T(1,128)S(1)}, u32[]{:S(2)}, u32[]{:S(2)}) %collective-permute-start.18) | collective-permute-done | bytes 16416 | tf_op jit(solution)/shard_map/ppermute | solution.py:24
  67.6 0.6 collective-permute-start.19
  68.2 3.4 %collective-permute-done.19 = f32[1,4096]{1,0:T(1,128)S(1)} collective-permute-done((f32[1,4096]{1,0:T(1,128)S(1)}, f32[1,4096]{1,0:T(1,128)S(1)}, u32[]{:S(2)}, u32[]{:S(2)}) %collective-permute-start.19) | collective-permute-done | bytes 16416 | tf_op jit(solution)/shard_map/ppermute | solution.py:24
  71.6 0.4 collective-permute-start.20
  72.0 0.4 collective-permute-start.9
  72.3 1.9 %collective-permute-start.10 = (bf16[24,4096]{1,0:T(8,128)(2,1)S(1)}, bf16[24,4096]{1,0:T(8,128)(2,1)S(1)}, u32[]{:S(2)}, u32[]{:S(2)}) collective-permute-start(bf16[24,4096]{1,0:T(8,128)(2,1)S(1)} %get-tuple-element.36.refs_2_), channel_id=1, source_target_pairs={{0,2},{1,3},{2,0},{3,1},{4,6},{5,7},{6,4},{7,5},{8,10},{9,11},{10,... | collective-permute-start | bytes 589832 | tf_op jit(solution)/shard_map/ppermute | solution.py:24
  74.2 1.3 %collective-permute-start.11 = (bf16[24,4096]{1,0:T(8,128)(2,1)S(1)}, bf16[24,4096]{1,0:T(8,128)(2,1)S(1)}, u32[]{:S(2)}, u32[]{:S(2)}) collective-permute-start(bf16[24,4096]{1,0:T(8,128)(2,1)S(1)} %get-tuple-element.37.refs_3_), channel_id=1, source_target_pairs={{0,3},{1,2},{2,1},{3,0},{4,7},{5,6},{6,5},{7,4},{8,11},{9,10},{10,... | collective-permute-start | bytes 589832 | tf_op jit(solution)/shard_map/ppermute | solution.py:24
  75.5 0.9 %collective-permute-done.20 = f32[1,4096]{1,0:T(1,128)S(1)} collective-permute-done((f32[1,4096]{1,0:T(1,128)S(1)}, f32[1,4096]{1,0:T(1,128)S(1)}, u32[]{:S(2)}, u32[]{:S(2)}) %collective-permute-start.20) | collective-permute-done | bytes 16416 | tf_op jit(solution)/shard_map/ppermute | solution.py:24
  76.4 0.6 add_multiply_fusion
  77.0 0.7 collective-permute-done.9.refs_0_
  77.6 1.9 %collective-permute-done.10.refs_1_ = bf16[24,4096]{1,0:T(8,128)(2,1)S(1)} collective-permute-done((bf16[24,4096]{1,0:T(8,128)(2,1)S(1)}, bf16[24,4096]{1,0:T(8,128)(2,1)S(1)}, u32[]{:S(2)}, u32[]{:S(2)}) %collective-permute-start.10) | collective-permute-done | bytes 196640 | tf_op jit(solution)/shard_map/ppermute | solution.py:24
  79.5 1.4 %collective-permute-done.11.refs_2_ = bf16[24,4096]{1,0:T(8,128)(2,1)S(1)} collective-permute-done((bf16[24,4096]{1,0:T(8,128)(2,1)S(1)}, bf16[24,4096]{1,0:T(8,128)(2,1)S(1)}, u32[]{:S(2)}, u32[]{:S(2)}) %collective-permute-start.11) | collective-permute-done | bytes 196640 | tf_op jit(solution)/shard_map/ppermute | solution.py:24
  80.9 1.0 %finish.1 = bf16[1,24,4096]{2,1,0:T(8,128)(2,1)} custom-call(f32[24,4096]{1,0:T(8,128)S(1)} %get-tuple-element.34.own_ref.refs_0_, bf16[24,4096]{1,0:T(8,128)(2,1)S(1)} %collective-permute-done.9.refs_0_, bf16[24,4096]{1,0:T(8,128)(2,1)S(1)} %collective-permute-done.10.refs_1_, bf16[24,4096]{1,0:T(8,128)(2,1)S(1)} %collective-permute-done.11.refs_2_, ...), custom_call_target="tpu_custom_call" | custom-call | tf_op jit(solution)/shard_map/finish/pallas_call | solution.py:309
  (14 shorter events, 0.1 us)
Async XLA Ops:
  0.6 10.2 %collective-permute-start.12 = (bf16[1,24,4096]{2,1,0:T(8,128)(2,1)}, bf16[1,24,4096]{2,1,0:T(8,128)(2,1)S(1)}, u32[]{:S(2)}, u32[]{:S(2)}) collective-permute-start(bf16[1,24,4096]{2,1,0:T(8,128)(2,1)} %refs_4_.3), channel_id=1, source_target_pairs={{0,1},{1,0},{2,3},{3,2},{4,5},{5,4},{6,7},{7,6},{8,9},{9,8},{10,11... | collective-permute-start | bytes 589832 | tf_op jit(solution)/shard_map/ppermute | solution.py:24
  5.1 9.8 %collective-permute-start.3 = (bf16[304,384]{1,0:T(8,128)(2,1)S(1)}, bf16[304,384]{1,0:T(8,128)(2,1)S(1)}, u32[]{:S(2)}, u32[]{:S(2)}) collective-permute-start(bf16[304,384]{1,0:T(8,128)(2,1)S(1)} %get-tuple-element.26), channel_id=1, source_target_pairs={{0,1},{1,0},{2,3},{3,2},{4,5},{5,4},{6,7},{7,6},{8,9},{9,8},{10,11... | collective-permute-start | bytes 700424 | tf_op jit(solution)/shard_map/ppermute | solution.py:24
  5.2 7.4 %collective-permute-start.13 = (bf16[1,24,4096]{2,1,0:T(8,128)(2,1)}, bf16[1,24,4096]{2,1,0:T(8,128)(2,1)S(1)}, u32[]{:S(2)}, u32[]{:S(2)}) collective-permute-start(bf16[1,24,4096]{2,1,0:T(8,128)(2,1)} %refs_4_.3), channel_id=1, source_target_pairs={{0,2},{1,3},{2,0},{3,1},{4,6},{5,7},{6,4},{7,5},{8,10},{9,11},{10,... | collective-permute-start | bytes 589832 | tf_op jit(solution)/shard_map/ppermute | solution.py:24
  8.7 30.7 %collective-permute-start.6 = (bf16[304,512]{1,0:T(8,128)(2,1)S(1)}, bf16[304,512]{1,0:T(8,128)(2,1)S(1)}, u32[]{:S(2)}, u32[]{:S(2)}) collective-permute-start(bf16[304,512]{1,0:T(8,128)(2,1)S(1)} %get-tuple-element.31), channel_id=1, source_target_pairs={{0,1},{1,0},{2,3},{3,2},{4,5},{5,4},{6,7},{7,6},{8,9},{9,8},{10,11... | collective-permute-start | bytes 933896 | tf_op jit(solution)/shard_map/ppermute | solution.py:24
  10.3 29.8 %collective-permute-start.7 = (bf16[304,512]{1,0:T(8,128)(2,1)S(1)}, bf16[304,512]{1,0:T(8,128)(2,1)S(1)}, u32[]{:S(2)}, u32[]{:S(2)}) collective-permute-start(bf16[304,512]{1,0:T(8,128)(2,1)S(1)} %get-tuple-element.32), channel_id=1, source_target_pairs={{0,2},{1,3},{2,0},{3,1},{4,6},{5,7},{6,4},{7,5},{8,10},{9,11},{10,... | collective-permute-start | bytes 933896 | tf_op jit(solution)/shard_map/ppermute | solution.py:24
  10.8 29.6 %collective-permute-start.8 = (bf16[304,512]{1,0:T(8,128)(2,1)S(1)}, bf16[304,512]{1,0:T(8,128)(2,1)S(1)}, u32[]{:S(2)}, u32[]{:S(2)}) collective-permute-start(bf16[304,512]{1,0:T(8,128)(2,1)S(1)} %get-tuple-element.33), channel_id=1, source_target_pairs={{0,3},{1,2},{2,1},{3,0},{4,7},{5,6},{6,5},{7,4},{8,11},{9,10},{10,... | collective-permute-start | bytes 933896 | tf_op jit(solution)/shard_map/ppermute | solution.py:24
  12.6 22.6 %collective-permute-start.4 = (bf16[304,384]{1,0:T(8,128)(2,1)S(1)}, bf16[304,384]{1,0:T(8,128)(2,1)S(1)}, u32[]{:S(2)}, u32[]{:S(2)}) collective-permute-start(bf16[304,384]{1,0:T(8,128)(2,1)S(1)} %get-tuple-element.27), channel_id=1, source_target_pairs={{0,2},{1,3},{2,0},{3,1},{4,6},{5,7},{6,4},{7,5},{8,10},{9,11},{10,... | collective-permute-start | bytes 700424 | tf_op jit(solution)/shard_map/ppermute | solution.py:24
  14.9 21.9 %collective-permute-start.5 = (bf16[304,384]{1,0:T(8,128)(2,1)S(1)}, bf16[304,384]{1,0:T(8,128)(2,1)S(1)}, u32[]{:S(2)}, u32[]{:S(2)}) collective-permute-start(bf16[304,384]{1,0:T(8,128)(2,1)S(1)} %get-tuple-element.28), channel_id=1, source_target_pairs={{0,3},{1,2},{2,1},{3,0},{4,7},{5,6},{6,5},{7,4},{8,11},{9,10},{10,... | collective-permute-start | bytes 700424 | tf_op jit(solution)/shard_map/ppermute | solution.py:24
  35.2 22.1 %collective-permute-start.14 = (bf16[1,24,2048]{2,1,0:T(8,128)(2,1)S(1)}, bf16[1,24,2048]{2,1,0:T(8,128)(2,1)S(1)}, u32[]{:S(2)}, u32[]{:S(2)}) collective-permute-start(bf16[1,24,2048]{2,1,0:T(8,128)(2,1)S(1)} %slice.8), channel_id=1, source_target_pairs={{0,2},{1,3},{2,0},{3,1},{4,6},{5,7},{6,4},{7,5},{8,10},{9,11},{10,... | collective-permute-start | bytes 294920 | tf_op jit(solution)/shard_map/ppermute | solution.py:24
  36.9 20.4 %collective-permute-start.15 = (bf16[1,24,2048]{2,1,0:T(8,128)(2,1)S(1)}, bf16[1,24,2048]{2,1,0:T(8,128)(2,1)S(1)}, u32[]{:S(2)}, u32[]{:S(2)}) collective-permute-start(bf16[1,24,2048]{2,1,0:T(8,128)(2,1)S(1)} %slice.9), channel_id=1, source_target_pairs={{0,1},{1,0},{2,3},{3,2},{4,5},{5,4},{6,7},{7,6},{8,9},{9,8},{10,11... | collective-permute-start | bytes 294920 | tf_op jit(solution)/shard_map/ppermute | solution.py:24
  39.5 16.5 %collective-permute-start = (bf16[304,128]{1,0:T(8,128)(2,1)S(1)}, bf16[304,128]{1,0:T(8,128)(2,1)S(1)}, u32[]{:S(2)}, u32[]{:S(2)}) collective-permute-start(bf16[304,128]{1,0:T(8,128)(2,1)S(1)} %get-tuple-element.21), channel_id=1, source_target_pairs={{0,1},{1,0},{2,3},{3,2},{4,5},{5,4},{6,7},{7,6},{8,9},{9,8},{10,11... | collective-permute-start | bytes 233480 | tf_op jit(solution)/shard_map/ppermute | solution.py:24
  40.1 15.9 %collective-permute-start.1 = (bf16[304,128]{1,0:T(8,128)(2,1)S(1)}, bf16[304,128]{1,0:T(8,128)(2,1)S(1)}, u32[]{:S(2)}, u32[]{:S(2)}) collective-permute-start(bf16[304,128]{1,0:T(8,128)(2,1)S(1)} %get-tuple-element.22), channel_id=1, source_target_pairs={{0,2},{1,3},{2,0},{3,1},{4,6},{5,7},{6,4},{7,5},{8,10},{9,11},{10,... | collective-permute-start | bytes 233480 | tf_op jit(solution)/shard_map/ppermute | solution.py:24
  40.4 15.6 %collective-permute-start.2 = (bf16[304,128]{1,0:T(8,128)(2,1)S(1)}, bf16[304,128]{1,0:T(8,128)(2,1)S(1)}, u32[]{:S(2)}, u32[]{:S(2)}) collective-permute-start(bf16[304,128]{1,0:T(8,128)(2,1)S(1)} %get-tuple-element.23), channel_id=1, source_target_pairs={{0,3},{1,2},{2,1},{3,0},{4,7},{5,6},{6,5},{7,4},{8,11},{9,10},{10,... | collective-permute-start | bytes 233480 | tf_op jit(solution)/shard_map/ppermute | solution.py:24
  52.7 4.5 %copy-start = (bf16[1,24,4096]{2,1,0:T(8,128)(2,1)S(1)}, bf16[1,24,4096]{2,1,0:T(8,128)(2,1)}, u32[]{:S(2)}) copy-start(bf16[1,24,4096]{2,1,0:T(8,128)(2,1)} %refs_4_.3) | copy-start | bytes 589828
  52.7 28.2 %copy-start.1 = (f32[4096]{0:T(1024)S(1)}, f32[4096]{0:T(1024)}, u32[]{:S(2)}) copy-start(f32[4096]{0:T(1024)} %param.9) | copy-start | bytes 49156
  57.8 1.2 %collective-permute-start.16 = (f32[1,4096]{1,0:T(1,128)S(1)}, f32[1,4096]{1,0:T(1,128)S(1)}, u32[]{:S(2)}, u32[]{:S(2)}) collective-permute-start(f32[1,4096]{1,0:T(1,128)S(1)} %gain_terms.1), channel_id=1, source_target_pairs={{0,4},{4,0},{8,12},{12,8},{16,20},{20,16},{24,28},{28,24},{1,5},{5... | collective-permute-start | bytes 49160 | tf_op jit(solution)/shard_map/ppermute | solution.py:24
  59.0 3.8 %collective-permute-start.17 = (f32[1,4096]{1,0:T(1,128)S(1)}, f32[1,4096]{1,0:T(1,128)S(1)}, u32[]{:S(2)}, u32[]{:S(2)}) collective-permute-start(f32[1,4096]{1,0:T(1,128)S(1)} %add.15), channel_id=1, source_target_pairs={{0,8},{4,12},{8,0},{12,4},{16,24},{20,28},{24,16},{28,20},{1,9},{5... | collective-permute-start | bytes 49160 | tf_op jit(solution)/shard_map/ppermute | solution.py:24
  62.9 4.7 %collective-permute-start.18 = (f32[1,4096]{1,0:T(1,128)S(1)}, f32[1,4096]{1,0:T(1,128)S(1)}, u32[]{:S(2)}, u32[]{:S(2)}) collective-permute-start(f32[1,4096]{1,0:T(1,128)S(1)} %add.16), channel_id=1, source_target_pairs={{0,16},{4,20},{8,24},{12,28},{16,0},{20,4},{24,8},{28,12},{1,17},{... | collective-permute-start | bytes 49160 | tf_op jit(solution)/shard_map/ppermute | solution.py:24
  67.6 4.0 %collective-permute-start.19 = (f32[1,4096]{1,0:T(1,128)S(1)}, f32[1,4096]{1,0:T(1,128)S(1)}, u32[]{:S(2)}, u32[]{:S(2)}) collective-permute-start(f32[1,4096]{1,0:T(1,128)S(1)} %add.17), channel_id=1, source_target_pairs={{0,1},{1,0},{2,3},{3,2},{4,5},{5,4},{6,7},{7,6},{8,9},{9,8},{10,11... | collective-permute-start | bytes 49160 | tf_op jit(solution)/shard_map/ppermute | solution.py:24
  71.6 4.8 %collective-permute-start.20 = (f32[1,4096]{1,0:T(1,128)S(1)}, f32[1,4096]{1,0:T(1,128)S(1)}, u32[]{:S(2)}, u32[]{:S(2)}) collective-permute-start(f32[1,4096]{1,0:T(1,128)S(1)} %add.18), channel_id=1, source_target_pairs={{0,2},{1,3},{2,0},{3,1},{4,6},{5,7},{6,4},{7,5},{8,10},{9,11},{10,... | collective-permute-start | bytes 49160 | tf_op jit(solution)/shard_map/ppermute | solution.py:24
  72.0 5.7 %collective-permute-start.9 = (bf16[24,4096]{1,0:T(8,128)(2,1)S(1)}, bf16[24,4096]{1,0:T(8,128)(2,1)S(1)}, u32[]{:S(2)}, u32[]{:S(2)}) collective-permute-start(bf16[24,4096]{1,0:T(8,128)(2,1)S(1)} %get-tuple-element.35.refs_1_), channel_id=1, source_target_pairs={{0,1},{1,0},{2,3},{3,2},{4,5},{5,4},{6,7},{7,6},{8,9},{9,8},{10,11... | collective-permute-start | bytes 589832 | tf_op jit(solution)/shard_map/ppermute | solution.py:24
  72.3 7.2 %collective-permute-start.10 = (bf16[24,4096]{1,0:T(8,128)(2,1)S(1)}, bf16[24,4096]{1,0:T(8,128)(2,1)S(1)}, u32[]{:S(2)}, u32[]{:S(2)}) collective-permute-start(bf16[24,4096]{1,0:T(8,128)(2,1)S(1)} %get-tuple-element.36.refs_2_), channel_id=1, source_target_pairs={{0,2},{1,3},{2,0},{3,1},{4,6},{5,7},{6,4},{7,5},{8,10},{9,11},{10,... | collective-permute-start | bytes 589832 | tf_op jit(solution)/shard_map/ppermute | solution.py:24
  74.2 6.7 %collective-permute-start.11 = (bf16[24,4096]{1,0:T(8,128)(2,1)S(1)}, bf16[24,4096]{1,0:T(8,128)(2,1)S(1)}, u32[]{:S(2)}, u32[]{:S(2)}) collective-permute-start(bf16[24,4096]{1,0:T(8,128)(2,1)S(1)} %get-tuple-element.37.refs_3_), channel_id=1, source_target_pairs={{0,3},{1,2},{2,1},{3,0},{4,7},{5,6},{6,5},{7,4},{8,11},{9,10},{10,... | collective-permute-start | bytes 589832 | tf_op jit(solution)/shard_map/ppermute | solution.py:24

commit v4 on v3

--- a/solution.py
+++ b/solution.py
@@ -9,9 +9,10 @@
 HEAD_DIM = 64
 LANES = 128
 PROJ_BLOCK = 1024
+TAIL_PAIRS = (2, 1)
 ATTN_ROWS = 512
 PACK_VMEM = 8 << 20
-LAYER_VMEM = 24 << 20
+LAYER_VMEM = 20 << 20
 F32 = jnp.float32
 BF16 = jnp.bfloat16
 
@@ -25,10 +26,25 @@
 
 
 def plan_chunks(layers, cols):
-    chunks = [(layer, 0, cols) for layer in range(layers)]
-    if cols > LANES:
-        chunks[-1:] = [(layers - 1, 0, cols - LANES), (layers - 1, cols - LANES, LANES)]
+    pairs = [(layer, first) for layer in range(layers) for first in range(0, cols, LANES)]
+    tail = [n for n in TAIL_PAIRS if len(pairs) >= 2 * sum(TAIL_PAIRS)] or [1]
+    cuts = [0, len(pairs) - sum(tail)]
+    for n in tail:
+        cuts.append(cuts[-1] + n)
+    chunks = []
+    for low, high in zip(cuts[:-1], cuts[1:]):
+        chunk = []
+        for layer, first in pairs[low:high]:
+            if chunk and chunk[-1][0] == layer:
+                chunk[-1] = (layer, chunk[-1][1], chunk[-1][2] + LANES)
+            else:
+                chunk.append((layer, first, LANES))
+        chunks.append(chunk)
     return chunks
+
+
+def chunk_width(chunk):
+    return sum(width for _, _, width in chunk)
 
 
 def in_hbm(arrays):
@@ -36,7 +52,7 @@
 
 
 def pack_chunk(chunk, arrays, seq_size):
-    layer, first, width = chunk
+    width = chunk_width(chunk)
     rows = [a.shape[2] for a in arrays]
     cols = arrays[0].shape[3] // seq_size
 
@@ -45,17 +61,20 @@
         me = lax.axis_index("seq")
         copies = []
         for j in list(range(1, seq_size)) + [0]:
-            start = pl.multiple_of((me ^ j) * cols + first, LANES)
-            base = 0
-            for i, ref in enumerate((q_ref, g_ref, k_ref, v_ref)):
-                copies.append(
-                    pltpu.make_async_copy(
-                        ref.at[layer, 0, :, pl.ds(start, width)],
-                        outs[j].at[pl.ds(base, rows[i]), :],
-                        sems.at[j, i],
+            left = 0
+            for n, (layer, first, part) in enumerate(chunk):
+                start = pl.multiple_of((me ^ j) * cols + first, LANES)
+                base = 0
+                for i, ref in enumerate((q_ref, g_ref, k_ref, v_ref)):
+                    copies.append(
+                        pltpu.make_async_copy(
+                            ref.at[layer, 0, :, pl.ds(start, part)],
+                            outs[j].at[pl.ds(base, rows[i]), pl.ds(left, part)],
+                            sems.at[j, n, i],
+                        )
                     )
-                )
-                base += rows[i]
+                    base += rows[i]
+                left += part
         for c in copies:
             c.start()
         for c in copies:
@@ -66,7 +85,7 @@
         out_shape=[jax.ShapeDtypeStruct((sum(rows), width), BF16)] * seq_size,
         in_specs=[pl.BlockSpec(memory_space=pltpu.HBM)] * 4,
         out_specs=[pl.BlockSpec(memory_space=pltpu.VMEM)] * seq_size,
-        scratch_shapes=[pltpu.SemaphoreType.DMA((seq_size, 4))],
+        scratch_shapes=[pltpu.SemaphoreType.DMA((seq_size, len(chunk), 4))],
         compiler_params=pltpu.CompilerParams(vmem_limit_bytes=PACK_VMEM),
     )(*in_hbm(arrays))
 
@@ -118,20 +137,18 @@
 
 
 def weight_copies(chunk, key_weight, value_weight, dest, sems):
-    layer, first, cols = chunk
     copies = []
-    for b in range(dest.shape[0] // PROJ_BLOCK):
-        rows = pl.ds(b * PROJ_BLOCK, PROJ_BLOCK)
-        copies.append(
-            [
+    left = 0
+    for n, (layer, first, part) in enumerate(chunk):
+        for i, src in enumerate((key_weight, value_weight)):
+            copies.append(
                 pltpu.make_async_copy(
-                    src.at[layer, rows, pl.ds(first, cols)],
-                    dest.at[rows, pl.ds(i * cols, cols)],
-                    sems.at[b, i],
+                    src.at[layer, :, pl.ds(first, part)],
+                    dest.at[:, pl.ds(i * chunk_width(chunk) + left, part)],
+                    sems.at[n, i],
                 )
-                for i, src in enumerate((key_weight, value_weight))
-            ]
-        )
+            )
+        left += part
     return copies
 
 
@@ -142,7 +159,7 @@
         outs, sems = rest[: len(chunks)], rest[len(chunks) :]
         copies = []
         for chunk, out, sem in zip(chunks, outs, sems):
-            copies += sum(weight_copies(chunk, kw, vw, out, sem), [])
+            copies += weight_copies(chunk, kw, vw, out, sem)
         for c in copies:
             c.start()
         for c in copies:
@@ -150,46 +167,28 @@
 
     return pl.pallas_call(
         kernel,
-        out_shape=[jax.ShapeDtypeStruct((width, 2 * cols), BF16) for _, _, cols in chunks],
+        out_shape=[jax.ShapeDtypeStruct((width, 2 * chunk_width(c)), BF16) for c in chunks],
         in_specs=[pl.BlockSpec(memory_space=pltpu.HBM)] * 2 + [pl.BlockSpec(memory_space=pl.ANY)],
         out_specs=[pl.BlockSpec(memory_space=pltpu.VMEM)] * len(chunks),
-        scratch_shapes=[pltpu.SemaphoreType.DMA((width // PROJ_BLOCK, 2)) for _ in chunks],
+        scratch_shapes=[pltpu.SemaphoreType.DMA((len(c), 2)) for c in chunks],
         compiler_params=pltpu.CompilerParams(vmem_limit_bytes=PACK_VMEM),
         name="load_weights",
     )(*in_hbm([key_weight, value_weight]), after)
 
 
-def chunk_terms(index, chunks, bufs, key_weight, value_weight, ready, prior, dec, enc):
+def chunk_terms(bufs, weight, prior, dec, enc, last):
     count = len(bufs)
-    width = key_weight.shape[1]
+    width = weight.shape[0]
     rows = enc * count
-    nblocks = width // PROJ_BLOCK
-    cols = chunks[index][2]
-    last = index == len(chunks) - 1
 
     def kernel(*refs):
-        refs = list(refs)
-        buf_refs = [refs.pop(0) for _ in range(count)]
-        if ready is None:
-            kw, vw = refs.pop(0), refs.pop(0)
-        else:
-            w_ref = refs.pop(0)
-        prior_ref = None if prior is None else refs.pop(0)
-        outs = [refs.pop(0) for _ in range(count if last else 1)]
-        kv_ref = refs.pop(0)
-        if ready is None:
-            w_ref, sems = refs.pop(0), refs.pop(0)
-            copies = weight_copies(chunks[index], kw, vw, w_ref, sems)
-            for pair in copies:
-                for c in pair:
-                    c.start()
+        buf_refs, w_ref, kv_ref = refs[:count], refs[count], refs[-1]
+        prior_ref = None if prior is None else refs[count + 1]
+        outs = refs[count + 1 + (prior is not None) : -1]
         attention_into(buf_refs, dec, enc, kv_ref)
         nt = (((1,), (1,)), ((), ()))
-        for b in range(nblocks):
+        for b in range(width // PROJ_BLOCK):
             bs = slice(b * PROJ_BLOCK, (b + 1) * PROJ_BLOCK)
-            if ready is None:
-                for c in copies[b]:
-                    c.wait()
             acc = lax.dot_general(kv_ref[...], w_ref[bs, :], nt, preferred_element_type=F32)
             if prior is not None:
                 acc += prior_ref[:, bs]
@@ -203,37 +202,30 @@
         out_shape = [jax.ShapeDtypeStruct((enc, width), F32 if j == 0 else BF16) for j in range(count)]
     else:
         out_shape = [jax.ShapeDtypeStruct((rows, width), F32)]
-    scratch = [pltpu.VMEM((rows, 2 * cols), BF16)]
-    if ready is None:
-        scratch += [pltpu.VMEM((width, 2 * cols), BF16), pltpu.SemaphoreType.DMA((nblocks, 2))]
     vmem = pl.BlockSpec(memory_space=pltpu.VMEM)
-    if ready is None:
-        weights, specs = in_hbm([key_weight, value_weight]), [pl.BlockSpec(memory_space=pltpu.HBM)] * 2
-    else:
-        weights, specs = [ready], [vmem]
-    tail = [] if prior is None else [prior]
+    operands = list(bufs) + [weight] + ([] if prior is None else [prior])
     return pl.pallas_call(
         kernel,
         out_shape=out_shape,
-        in_specs=[vmem] * count + specs + [vmem] * len(tail),
+        in_specs=[vmem] * len(operands),
         out_specs=[vmem] * len(out_shape),
-        scratch_shapes=scratch,
+        scratch_shapes=[pltpu.VMEM((rows, weight.shape[1]), BF16)],
         compiler_params=pltpu.CompilerParams(vmem_limit_bytes=LAYER_VMEM),
-    )(*bufs, *weights, *tail)
+    )(*operands)
 
 
 def gather_rows(enc_final, seq_size):
     enc, width = enc_final.shape[1], enc_final.shape[2]
     rows = {0: [(enc_final, 0, 0, width)]}
     if seq_size == 4:
-        half = width // 2
+        half = width // 2 // LANES * LANES
         near = {j: exchange(enc_final, "seq", seq_size, j) for j in (1, 2)}
         for j in (1, 2):
             rows[j] = [(near[j], 0, 0, width)]
         sends = [near[1][:, :, :half], near[2][:, :, half:]]
         low = exchange(sends[0], "seq", seq_size, 2)
         high = exchange(sends[1], "seq", seq_size, 1)
-        rows[3] = [(low, 0, 0, half), (high, 0, half, half)]
+        rows[3] = [(low, 0, 0, half), (high, 0, half, width - half)]
         return rows
     have, order = [enc_final], [0]
     step = 1
@@ -331,12 +323,11 @@
         for j in range(1, seq):
             moved.append(exchange(bufs[j], "seq", seq, j))
         gathered.append(moved)
-    ready = load_weights(chunks[1:], key_weight, value_weight, gathered[-1][0])
+    weights = load_weights(chunks, key_weight, value_weight, gathered[-1][0])
     prior = None
     for index in range(len(chunks)):
         outs = chunk_terms(
-            index, chunks, gathered[index], key_weight, value_weight,
-            ready[index - 1] if index else None, prior, dec, enc,
+            gathered[index], weights[index], prior, dec, enc, index == len(chunks) - 1
         )
         prior = outs[0]
     received = [exchange(outs[j], "seq", seq, j) for j in range(1, seq)]
@@ -365,7 +356,9 @@
     )
 
     def whole(*args):
-        step = jax.shard_map(body, mesh=mesh, in_specs=placed, out_specs=(P("dp", "seq", None), P()), check_vma=False)
+        step = jax.shard_map(
+            body, mesh=mesh, in_specs=placed, out_specs=(P("dp", "seq", None), P()), check_vma=False
+        )
         return step(*args)
 
     return whole

time: 82.2 us -> 86.3 us (1.050)
  waiting for transfers between devices: 31.1 us -> 36.7 us
  starting transfers between devices: 29.6 us -> 27.7 us
    ppermute x21, waiting for transfers between devices: 31.1 us -> 36.7 us  [exchange(): return lax.ppermute(value, axis, xor_pairs(size, step))]
    ppermute x21, starting transfers between devices: 29.6 us -> 27.7 us  [exchange(): return lax.ppermute(value, axis, xor_pairs(size, step))]
  transfers between devices with their start and end apart: 21 -> 21, of which waited for: 9 -> 9; matrix products, arithmetic and copies ran while one was open for 1% -> 1% of each run, Pallas kernels for 22% -> 20%
where the time goes in v4:
time: 86.3 us; the launch traced here: 86.1 us
  waiting for transfers between devices  36.7 us (43%)
  starting transfers between devices  27.7 us (32%)
  Pallas kernels  20.2 us (23%)
    ppermute x21, waiting for transfers between devices, exchange(): return lax.ppermute(value, axis, xor_pairs(size, step))  36.7 us
    ppermute x21, starting transfers between devices, exchange(): return lax.ppermute(value, axis, xor_pairs(size, step))  27.7 us
    pallas_call x3, Pallas kernels, chunk_terms(): pl.pallas_call(kernel, out_shape=out_shape, in_specs=[vmem] * len(operand...  8.61 us
    pallas_call x1, Pallas kernels, load_weights(): pl.pallas_call(kernel, out_shape=[jax.ShapeDtypeStruct((width, 2 * chunk_...  5.89 us
    pallas_call x3, Pallas kernels, pack_chunk(): pl.pallas_call(kernel, out_shape=[jax.ShapeDtypeStruct((sum(rows), width)...  4.19 us
  transfers between devices with their start and end apart: 21, of which 9 were waited for; matrix products, arithmetic and copies ran while one was open for 1% of the time, Pallas kernels for 20%

profile of v4, /device:TPU:0, one launch (start us, length us, event | category | flops | bytes accessed | tf_op | source)
XLA Modules:
  0.0 86.1 jit_solution(14267172694980470786)
XLA Ops:
  0.6 1.3 %shard_map.96 = (bf16[304,256]{1,0:T(8,128)(2,1)S(1)}, bf16[304,256]{1,0:T(8,128)(2,1)S(1)}, bf16[304,256]{1,0:T(8,128)(2,1)S(1)}, bf16[304,256]{1,0:T(8,128)(2,1)S(1)}) custom-call(bf16[2,1,128,2048]{3,2,1,0:T(8,128)(2,1)} %q_ref.5, bf16[2,1,128,2048]{3,2,1,0:T(8,128)(2,1)} %g_ref.5, bf16[2,1,24,2048]{3,2,1,0:T(8,128)(2,1)} %k_ref.5, ...), custom_call_target="tpu_custom_call" | custom-call | tf_op jit(solution)/shard_map/pallas_call | solution.py:83
  2.0 3.0 %collective-permute-start.3 = (bf16[304,256]{1,0:T(8,128)(2,1)S(1)}, bf16[304,256]{1,0:T(8,128)(2,1)S(1)}, u32[]{:S(2)}, u32[]{:S(2)}) collective-permute-start(bf16[304,256]{1,0:T(8,128)(2,1)S(1)} %get-tuple-element.27), channel_id=1, source_target_pairs={{0,1},{1,0},{2,3},{3,2},{4,5},{5,4},{6,7},{7,6},{8,9},{9,8},{10,11... | collective-permute-start | bytes 466952 | tf_op jit(solution)/shard_map/ppermute | solution.py:25
  5.0 1.8 %shard_map.97 = (bf16[304,640]{1,0:T(8,128)(2,1)S(1)}, bf16[304,640]{1,0:T(8,128)(2,1)S(1)}, bf16[304,640]{1,0:T(8,128)(2,1)S(1)}, bf16[304,640]{1,0:T(8,128)(2,1)S(1)}) custom-call(bf16[2,1,128,2048]{3,2,1,0:T(8,128)(2,1)} %q_ref.5, bf16[2,1,128,2048]{3,2,1,0:T(8,128)(2,1)} %g_ref.5, bf16[2,1,24,2048]{3,2,1,0:T(8,128)(2,1)} %k_ref.5, ...), custom_call_target="tpu_custom_call" | custom-call | tf_op jit(solution)/shard_map/pallas_call | solution.py:83
  6.8 0.1 collective-permute-start.6
  6.9 2.0 %collective-permute-start.7 = (bf16[304,640]{1,0:T(8,128)(2,1)S(1)}, bf16[304,640]{1,0:T(8,128)(2,1)S(1)}, u32[]{:S(2)}, u32[]{:S(2)}) collective-permute-start(bf16[304,640]{1,0:T(8,128)(2,1)S(1)} %get-tuple-element.33), channel_id=1, source_target_pairs={{0,2},{1,3},{2,0},{3,1},{4,6},{5,7},{6,4},{7,5},{8,10},{9,11},{10,... | collective-permute-start | bytes 1167368 | tf_op jit(solution)/shard_map/ppermute | solution.py:25
  8.9 1.4 %collective-permute-start.8 = (bf16[304,640]{1,0:T(8,128)(2,1)S(1)}, bf16[304,640]{1,0:T(8,128)(2,1)S(1)}, u32[]{:S(2)}, u32[]{:S(2)}) collective-permute-start(bf16[304,640]{1,0:T(8,128)(2,1)S(1)} %get-tuple-element.34), channel_id=1, source_target_pairs={{0,3},{1,2},{2,1},{3,0},{4,7},{5,6},{6,5},{7,4},{8,11},{9,10},{10,... | collective-permute-start | bytes 1167368 | tf_op jit(solution)/shard_map/ppermute | solution.py:25
  10.3 0.1 collective-permute-start.12
  10.4 2.0 %collective-permute-start.13 = (bf16[1,24,4096]{2,1,0:T(8,128)(2,1)S(1)}, bf16[1,24,4096]{2,1,0:T(8,128)(2,1)S(1)}, u32[]{:S(2)}, u32[]{:S(2)}) collective-permute-start(bf16[1,24,4096]{2,1,0:T(8,128)(2,1)S(1)} %copy-done), channel_id=1, source_target_pairs={{0,2},{1,3},{2,0},{3,1},{4,6},{5,7},{6,4},{7,5},{8,10},{9,11},{10,... | collective-permute-start | bytes 589832 | tf_op jit(solution)/shard_map/ppermute | solution.py:25
  12.4 17.6 %collective-permute-done.12.refs_5_ = bf16[1,24,4096]{2,1,0:T(8,128)(2,1)S(1)} collective-permute-done((bf16[1,24,4096]{2,1,0:T(8,128)(2,1)S(1)}, bf16[1,24,4096]{2,1,0:T(8,128)(2,1)S(1)}, u32[]{:S(2)}, u32[]{:S(2)}) %collective-permute-start.12) | collective-permute-done | bytes 196640 | tf_op jit(solution)/shard_map/ppermute | solution.py:25
  30.0 1.8 %collective-permute-start.4 = (bf16[304,256]{1,0:T(8,128)(2,1)S(1)}, bf16[304,256]{1,0:T(8,128)(2,1)S(1)}, u32[]{:S(2)}, u32[]{:S(2)}) collective-permute-start(bf16[304,256]{1,0:T(8,128)(2,1)S(1)} %get-tuple-element.28), channel_id=1, source_target_pairs={{0,2},{1,3},{2,0},{3,1},{4,6},{5,7},{6,4},{7,5},{8,10},{9,11},{10,... | collective-permute-start | bytes 466952 | tf_op jit(solution)/shard_map/ppermute | solution.py:25
  31.7 0.0 collective-permute-done.13.refs_6_
  31.7 1.4 %collective-permute-start.5 = (bf16[304,256]{1,0:T(8,128)(2,1)S(1)}, bf16[304,256]{1,0:T(8,128)(2,1)S(1)}, u32[]{:S(2)}, u32[]{:S(2)}) collective-permute-start(bf16[304,256]{1,0:T(8,128)(2,1)S(1)} %get-tuple-element.29), channel_id=1, source_target_pairs={{0,3},{1,2},{2,1},{3,0},{4,7},{5,6},{6,5},{7,4},{8,11},{9,10},{10,... | collective-permute-start | bytes 466952 | tf_op jit(solution)/shard_map/ppermute | solution.py:25
  33.2 5.3 %collective-permute-done.4.refs_2_ = bf16[304,256]{1,0:T(8,128)(2,1)S(1)} collective-permute-done((bf16[304,256]{1,0:T(8,128)(2,1)S(1)}, bf16[304,256]{1,0:T(8,128)(2,1)S(1)}, u32[]{:S(2)}, u32[]{:S(2)}) %collective-permute-start.4) | collective-permute-done | bytes 155680 | tf_op jit(solution)/shard_map/ppermute | solution.py:25
  38.5 1.4 %collective-permute-start.14 = (bf16[1,24,2048]{2,1,0:T(8,128)(2,1)S(1)}, bf16[1,24,2048]{2,1,0:T(8,128)(2,1)S(1)}, u32[]{:S(2)}, u32[]{:S(2)}) collective-permute-start(bf16[1,24,2048]{2,1,0:T(8,128)(2,1)S(1)} %slice.8), channel_id=1, source_target_pairs={{0,2},{1,3},{2,0},{3,1},{4,6},{5,7},{6,4},{7,5},{8,10},{9,11},{10,... | collective-permute-start | bytes 294920 | tf_op jit(solution)/shard_map/ppermute | solution.py:25
  40.0 1.5 %collective-permute-start.15 = (bf16[1,24,2048]{2,1,0:T(8,128)(2,1)S(1)}, bf16[1,24,2048]{2,1,0:T(8,128)(2,1)S(1)}, u32[]{:S(2)}, u32[]{:S(2)}) collective-permute-start(bf16[1,24,2048]{2,1,0:T(8,128)(2,1)S(1)} %slice.9), channel_id=1, source_target_pairs={{0,1},{1,0},{2,3},{3,2},{4,5},{5,4},{6,7},{7,6},{8,9},{9,8},{10,11... | collective-permute-start | bytes 294920 | tf_op jit(solution)/shard_map/ppermute | solution.py:25
  41.5 1.1 %shard_map.95 = (bf16[304,128]{1,0:T(8,128)(2,1)S(1)}, bf16[304,128]{1,0:T(8,128)(2,1)S(1)}, bf16[304,128]{1,0:T(8,128)(2,1)S(1)}, bf16[304,128]{1,0:T(8,128)(2,1)S(1)}) custom-call(bf16[2,1,128,2048]{3,2,1,0:T(8,128)(2,1)} %q_ref.5, bf16[2,1,128,2048]{3,2,1,0:T(8,128)(2,1)} %g_ref.5, bf16[2,1,24,2048]{3,2,1,0:T(8,128)(2,1)} %k_ref.5, ...), custom_call_target="tpu_custom_call" | custom-call | tf_op jit(solution)/shard_map/pallas_call | solution.py:83
  42.6 0.0 collective-permute-done.6.refs_1_
  42.6 0.6 collective-permute-start
  43.2 0.0 collective-permute-done.7.refs_2_
  43.2 0.6 collective-permute-start.1
  43.8 0.0 collective-permute-done.8.refs_3_
  43.8 2.4 %collective-permute-start.2 = (bf16[304,128]{1,0:T(8,128)(2,1)S(1)}, bf16[304,128]{1,0:T(8,128)(2,1)S(1)}, u32[]{:S(2)}, u32[]{:S(2)}) collective-permute-start(bf16[304,128]{1,0:T(8,128)(2,1)S(1)} %get-tuple-element.24), channel_id=1, source_target_pairs={{0,3},{1,2},{2,1},{3,0},{4,7},{5,6},{6,5},{7,4},{8,11},{9,10},{10,... | collective-permute-start | bytes 233480 | tf_op jit(solution)/shard_map/ppermute | solution.py:25
  46.1 5.9 %load_weights.1 = (bf16[4096,1280]{1,0:T(8,128)(2,1)S(1)}, bf16[4096,512]{1,0:T(8,128)(2,1)S(1)}, bf16[4096,256]{1,0:T(8,128)(2,1)S(1)}) custom-call(bf16[2,4096,512]{2,1,0:T(8,128)(2,1)} %kw.1, bf16[2,4096,512]{2,1,0:T(8,128)(2,1)} %vw.1, bf16[304,128]{1,0:T(8,128)(2,1)S(1)} %get-tuple-element.21.after_ref.refs_0_), custom_call_target="tpu_custom_call" | custom-call | tf_op jit(solution)/shard_map/load_weights/pallas_call | solution.py:168
  52.0 5.1 %shard_map.98.refs_5_ = f32[96,4096]{1,0:T(8,128)S(1)} custom-call(bf16[304,640]{1,0:T(8,128)(2,1)S(1)} %get-tuple-element.31.refs_0_, bf16[304,640]{1,0:T(8,128)(2,1)S(1)} %collective-permute-done.6.refs_1_, bf16[304,640]{1,0:T(8,128)(2,1)S(1)} %collective-permute-done.7.refs_2_, bf16[304,640]{1,0:T(8,128)(2,1)S(1)} %collective-permute-done.8.refs_3_, ...), custom_call_target="tpu_custom_call" | custom-call | tf_op jit(solution)/shard_map/pallas_call | solution.py:207
  57.2 2.2 %shard_map.99.refs_5_ = f32[96,4096]{1,0:T(8,128)S(1)} custom-call(bf16[304,256]{1,0:T(8,128)(2,1)S(1)} %get-tuple-element.26.refs_0_, bf16[304,256]{1,0:T(8,128)(2,1)S(1)} %collective-permute-done.3.refs_1_, bf16[304,256]{1,0:T(8,128)(2,1)S(1)} %collective-permute-done.4.refs_2_, bf16[304,256]{1,0:T(8,128)(2,1)S(1)} %collective-permute-done.5.refs_3_, ...), custom_call_target="tpu_custom_call" | custom-call | tf_op jit(solution)/shard_map/pallas_call | solution.py:207
  59.4 0.0 copy-start.1
  59.4 0.0 collective-permute-done.refs_1_
  59.4 0.0 collective-permute-done.2.refs_3_
  59.4 1.2 %shard_map.100 = (f32[24,4096]{1,0:T(8,128)S(1)}, bf16[24,4096]{1,0:T(8,128)(2,1)S(1)}, bf16[24,4096]{1,0:T(8,128)(2,1)S(1)}, bf16[24,4096]{1,0:T(8,128)(2,1)S(1)}) custom-call(bf16[304,128]{1,0:T(8,128)(2,1)S(1)} %get-tuple-element.21.after_ref.refs_0_, bf16[304,128]{1,0:T(8,128)(2,1)S(1)} %collective-permute-done.refs_1_, ...), custom_call_target="tpu_custom_call" | custom-call | tf_op jit(solution)/shard_map/pallas_call | solution.py:207
  60.7 0.0 collective-permute-done.14.refs_7_
  60.7 0.5 gain_terms.1
  61.2 0.1 collective-permute-start.16
  61.3 1.2 %collective-permute-done.16 = f32[1,4096]{1,0:T(1,128)S(1)} collective-permute-done((f32[1,4096]{1,0:T(1,128)S(1)}, f32[1,4096]{1,0:T(1,128)S(1)}, u32[]{:S(2)}, u32[]{:S(2)}) %collective-permute-start.16) | collective-permute-done | bytes 16416 | tf_op jit(solution)/shard_map/ppermute | solution.py:25
  62.5 1.7 %collective-permute-start.17 = (f32[1,4096]{1,0:T(1,128)S(1)}, f32[1,4096]{1,0:T(1,128)S(1)}, u32[]{:S(2)}, u32[]{:S(2)}) collective-permute-start(f32[1,4096]{1,0:T(1,128)S(1)} %add.15), channel_id=1, source_target_pairs={{0,8},{4,12},{8,0},{12,4},{16,24},{20,28},{24,16},{28,20},{1,9},{5... | collective-permute-start | bytes 49160 | tf_op jit(solution)/shard_map/ppermute | solution.py:25
  64.1 2.2 %collective-permute-done.17 = f32[1,4096]{1,0:T(1,128)S(1)} collective-permute-done((f32[1,4096]{1,0:T(1,128)S(1)}, f32[1,4096]{1,0:T(1,128)S(1)}, u32[]{:S(2)}, u32[]{:S(2)}) %collective-permute-start.17) | collective-permute-done | bytes 16416 | tf_op jit(solution)/shard_map/ppermute | solution.py:25
  66.3 2.7 %collective-permute-start.18 = (f32[1,4096]{1,0:T(1,128)S(1)}, f32[1,4096]{1,0:T(1,128)S(1)}, u32[]{:S(2)}, u32[]{:S(2)}) collective-permute-start(f32[1,4096]{1,0:T(1,128)S(1)} %add.16), channel_id=1, source_target_pairs={{0,16},{4,20},{8,24},{12,28},{16,0},{20,4},{24,8},{28,12},{1,17},{... | collective-permute-start | bytes 49160 | tf_op jit(solution)/shard_map/ppermute | solution.py:25
  69.0 2.0 %collective-permute-done.18 = f32[1,4096]{1,0:T(1,128)S(1)} collective-permute-done((f32[1,4096]{1,0:T(1,128)S(1)}, f32[1,4096]{1,0:T(1,128)S(1)}, u32[]{:S(2)}, u32[]{:S(2)}) %collective-permute-start.18) | collective-permute-done | bytes 16416 | tf_op jit(solution)/shard_map/ppermute | solution.py:25
  71.0 0.6 collective-permute-start.19
  71.6 3.2 %collective-permute-done.19 = f32[1,4096]{1,0:T(1,128)S(1)} collective-permute-done((f32[1,4096]{1,0:T(1,128)S(1)}, f32[1,4096]{1,0:T(1,128)S(1)}, u32[]{:S(2)}, u32[]{:S(2)}) %collective-permute-start.19) | collective-permute-done | bytes 16416 | tf_op jit(solution)/shard_map/ppermute | solution.py:25
  74.9 0.9 %collective-permute-start.20 = (f32[1,4096]{1,0:T(1,128)S(1)}, f32[1,4096]{1,0:T(1,128)S(1)}, u32[]{:S(2)}, u32[]{:S(2)}) collective-permute-start(f32[1,4096]{1,0:T(1,128)S(1)} %add.18), channel_id=1, source_target_pairs={{0,2},{1,3},{2,0},{3,1},{4,6},{5,7},{6,4},{7,5},{8,10},{9,11},{10,... | collective-permute-start | bytes 49160 | tf_op jit(solution)/shard_map/ppermute | solution.py:25
  75.8 1.2 %collective-permute-start.10 = (bf16[24,4096]{1,0:T(8,128)(2,1)S(1)}, bf16[24,4096]{1,0:T(8,128)(2,1)S(1)}, u32[]{:S(2)}, u32[]{:S(2)}) collective-permute-start(bf16[24,4096]{1,0:T(8,128)(2,1)S(1)} %get-tuple-element.38.refs_2_), channel_id=1, source_target_pairs={{0,2},{1,3},{2,0},{3,1},{4,6},{5,7},{6,4},{7,5},{8,10},{9,11},{10,... | collective-permute-start | bytes 589832 | tf_op jit(solution)/shard_map/ppermute | solution.py:25
  77.0 0.6 collective-permute-start.11
  77.5 1.7 %collective-permute-start.9 = (bf16[24,4096]{1,0:T(8,128)(2,1)S(1)}, bf16[24,4096]{1,0:T(8,128)(2,1)S(1)}, u32[]{:S(2)}, u32[]{:S(2)}) collective-permute-start(bf16[24,4096]{1,0:T(8,128)(2,1)S(1)} %get-tuple-element.37.refs_1_), channel_id=1, source_target_pairs={{0,1},{1,0},{2,3},{3,2},{4,5},{5,4},{6,7},{7,6},{8,9},{9,8},{10,11... | collective-permute-start | bytes 589832 | tf_op jit(solution)/shard_map/ppermute | solution.py:25
  79.3 0.6 add_multiply_fusion
  79.9 2.4 %collective-permute-done.10.refs_1_ = bf16[24,4096]{1,0:T(8,128)(2,1)S(1)} collective-permute-done((bf16[24,4096]{1,0:T(8,128)(2,1)S(1)}, bf16[24,4096]{1,0:T(8,128)(2,1)S(1)}, u32[]{:S(2)}, u32[]{:S(2)}) %collective-permute-start.10) | collective-permute-done | bytes 196640 | tf_op jit(solution)/shard_map/ppermute | solution.py:25
  82.3 1.3 %collective-permute-done.11.refs_2_ = bf16[24,4096]{1,0:T(8,128)(2,1)S(1)} collective-permute-done((bf16[24,4096]{1,0:T(8,128)(2,1)S(1)}, bf16[24,4096]{1,0:T(8,128)(2,1)S(1)}, u32[]{:S(2)}, u32[]{:S(2)}) %collective-permute-start.11) | collective-permute-done | bytes 196640 | tf_op jit(solution)/shard_map/ppermute | solution.py:25
  83.5 1.5 %collective-permute-done.9.refs_0_ = bf16[24,4096]{1,0:T(8,128)(2,1)S(1)} collective-permute-done((bf16[24,4096]{1,0:T(8,128)(2,1)S(1)}, bf16[24,4096]{1,0:T(8,128)(2,1)S(1)}, u32[]{:S(2)}, u32[]{:S(2)}) %collective-permute-start.9) | collective-permute-done | bytes 196640 | tf_op jit(solution)/shard_map/ppermute | solution.py:25
  85.1 1.0 %finish.1 = bf16[1,24,4096]{2,1,0:T(8,128)(2,1)} custom-call(f32[24,4096]{1,0:T(8,128)S(1)} %get-tuple-element.36.own_ref.refs_0_, bf16[24,4096]{1,0:T(8,128)(2,1)S(1)} %collective-permute-done.9.refs_0_, bf16[24,4096]{1,0:T(8,128)(2,1)S(1)} %collective-permute-done.10.refs_1_, bf16[24,4096]{1,0:T(8,128)(2,1)S(1)} %collective-permute-done.11.refs_2_, ...), custom_call_target="tpu_custom_call" | custom-call | tf_op jit(solution)/shard_map/finish/pallas_call | solution.py:301
  (14 shorter events, 0.1 us)
Async XLA Ops:
  0.6 9.7 %copy-start = (bf16[1,24,4096]{2,1,0:T(8,128)(2,1)S(1)}, bf16[1,24,4096]{2,1,0:T(8,128)(2,1)}, u32[]{:S(2)}) copy-start(bf16[1,24,4096]{2,1,0:T(8,128)(2,1)} %refs_4_.1) | copy-start | bytes 589828
  2.0 8.5 %collective-permute-start.3 = (bf16[304,256]{1,0:T(8,128)(2,1)S(1)}, bf16[304,256]{1,0:T(8,128)(2,1)S(1)}, u32[]{:S(2)}, u32[]{:S(2)}) collective-permute-start(bf16[304,256]{1,0:T(8,128)(2,1)S(1)} %get-tuple-element.27), channel_id=1, source_target_pairs={{0,1},{1,0},{2,3},{3,2},{4,5},{5,4},{6,7},{7,6},{8,9},{9,8},{10,11... | collective-permute-start | bytes 466952 | tf_op jit(solution)/shard_map/ppermute | solution.py:25
  6.8 35.8 %collective-permute-start.6 = (bf16[304,640]{1,0:T(8,128)(2,1)S(1)}, bf16[304,640]{1,0:T(8,128)(2,1)S(1)}, u32[]{:S(2)}, u32[]{:S(2)}) collective-permute-start(bf16[304,640]{1,0:T(8,128)(2,1)S(1)} %get-tuple-element.32), channel_id=1, source_target_pairs={{0,1},{1,0},{2,3},{3,2},{4,5},{5,4},{6,7},{7,6},{8,9},{9,8},{10,11... | collective-permute-start | bytes 1167368 | tf_op jit(solution)/shard_map/ppermute | solution.py:25
  6.9 36.3 %collective-permute-start.7 = (bf16[304,640]{1,0:T(8,128)(2,1)S(1)}, bf16[304,640]{1,0:T(8,128)(2,1)S(1)}, u32[]{:S(2)}, u32[]{:S(2)}) collective-permute-start(bf16[304,640]{1,0:T(8,128)(2,1)S(1)} %get-tuple-element.33), channel_id=1, source_target_pairs={{0,2},{1,3},{2,0},{3,1},{4,6},{5,7},{6,4},{7,5},{8,10},{9,11},{10,... | collective-permute-start | bytes 1167368 | tf_op jit(solution)/shard_map/ppermute | solution.py:25
  8.9 34.9 %collective-permute-start.8 = (bf16[304,640]{1,0:T(8,128)(2,1)S(1)}, bf16[304,640]{1,0:T(8,128)(2,1)S(1)}, u32[]{:S(2)}, u32[]{:S(2)}) collective-permute-start(bf16[304,640]{1,0:T(8,128)(2,1)S(1)} %get-tuple-element.34), channel_id=1, source_target_pairs={{0,3},{1,2},{2,1},{3,0},{4,7},{5,6},{6,5},{7,4},{8,11},{9,10},{10,... | collective-permute-start | bytes 1167368 | tf_op jit(solution)/shard_map/ppermute | solution.py:25
  10.3 19.6 %collective-permute-start.12 = (bf16[1,24,4096]{2,1,0:T(8,128)(2,1)S(1)}, bf16[1,24,4096]{2,1,0:T(8,128)(2,1)S(1)}, u32[]{:S(2)}, u32[]{:S(2)}) collective-permute-start(bf16[1,24,4096]{2,1,0:T(8,128)(2,1)S(1)} %copy-done), channel_id=1, source_target_pairs={{0,1},{1,0},{2,3},{3,2},{4,5},{5,4},{6,7},{7,6},{8,9},{9,8},{10,11... | collective-permute-start | bytes 589832 | tf_op jit(solution)/shard_map/ppermute | solution.py:25
  10.4 21.3 %collective-permute-start.13 = (bf16[1,24,4096]{2,1,0:T(8,128)(2,1)S(1)}, bf16[1,24,4096]{2,1,0:T(8,128)(2,1)S(1)}, u32[]{:S(2)}, u32[]{:S(2)}) collective-permute-start(bf16[1,24,4096]{2,1,0:T(8,128)(2,1)S(1)} %copy-done), channel_id=1, source_target_pairs={{0,2},{1,3},{2,0},{3,1},{4,6},{5,7},{6,4},{7,5},{8,10},{9,11},{10,... | collective-permute-start | bytes 589832 | tf_op jit(solution)/shard_map/ppermute | solution.py:25
  30.0 8.6 %collective-permute-start.4 = (bf16[304,256]{1,0:T(8,128)(2,1)S(1)}, bf16[304,256]{1,0:T(8,128)(2,1)S(1)}, u32[]{:S(2)}, u32[]{:S(2)}) collective-permute-start(bf16[304,256]{1,0:T(8,128)(2,1)S(1)} %get-tuple-element.28), channel_id=1, source_target_pairs={{0,2},{1,3},{2,0},{3,1},{4,6},{5,7},{6,4},{7,5},{8,10},{9,11},{10,... | collective-permute-start | bytes 466952 | tf_op jit(solution)/shard_map/ppermute | solution.py:25
  31.7 8.2 %collective-permute-start.5 = (bf16[304,256]{1,0:T(8,128)(2,1)S(1)}, bf16[304,256]{1,0:T(8,128)(2,1)S(1)}, u32[]{:S(2)}, u32[]{:S(2)}) collective-permute-start(bf16[304,256]{1,0:T(8,128)(2,1)S(1)} %get-tuple-element.29), channel_id=1, source_target_pairs={{0,3},{1,2},{2,1},{3,0},{4,7},{5,6},{6,5},{7,4},{8,11},{9,10},{10,... | collective-permute-start | bytes 466952 | tf_op jit(solution)/shard_map/ppermute | solution.py:25
  38.5 22.2 %collective-permute-start.14 = (bf16[1,24,2048]{2,1,0:T(8,128)(2,1)S(1)}, bf16[1,24,2048]{2,1,0:T(8,128)(2,1)S(1)}, u32[]{:S(2)}, u32[]{:S(2)}) collective-permute-start(bf16[1,24,2048]{2,1,0:T(8,128)(2,1)S(1)} %slice.8), channel_id=1, source_target_pairs={{0,2},{1,3},{2,0},{3,1},{4,6},{5,7},{6,4},{7,5},{8,10},{9,11},{10,... | collective-permute-start | bytes 294920 | tf_op jit(solution)/shard_map/ppermute | solution.py:25
  40.0 20.7 %collective-permute-start.15 = (bf16[1,24,2048]{2,1,0:T(8,128)(2,1)S(1)}, bf16[1,24,2048]{2,1,0:T(8,128)(2,1)S(1)}, u32[]{:S(2)}, u32[]{:S(2)}) collective-permute-start(bf16[1,24,2048]{2,1,0:T(8,128)(2,1)S(1)} %slice.9), channel_id=1, source_target_pairs={{0,1},{1,0},{2,3},{3,2},{4,5},{5,4},{6,7},{7,6},{8,9},{9,8},{10,11... | collective-permute-start | bytes 294920 | tf_op jit(solution)/shard_map/ppermute | solution.py:25
  42.6 16.8 %collective-permute-start = (bf16[304,128]{1,0:T(8,128)(2,1)S(1)}, bf16[304,128]{1,0:T(8,128)(2,1)S(1)}, u32[]{:S(2)}, u32[]{:S(2)}) collective-permute-start(bf16[304,128]{1,0:T(8,128)(2,1)S(1)} %get-tuple-element.22), channel_id=1, source_target_pairs={{0,1},{1,0},{2,3},{3,2},{4,5},{5,4},{6,7},{7,6},{8,9},{9,8},{10,11... | collective-permute-start | bytes 233480 | tf_op jit(solution)/shard_map/ppermute | solution.py:25
  43.2 16.3 %collective-permute-start.1 = (bf16[304,128]{1,0:T(8,128)(2,1)S(1)}, bf16[304,128]{1,0:T(8,128)(2,1)S(1)}, u32[]{:S(2)}, u32[]{:S(2)}) collective-permute-start(bf16[304,128]{1,0:T(8,128)(2,1)S(1)} %get-tuple-element.23), channel_id=1, source_target_pairs={{0,2},{1,3},{2,0},{3,1},{4,6},{5,7},{6,4},{7,5},{8,10},{9,11},{10,... | collective-permute-start | bytes 233480 | tf_op jit(solution)/shard_map/ppermute | solution.py:25
  43.8 15.7 %collective-permute-start.2 = (bf16[304,128]{1,0:T(8,128)(2,1)S(1)}, bf16[304,128]{1,0:T(8,128)(2,1)S(1)}, u32[]{:S(2)}, u32[]{:S(2)}) collective-permute-start(bf16[304,128]{1,0:T(8,128)(2,1)S(1)} %get-tuple-element.24), channel_id=1, source_target_pairs={{0,3},{1,2},{2,1},{3,0},{4,7},{5,6},{6,5},{7,4},{8,11},{9,10},{10,... | collective-permute-start | bytes 233480 | tf_op jit(solution)/shard_map/ppermute | solution.py:25
  59.4 25.7 %copy-start.1 = (f32[4096]{0:T(1024)S(1)}, f32[4096]{0:T(1024)}, u32[]{:S(2)}) copy-start(f32[4096]{0:T(1024)} %param.9) | copy-start | bytes 49156
  61.2 1.2 %collective-permute-start.16 = (f32[1,4096]{1,0:T(1,128)S(1)}, f32[1,4096]{1,0:T(1,128)S(1)}, u32[]{:S(2)}, u32[]{:S(2)}) collective-permute-start(f32[1,4096]{1,0:T(1,128)S(1)} %gain_terms.1), channel_id=1, source_target_pairs={{0,4},{4,0},{8,12},{12,8},{16,20},{20,16},{24,28},{28,24},{1,5},{5... | collective-permute-start | bytes 49160 | tf_op jit(solution)/shard_map/ppermute | solution.py:25
  62.5 3.8 %collective-permute-start.17 = (f32[1,4096]{1,0:T(1,128)S(1)}, f32[1,4096]{1,0:T(1,128)S(1)}, u32[]{:S(2)}, u32[]{:S(2)}) collective-permute-start(f32[1,4096]{1,0:T(1,128)S(1)} %add.15), channel_id=1, source_target_pairs={{0,8},{4,12},{8,0},{12,4},{16,24},{20,28},{24,16},{28,20},{1,9},{5... | collective-permute-start | bytes 49160 | tf_op jit(solution)/shard_map/ppermute | solution.py:25
  66.3 4.7 %collective-permute-start.18 = (f32[1,4096]{1,0:T(1,128)S(1)}, f32[1,4096]{1,0:T(1,128)S(1)}, u32[]{:S(2)}, u32[]{:S(2)}) collective-permute-start(f32[1,4096]{1,0:T(1,128)S(1)} %add.16), channel_id=1, source_target_pairs={{0,16},{4,20},{8,24},{12,28},{16,0},{20,4},{24,8},{28,12},{1,17},{... | collective-permute-start | bytes 49160 | tf_op jit(solution)/shard_map/ppermute | solution.py:25
  71.0 3.8 %collective-permute-start.19 = (f32[1,4096]{1,0:T(1,128)S(1)}, f32[1,4096]{1,0:T(1,128)S(1)}, u32[]{:S(2)}, u32[]{:S(2)}) collective-permute-start(f32[1,4096]{1,0:T(1,128)S(1)} %add.17), channel_id=1, source_target_pairs={{0,1},{1,0},{2,3},{3,2},{4,5},{5,4},{6,7},{7,6},{8,9},{9,8},{10,11... | collective-permute-start | bytes 49160 | tf_op jit(solution)/shard_map/ppermute | solution.py:25
  74.9 4.4 %collective-permute-start.20 = (f32[1,4096]{1,0:T(1,128)S(1)}, f32[1,4096]{1,0:T(1,128)S(1)}, u32[]{:S(2)}, u32[]{:S(2)}) collective-permute-start(f32[1,4096]{1,0:T(1,128)S(1)} %add.18), channel_id=1, source_target_pairs={{0,2},{1,3},{2,0},{3,1},{4,6},{5,7},{6,4},{7,5},{8,10},{9,11},{10,... | collective-permute-start | bytes 49160 | tf_op jit(solution)/shard_map/ppermute | solution.py:25
  75.8 6.5 %collective-permute-start.10 = (bf16[24,4096]{1,0:T(8,128)(2,1)S(1)}, bf16[24,4096]{1,0:T(8,128)(2,1)S(1)}, u32[]{:S(2)}, u32[]{:S(2)}) collective-permute-start(bf16[24,4096]{1,0:T(8,128)(2,1)S(1)} %get-tuple-element.38.refs_2_), channel_id=1, source_target_pairs={{0,2},{1,3},{2,0},{3,1},{4,6},{5,7},{6,4},{7,5},{8,10},{9,11},{10,... | collective-permute-start | bytes 589832 | tf_op jit(solution)/shard_map/ppermute | solution.py:25
  77.0 6.6 %collective-permute-start.11 = (bf16[24,4096]{1,0:T(8,128)(2,1)S(1)}, bf16[24,4096]{1,0:T(8,128)(2,1)S(1)}, u32[]{:S(2)}, u32[]{:S(2)}) collective-permute-start(bf16[24,4096]{1,0:T(8,128)(2,1)S(1)} %get-tuple-element.39.refs_3_), channel_id=1, source_target_pairs={{0,3},{1,2},{2,1},{3,0},{4,7},{5,6},{6,5},{7,4},{8,11},{9,10},{10,... | collective-permute-start | bytes 589832 | tf_op jit(solution)/shard_map/ppermute | solution.py:25
  77.5 7.5 %collective-permute-start.9 = (bf16[24,4096]{1,0:T(8,128)(2,1)S(1)}, bf16[24,4096]{1,0:T(8,128)(2,1)S(1)}, u32[]{:S(2)}, u32[]{:S(2)}) collective-permute-start(bf16[24,4096]{1,0:T(8,128)(2,1)S(1)} %get-tuple-element.37.refs_1_), channel_id=1, source_target_pairs={{0,1},{1,0},{2,3},{3,2},{4,5},{5,4},{6,7},{7,6},{8,9},{9,8},{10,11... | collective-permute-start | bytes 589832 | tf_op jit(solution)/shard_map/ppermute | solution.py:25

commit v5 on v4

--- a/solution.py
+++ b/solution.py
@@ -8,7 +8,7 @@
 
 HEAD_DIM = 64
 LANES = 128
-PROJ_BLOCK = 1024
+PROJ_BLOCK = 2048
 TAIL_PAIRS = (2, 1)
 ATTN_ROWS = 512
 PACK_VMEM = 8 << 20
@@ -218,7 +218,7 @@
     enc, width = enc_final.shape[1], enc_final.shape[2]
     rows = {0: [(enc_final, 0, 0, width)]}
     if seq_size == 4:
-        half = width // 2 // LANES * LANES
+        half = 9 * width // 16 // LANES * LANES
         near = {j: exchange(enc_final, "seq", seq_size, j) for j in (1, 2)}
         for j in (1, 2):
             rows[j] = [(near[j], 0, 0, width)]
@@ -304,6 +304,26 @@
         compiler_params=pltpu.CompilerParams(vmem_limit_bytes=PACK_VMEM),
         name="finish",
     )(own, *received, enc_final, norm_gain.reshape(1, width))
+
+
+def peer_steps(docs, seq_size):
+    steps = [1 << b for b in range(seq_size.bit_length() - 1)]
+    if docs % 2:
+        return [(step, 0) for step in steps]
+    return [(steps[n], steps[n + 1] if n + 1 < len(steps) else 0) for n in range(0, len(steps), 2)]
+
+
+def add_peers(value, docs, seq_size, low, high):
+    if not high:
+        return value + exchange(value, "seq", seq_size, low)
+    spots = [(d, s) for d in range(docs) for s in range(seq_size)]
+    one = [(d * seq_size + s, d * seq_size + (s ^ (low if d % 2 else low ^ high))) for d, s in spots]
+    two = [(d * seq_size + s, d * seq_size + (s ^ high)) for d, s in spots if d % 2]
+    first = lax.ppermute(value, ("dp", "seq"), one)
+    second = lax.ppermute(value, ("dp", "seq"), two)
+    own = jnp.where(lax.axis_index("dp") % 2 == 0, value, 0.0)
+    part = (first + second) + own
+    return part + exchange(part, "dp", docs, 1)
 
 
 def body(
@@ -326,20 +346,15 @@
     weights = load_weights(chunks, key_weight, value_weight, gathered[-1][0])
     prior = None
     for index in range(len(chunks)):
-        outs = chunk_terms(
-            gathered[index], weights[index], prior, dec, enc, index == len(chunks) - 1
-        )
+        outs = chunk_terms(gathered[index], weights[index], prior, dec, enc, index == len(chunks) - 1)
         prior = outs[0]
     received = [exchange(outs[j], "seq", seq, j) for j in range(1, seq)]
     gain = gain_terms(outs, rows)
     enc_grad = finish(outs[0], received, enc_final, norm_gain)
-    stages = [
-        (axis, size, 1 << b)
-        for axis, size in (("dp", docs), ("seq", seq))
-        for b in range(size.bit_length() - 1)
-    ]
-    for axis, size, step in stages:
-        gain = gain + exchange(gain, axis, size, step)
+    for b in range(docs.bit_length() - 1):
+        gain = gain + exchange(gain, "dp", docs, 1 << b)
+    for low, high in peer_steps(docs, seq):
+        gain = add_peers(gain, docs, seq, low, high)
     return (enc_grad, gain[0] / docs)
 
 
@@ -356,9 +371,7 @@
     )
 
     def whole(*args):
-        step = jax.shard_map(
-            body, mesh=mesh, in_specs=placed, out_specs=(P("dp", "seq", None), P()), check_vma=False
-        )
+        step = jax.shard_map(body, mesh=mesh, in_specs=placed, out_specs=(P("dp", "seq", None), P()), check_vma=False)
         return step(*args)
 
     return whole

time: 86.3 us -> 90.8 us (1.052)
  waiting for transfers between devices: 36.7 us -> 40.8 us
    ppermute x0 -> x2, waiting for transfers between devices: none -> 3.69 us  [the longest x1 3.69 us: add_peers(): first = lax.ppermute(value, ('dp', 'seq'), one)]
    ppermute x0 -> x2, starting transfers between devices: none -> 0.99 us  [the longest x1 0.65 us: add_peers(): second = lax.ppermute(value, ('dp', 'seq'), two)]
    ppermute x21 -> x20, starting transfers between devices: 27.7 us -> 27 us  [exchange(): return lax.ppermute(value, axis, xor_pairs(size, step))]
    ppermute x21 -> x20, waiting for transfers between devices: 36.7 us -> 37.1 us  [exchange(): return lax.ppermute(value, axis, xor_pairs(size, step))]
  transfers between devices with their start and end apart: 21 -> 22, of which waited for: 9 -> 8; matrix products, arithmetic and copies ran while one was open for 1% -> 1% of each run, Pallas kernels for 20% -> 19%
where the time goes in v5:
time: 90.8 us; the launch traced here: 90.6 us
  waiting for transfers between devices  40.8 us (45%)
  starting transfers between devices  28 us (31%)
  Pallas kernels  20.2 us (22%)
    ppermute x20, waiting for transfers between devices, exchange(): return lax.ppermute(value, axis, xor_pairs(size, step))  37.1 us
    ppermute x20, starting transfers between devices, exchange(): return lax.ppermute(value, axis, xor_pairs(size, step))  27 us
    pallas_call x3, Pallas kernels, chunk_terms(): pl.pallas_call(kernel, out_shape=out_shape, in_specs=[vmem] * len(operand...  8.61 us
    pallas_call x1, Pallas kernels, load_weights(): pl.pallas_call(kernel, out_shape=[jax.ShapeDtypeStruct((width, 2 * chunk_...  5.89 us
    pallas_call x3, Pallas kernels, pack_chunk(): pl.pallas_call(kernel, out_shape=[jax.ShapeDtypeStruct((sum(rows), width)...  4.19 us
    ppermute x1, waiting for transfers between devices, add_peers(): first = lax.ppermute(value, ('dp', 'seq'), one)  3.69 us
  transfers between devices with their start and end apart: 22, of which 8 were waited for; matrix products, arithmetic and copies ran while one was open for 1% of the time, Pallas kernels for 19%

profile of v5, /device:TPU:0, one launch (start us, length us, event | category | flops | bytes accessed | tf_op | source)
XLA Modules:
  0.0 90.6 jit_solution(7882116677858963837)
XLA Ops:
  0.6 1.3 %shard_map.96 = (bf16[304,256]{1,0:T(8,128)(2,1)S(1)}, bf16[304,256]{1,0:T(8,128)(2,1)S(1)}, bf16[304,256]{1,0:T(8,128)(2,1)S(1)}, bf16[304,256]{1,0:T(8,128)(2,1)S(1)}) custom-call(bf16[2,1,128,2048]{3,2,1,0:T(8,128)(2,1)} %q_ref.5, bf16[2,1,128,2048]{3,2,1,0:T(8,128)(2,1)} %g_ref.5, bf16[2,1,24,2048]{3,2,1,0:T(8,128)(2,1)} %k_ref.5, ...), custom_call_target="tpu_custom_call" | custom-call | tf_op jit(solution)/shard_map/pallas_call | solution.py:83
  2.0 3.0 %collective-permute-start.3 = (bf16[304,256]{1,0:T(8,128)(2,1)S(1)}, bf16[304,256]{1,0:T(8,128)(2,1)S(1)}, u32[]{:S(2)}, u32[]{:S(2)}) collective-permute-start(bf16[304,256]{1,0:T(8,128)(2,1)S(1)} %get-tuple-element.27), channel_id=1, source_target_pairs={{0,1},{1,0},{2,3},{3,2},{4,5},{5,4},{6,7},{7,6},{8,9},{9,8},{10,11... | collective-permute-start | bytes 466952 | tf_op jit(solution)/shard_map/ppermute | solution.py:25
  5.0 1.8 %shard_map.97 = (bf16[304,640]{1,0:T(8,128)(2,1)S(1)}, bf16[304,640]{1,0:T(8,128)(2,1)S(1)}, bf16[304,640]{1,0:T(8,128)(2,1)S(1)}, bf16[304,640]{1,0:T(8,128)(2,1)S(1)}) custom-call(bf16[2,1,128,2048]{3,2,1,0:T(8,128)(2,1)} %q_ref.5, bf16[2,1,128,2048]{3,2,1,0:T(8,128)(2,1)} %g_ref.5, bf16[2,1,24,2048]{3,2,1,0:T(8,128)(2,1)} %k_ref.5, ...), custom_call_target="tpu_custom_call" | custom-call | tf_op jit(solution)/shard_map/pallas_call | solution.py:83
  6.8 0.1 collective-permute-start.6
  6.9 2.0 %collective-permute-start.7 = (bf16[304,640]{1,0:T(8,128)(2,1)S(1)}, bf16[304,640]{1,0:T(8,128)(2,1)S(1)}, u32[]{:S(2)}, u32[]{:S(2)}) collective-permute-start(bf16[304,640]{1,0:T(8,128)(2,1)S(1)} %get-tuple-element.33), channel_id=1, source_target_pairs={{0,2},{1,3},{2,0},{3,1},{4,6},{5,7},{6,4},{7,5},{8,10},{9,11},{10,... | collective-permute-start | bytes 1167368 | tf_op jit(solution)/shard_map/ppermute | solution.py:25
  8.9 1.4 %collective-permute-start.8 = (bf16[304,640]{1,0:T(8,128)(2,1)S(1)}, bf16[304,640]{1,0:T(8,128)(2,1)S(1)}, u32[]{:S(2)}, u32[]{:S(2)}) collective-permute-start(bf16[304,640]{1,0:T(8,128)(2,1)S(1)} %get-tuple-element.34), channel_id=1, source_target_pairs={{0,3},{1,2},{2,1},{3,0},{4,7},{5,6},{6,5},{7,4},{8,11},{9,10},{10,... | collective-permute-start | bytes 1167368 | tf_op jit(solution)/shard_map/ppermute | solution.py:25
  10.3 1.5 %collective-permute-start.4 = (bf16[304,256]{1,0:T(8,128)(2,1)S(1)}, bf16[304,256]{1,0:T(8,128)(2,1)S(1)}, u32[]{:S(2)}, u32[]{:S(2)}) collective-permute-start(bf16[304,256]{1,0:T(8,128)(2,1)S(1)} %get-tuple-element.28), channel_id=1, source_target_pairs={{0,2},{1,3},{2,0},{3,1},{4,6},{5,7},{6,4},{7,5},{8,10},{9,11},{10,... | collective-permute-start | bytes 466952 | tf_op jit(solution)/shard_map/ppermute | solution.py:25
  11.9 0.0 collective-permute-done.3.refs_1_
  11.9 0.5 collective-permute-start.12
  12.4 16.7 %collective-permute-done.4.refs_2_ = bf16[304,256]{1,0:T(8,128)(2,1)S(1)} collective-permute-done((bf16[304,256]{1,0:T(8,128)(2,1)S(1)}, bf16[304,256]{1,0:T(8,128)(2,1)S(1)}, u32[]{:S(2)}, u32[]{:S(2)}) %collective-permute-start.4) | collective-permute-done | bytes 155680 | tf_op jit(solution)/shard_map/ppermute | solution.py:25
  29.1 1.7 %collective-permute-start.13 = (bf16[1,24,4096]{2,1,0:T(8,128)(2,1)S(1)}, bf16[1,24,4096]{2,1,0:T(8,128)(2,1)S(1)}, u32[]{:S(2)}, u32[]{:S(2)}) collective-permute-start(bf16[1,24,4096]{2,1,0:T(8,128)(2,1)S(1)} %copy-done), channel_id=1, source_target_pairs={{0,2},{1,3},{2,0},{3,1},{4,6},{5,7},{6,4},{7,5},{8,10},{9,11},{10,... | collective-permute-start | bytes 589832 | tf_op jit(solution)/shard_map/ppermute | solution.py:25
  30.8 1.9 %collective-permute-start.5 = (bf16[304,256]{1,0:T(8,128)(2,1)S(1)}, bf16[304,256]{1,0:T(8,128)(2,1)S(1)}, u32[]{:S(2)}, u32[]{:S(2)}) collective-permute-start(bf16[304,256]{1,0:T(8,128)(2,1)S(1)} %get-tuple-element.29), channel_id=1, source_target_pairs={{0,3},{1,2},{2,1},{3,0},{4,7},{5,6},{6,5},{7,4},{8,11},{9,10},{10,... | collective-permute-start | bytes 466952 | tf_op jit(solution)/shard_map/ppermute | solution.py:25
  32.7 6.4 %collective-permute-done.13.refs_6_ = bf16[1,24,4096]{2,1,0:T(8,128)(2,1)S(1)} collective-permute-done((bf16[1,24,4096]{2,1,0:T(8,128)(2,1)S(1)}, bf16[1,24,4096]{2,1,0:T(8,128)(2,1)S(1)}, u32[]{:S(2)}, u32[]{:S(2)}) %collective-permute-start.13) | collective-permute-done | bytes 196640 | tf_op jit(solution)/shard_map/ppermute | solution.py:25
  39.1 1.7 %collective-permute-start.14 = (bf16[1,24,2304]{2,1,0:T(8,128)(2,1)S(1)}, bf16[1,24,2304]{2,1,0:T(8,128)(2,1)S(1)}, u32[]{:S(2)}, u32[]{:S(2)}) collective-permute-start(bf16[1,24,2304]{2,1,0:T(8,128)(2,1)S(1)} %slice.8), channel_id=1, source_target_pairs={{0,2},{1,3},{2,0},{3,1},{4,6},{5,7},{6,4},{7,5},{8,10},{9,11},{10,... | collective-permute-start | bytes 331784 | tf_op jit(solution)/shard_map/ppermute | solution.py:25
  40.8 0.0 collective-permute-done.5.refs_3_
  40.8 1.6 %collective-permute-start.15 = (bf16[1,24,1792]{2,1,0:T(8,128)(2,1)S(1)}, bf16[1,24,1792]{2,1,0:T(8,128)(2,1)S(1)}, u32[]{:S(2)}, u32[]{:S(2)}) collective-permute-start(bf16[1,24,1792]{2,1,0:T(8,128)(2,1)S(1)} %slice.9), channel_id=1, source_target_pairs={{0,1},{1,0},{2,3},{3,2},{4,5},{5,4},{6,7},{7,6},{8,9},{9,8},{10,11... | collective-permute-start | bytes 258056 | tf_op jit(solution)/shard_map/ppermute | solution.py:25
  42.4 1.1 %shard_map.95 = (bf16[304,128]{1,0:T(8,128)(2,1)S(1)}, bf16[304,128]{1,0:T(8,128)(2,1)S(1)}, bf16[304,128]{1,0:T(8,128)(2,1)S(1)}, bf16[304,128]{1,0:T(8,128)(2,1)S(1)}) custom-call(bf16[2,1,128,2048]{3,2,1,0:T(8,128)(2,1)} %q_ref.5, bf16[2,1,128,2048]{3,2,1,0:T(8,128)(2,1)} %g_ref.5, bf16[2,1,24,2048]{3,2,1,0:T(8,128)(2,1)} %k_ref.5, ...), custom_call_target="tpu_custom_call" | custom-call | tf_op jit(solution)/shard_map/pallas_call | solution.py:83
  43.5 0.0 collective-permute-done.6.refs_1_
  43.5 0.6 collective-permute-start
  44.1 0.0 collective-permute-done.7.refs_2_
  44.1 0.3 collective-permute-start.1
  44.4 0.0 collective-permute-done.8.refs_3_
  44.4 2.6 %collective-permute-start.2 = (bf16[304,128]{1,0:T(8,128)(2,1)S(1)}, bf16[304,128]{1,0:T(8,128)(2,1)S(1)}, u32[]{:S(2)}, u32[]{:S(2)}) collective-permute-start(bf16[304,128]{1,0:T(8,128)(2,1)S(1)} %get-tuple-element.24), channel_id=1, source_target_pairs={{0,3},{1,2},{2,1},{3,0},{4,7},{5,6},{6,5},{7,4},{8,11},{9,10},{10,... | collective-permute-start | bytes 233480 | tf_op jit(solution)/shard_map/ppermute | solution.py:25
  47.1 5.9 %load_weights.1 = (bf16[4096,1280]{1,0:T(8,128)(2,1)S(1)}, bf16[4096,512]{1,0:T(8,128)(2,1)S(1)}, bf16[4096,256]{1,0:T(8,128)(2,1)S(1)}) custom-call(bf16[2,4096,512]{2,1,0:T(8,128)(2,1)} %kw.1, bf16[2,4096,512]{2,1,0:T(8,128)(2,1)} %vw.1, bf16[304,128]{1,0:T(8,128)(2,1)S(1)} %get-tuple-element.21.after_ref.refs_0_), custom_call_target="tpu_custom_call" | custom-call | tf_op jit(solution)/shard_map/load_weights/pallas_call | solution.py:168
  53.0 5.1 %shard_map.98.refs_5_ = f32[96,4096]{1,0:T(8,128)S(1)} custom-call(bf16[304,640]{1,0:T(8,128)(2,1)S(1)} %get-tuple-element.31.refs_0_, bf16[304,640]{1,0:T(8,128)(2,1)S(1)} %collective-permute-done.6.refs_1_, bf16[304,640]{1,0:T(8,128)(2,1)S(1)} %collective-permute-done.7.refs_2_, bf16[304,640]{1,0:T(8,128)(2,1)S(1)} %collective-permute-done.8.refs_3_, ...), custom_call_target="tpu_custom_call" | custom-call | tf_op jit(solution)/shard_map/pallas_call | solution.py:207
  58.1 2.2 %shard_map.99.refs_5_ = f32[96,4096]{1,0:T(8,128)S(1)} custom-call(bf16[304,256]{1,0:T(8,128)(2,1)S(1)} %get-tuple-element.26.refs_0_, bf16[304,256]{1,0:T(8,128)(2,1)S(1)} %collective-permute-done.3.refs_1_, bf16[304,256]{1,0:T(8,128)(2,1)S(1)} %collective-permute-done.4.refs_2_, bf16[304,256]{1,0:T(8,128)(2,1)S(1)} %collective-permute-done.5.refs_3_, ...), custom_call_target="tpu_custom_call" | custom-call | tf_op jit(solution)/shard_map/pallas_call | solution.py:207
  60.3 0.0 copy-start.1
  60.4 0.0 collective-permute-done.refs_1_
  60.4 0.0 collective-permute-done.1.refs_2_
  60.4 1.2 %shard_map.100 = (f32[24,4096]{1,0:T(8,128)S(1)}, bf16[24,4096]{1,0:T(8,128)(2,1)S(1)}, bf16[24,4096]{1,0:T(8,128)(2,1)S(1)}, bf16[24,4096]{1,0:T(8,128)(2,1)S(1)}) custom-call(bf16[304,128]{1,0:T(8,128)(2,1)S(1)} %get-tuple-element.21.after_ref.refs_0_, bf16[304,128]{1,0:T(8,128)(2,1)S(1)} %collective-permute-done.refs_1_, ...), custom_call_target="tpu_custom_call" | custom-call | tf_op jit(solution)/shard_map/pallas_call | solution.py:207
  61.6 0.5 gain_terms.1
  62.2 0.1 collective-permute-start.16
  62.3 1.2 %collective-permute-done.16 = f32[1,4096]{1,0:T(1,128)S(1)} collective-permute-done((f32[1,4096]{1,0:T(1,128)S(1)}, f32[1,4096]{1,0:T(1,128)S(1)}, u32[]{:S(2)}, u32[]{:S(2)}) %collective-permute-start.16) | collective-permute-done | bytes 16416 | tf_op jit(solution)/shard_map/ppermute | solution.py:25
  63.4 1.6 %collective-permute-start.17 = (f32[1,4096]{1,0:T(1,128)S(1)}, f32[1,4096]{1,0:T(1,128)S(1)}, u32[]{:S(2)}, u32[]{:S(2)}) collective-permute-start(f32[1,4096]{1,0:T(1,128)S(1)} %add.22), channel_id=1, source_target_pairs={{0,8},{4,12},{8,0},{12,4},{16,24},{20,28},{24,16},{28,20},{1,9},{5... | collective-permute-start | bytes 49160 | tf_op jit(solution)/shard_map/ppermute | solution.py:25
  65.1 2.2 %collective-permute-done.17 = f32[1,4096]{1,0:T(1,128)S(1)} collective-permute-done((f32[1,4096]{1,0:T(1,128)S(1)}, f32[1,4096]{1,0:T(1,128)S(1)}, u32[]{:S(2)}, u32[]{:S(2)}) %collective-permute-start.17) | collective-permute-done | bytes 16416 | tf_op jit(solution)/shard_map/ppermute | solution.py:25
  67.3 2.7 %collective-permute-start.18 = (f32[1,4096]{1,0:T(1,128)S(1)}, f32[1,4096]{1,0:T(1,128)S(1)}, u32[]{:S(2)}, u32[]{:S(2)}) collective-permute-start(f32[1,4096]{1,0:T(1,128)S(1)} %add.23), channel_id=1, source_target_pairs={{0,16},{4,20},{8,24},{12,28},{16,0},{20,4},{24,8},{28,12},{1,17},{... | collective-permute-start | bytes 49160 | tf_op jit(solution)/shard_map/ppermute | solution.py:25
  69.9 2.0 %collective-permute-done.18 = f32[1,4096]{1,0:T(1,128)S(1)} collective-permute-done((f32[1,4096]{1,0:T(1,128)S(1)}, f32[1,4096]{1,0:T(1,128)S(1)}, u32[]{:S(2)}, u32[]{:S(2)}) %collective-permute-start.18) | collective-permute-done | bytes 16416 | tf_op jit(solution)/shard_map/ppermute | solution.py:25
  72.0 0.3 collective-permute-start.19
  72.3 0.7 collective-permute-start.20
  73.0 3.7 %collective-permute-done.19 = f32[1,4096]{1,0:T(1,128)S(1)} collective-permute-done((f32[1,4096]{1,0:T(1,128)S(1)}, f32[1,4096]{1,0:T(1,128)S(1)}, u32[]{:S(2)}, u32[]{:S(2)}) %collective-permute-start.19) | collective-permute-done | bytes 16416 | tf_op jit(solution)/shard_map/ppermute | solution.py:322
  76.7 0.1 collective-permute-start.21
  76.8 0.6 collective-permute-start.10
  77.4 1.5 %collective-permute-start.11 = (bf16[24,4096]{1,0:T(8,128)(2,1)S(1)}, bf16[24,4096]{1,0:T(8,128)(2,1)S(1)}, u32[]{:S(2)}, u32[]{:S(2)}) collective-permute-start(bf16[24,4096]{1,0:T(8,128)(2,1)S(1)} %get-tuple-element.39.refs_3_), channel_id=1, source_target_pairs={{0,3},{1,2},{2,1},{3,0},{4,7},{5,6},{6,5},{7,4},{8,11},{9,10},{10,... | collective-permute-start | bytes 589832 | tf_op jit(solution)/shard_map/ppermute | solution.py:25
  78.9 1.5 %collective-permute-start.9 = (bf16[24,4096]{1,0:T(8,128)(2,1)S(1)}, bf16[24,4096]{1,0:T(8,128)(2,1)S(1)}, u32[]{:S(2)}, u32[]{:S(2)}) collective-permute-start(bf16[24,4096]{1,0:T(8,128)(2,1)S(1)} %get-tuple-element.37.refs_1_), channel_id=1, source_target_pairs={{0,1},{1,0},{2,3},{3,2},{4,5},{5,4},{6,7},{7,6},{8,9},{9,8},{10,11... | collective-permute-start | bytes 589832 | tf_op jit(solution)/shard_map/ppermute | solution.py:25
  80.4 0.6 add_multiply_fusion
  81.0 7.3 %collective-permute-done.10.refs_1_ = bf16[24,4096]{1,0:T(8,128)(2,1)S(1)} collective-permute-done((bf16[24,4096]{1,0:T(8,128)(2,1)S(1)}, bf16[24,4096]{1,0:T(8,128)(2,1)S(1)}, u32[]{:S(2)}, u32[]{:S(2)}) %collective-permute-start.10) | collective-permute-done | bytes 196640 | tf_op jit(solution)/shard_map/ppermute | solution.py:25
  88.3 1.2 %collective-permute-done.9.refs_0_ = bf16[24,4096]{1,0:T(8,128)(2,1)S(1)} collective-permute-done((bf16[24,4096]{1,0:T(8,128)(2,1)S(1)}, bf16[24,4096]{1,0:T(8,128)(2,1)S(1)}, u32[]{:S(2)}, u32[]{:S(2)}) %collective-permute-start.9) | collective-permute-done | bytes 196640 | tf_op jit(solution)/shard_map/ppermute | solution.py:25
  89.6 1.0 %finish.1 = bf16[1,24,4096]{2,1,0:T(8,128)(2,1)} custom-call(f32[24,4096]{1,0:T(8,128)S(1)} %get-tuple-element.36.own_ref.refs_0_, bf16[24,4096]{1,0:T(8,128)(2,1)S(1)} %collective-permute-done.9.refs_0_, bf16[24,4096]{1,0:T(8,128)(2,1)S(1)} %collective-permute-done.10.refs_1_, bf16[24,4096]{1,0:T(8,128)(2,1)S(1)} %collective-permute-done.11.refs_2_, ...), custom_call_target="tpu_custom_call" | custom-call | tf_op jit(solution)/shard_map/finish/pallas_call | solution.py:301
  (16 shorter events, 0.1 us)
Async XLA Ops:
  0.6 11.2 %copy-start = (bf16[1,24,4096]{2,1,0:T(8,128)(2,1)S(1)}, bf16[1,24,4096]{2,1,0:T(8,128)(2,1)}, u32[]{:S(2)}) copy-start(bf16[1,24,4096]{2,1,0:T(8,128)(2,1)} %refs_4_.1) | copy-start | bytes 589828
  2.0 9.9 %collective-permute-start.3 = (bf16[304,256]{1,0:T(8,128)(2,1)S(1)}, bf16[304,256]{1,0:T(8,128)(2,1)S(1)}, u32[]{:S(2)}, u32[]{:S(2)}) collective-permute-start(bf16[304,256]{1,0:T(8,128)(2,1)S(1)} %get-tuple-element.27), channel_id=1, source_target_pairs={{0,1},{1,0},{2,3},{3,2},{4,5},{5,4},{6,7},{7,6},{8,9},{9,8},{10,11... | collective-permute-start | bytes 466952 | tf_op jit(solution)/shard_map/ppermute | solution.py:25
  6.8 36.7 %collective-permute-start.6 = (bf16[304,640]{1,0:T(8,128)(2,1)S(1)}, bf16[304,640]{1,0:T(8,128)(2,1)S(1)}, u32[]{:S(2)}, u32[]{:S(2)}) collective-permute-start(bf16[304,640]{1,0:T(8,128)(2,1)S(1)} %get-tuple-element.32), channel_id=1, source_target_pairs={{0,1},{1,0},{2,3},{3,2},{4,5},{5,4},{6,7},{7,6},{8,9},{9,8},{10,11... | collective-permute-start | bytes 1167368 | tf_op jit(solution)/shard_map/ppermute | solution.py:25
  6.9 37.2 %collective-permute-start.7 = (bf16[304,640]{1,0:T(8,128)(2,1)S(1)}, bf16[304,640]{1,0:T(8,128)(2,1)S(1)}, u32[]{:S(2)}, u32[]{:S(2)}) collective-permute-start(bf16[304,640]{1,0:T(8,128)(2,1)S(1)} %get-tuple-element.33), channel_id=1, source_target_pairs={{0,2},{1,3},{2,0},{3,1},{4,6},{5,7},{6,4},{7,5},{8,10},{9,11},{10,... | collective-permute-start | bytes 1167368 | tf_op jit(solution)/shard_map/ppermute | solution.py:25
  8.9 35.5 %collective-permute-start.8 = (bf16[304,640]{1,0:T(8,128)(2,1)S(1)}, bf16[304,640]{1,0:T(8,128)(2,1)S(1)}, u32[]{:S(2)}, u32[]{:S(2)}) collective-permute-start(bf16[304,640]{1,0:T(8,128)(2,1)S(1)} %get-tuple-element.34), channel_id=1, source_target_pairs={{0,3},{1,2},{2,1},{3,0},{4,7},{5,6},{6,5},{7,4},{8,11},{9,10},{10,... | collective-permute-start | bytes 1167368 | tf_op jit(solution)/shard_map/ppermute | solution.py:25
  10.3 18.8 %collective-permute-start.4 = (bf16[304,256]{1,0:T(8,128)(2,1)S(1)}, bf16[304,256]{1,0:T(8,128)(2,1)S(1)}, u32[]{:S(2)}, u32[]{:S(2)}) collective-permute-start(bf16[304,256]{1,0:T(8,128)(2,1)S(1)} %get-tuple-element.28), channel_id=1, source_target_pairs={{0,2},{1,3},{2,0},{3,1},{4,6},{5,7},{6,4},{7,5},{8,10},{9,11},{10,... | collective-permute-start | bytes 466952 | tf_op jit(solution)/shard_map/ppermute | solution.py:25
  11.9 18.9 %collective-permute-start.12 = (bf16[1,24,4096]{2,1,0:T(8,128)(2,1)S(1)}, bf16[1,24,4096]{2,1,0:T(8,128)(2,1)S(1)}, u32[]{:S(2)}, u32[]{:S(2)}) collective-permute-start(bf16[1,24,4096]{2,1,0:T(8,128)(2,1)S(1)} %copy-done), channel_id=1, source_target_pairs={{0,1},{1,0},{2,3},{3,2},{4,5},{5,4},{6,7},{7,6},{8,9},{9,8},{10,11... | collective-permute-start | bytes 589832 | tf_op jit(solution)/shard_map/ppermute | solution.py:25
  29.1 10.0 %collective-permute-start.13 = (bf16[1,24,4096]{2,1,0:T(8,128)(2,1)S(1)}, bf16[1,24,4096]{2,1,0:T(8,128)(2,1)S(1)}, u32[]{:S(2)}, u32[]{:S(2)}) collective-permute-start(bf16[1,24,4096]{2,1,0:T(8,128)(2,1)S(1)} %copy-done), channel_id=1, source_target_pairs={{0,2},{1,3},{2,0},{3,1},{4,6},{5,7},{6,4},{7,5},{8,10},{9,11},{10,... | collective-permute-start | bytes 589832 | tf_op jit(solution)/shard_map/ppermute | solution.py:25
  30.8 10.0 %collective-permute-start.5 = (bf16[304,256]{1,0:T(8,128)(2,1)S(1)}, bf16[304,256]{1,0:T(8,128)(2,1)S(1)}, u32[]{:S(2)}, u32[]{:S(2)}) collective-permute-start(bf16[304,256]{1,0:T(8,128)(2,1)S(1)} %get-tuple-element.29), channel_id=1, source_target_pairs={{0,3},{1,2},{2,1},{3,0},{4,7},{5,6},{6,5},{7,4},{8,11},{9,10},{10,... | collective-permute-start | bytes 466952 | tf_op jit(solution)/shard_map/ppermute | solution.py:25
  39.1 22.5 %collective-permute-start.14 = (bf16[1,24,2304]{2,1,0:T(8,128)(2,1)S(1)}, bf16[1,24,2304]{2,1,0:T(8,128)(2,1)S(1)}, u32[]{:S(2)}, u32[]{:S(2)}) collective-permute-start(bf16[1,24,2304]{2,1,0:T(8,128)(2,1)S(1)} %slice.8), channel_id=1, source_target_pairs={{0,2},{1,3},{2,0},{3,1},{4,6},{5,7},{6,4},{7,5},{8,10},{9,11},{10,... | collective-permute-start | bytes 331784 | tf_op jit(solution)/shard_map/ppermute | solution.py:25
  40.8 20.8 %collective-permute-start.15 = (bf16[1,24,1792]{2,1,0:T(8,128)(2,1)S(1)}, bf16[1,24,1792]{2,1,0:T(8,128)(2,1)S(1)}, u32[]{:S(2)}, u32[]{:S(2)}) collective-permute-start(bf16[1,24,1792]{2,1,0:T(8,128)(2,1)S(1)} %slice.9), channel_id=1, source_target_pairs={{0,1},{1,0},{2,3},{3,2},{4,5},{5,4},{6,7},{7,6},{8,9},{9,8},{10,11... | collective-permute-start | bytes 258056 | tf_op jit(solution)/shard_map/ppermute | solution.py:25
  43.5 16.8 %collective-permute-start = (bf16[304,128]{1,0:T(8,128)(2,1)S(1)}, bf16[304,128]{1,0:T(8,128)(2,1)S(1)}, u32[]{:S(2)}, u32[]{:S(2)}) collective-permute-start(bf16[304,128]{1,0:T(8,128)(2,1)S(1)} %get-tuple-element.22), channel_id=1, source_target_pairs={{0,1},{1,0},{2,3},{3,2},{4,5},{5,4},{6,7},{7,6},{8,9},{9,8},{10,11... | collective-permute-start | bytes 233480 | tf_op jit(solution)/shard_map/ppermute | solution.py:25
  44.1 16.3 %collective-permute-start.1 = (bf16[304,128]{1,0:T(8,128)(2,1)S(1)}, bf16[304,128]{1,0:T(8,128)(2,1)S(1)}, u32[]{:S(2)}, u32[]{:S(2)}) collective-permute-start(bf16[304,128]{1,0:T(8,128)(2,1)S(1)} %get-tuple-element.23), channel_id=1, source_target_pairs={{0,2},{1,3},{2,0},{3,1},{4,6},{5,7},{6,4},{7,5},{8,10},{9,11},{10,... | collective-permute-start | bytes 233480 | tf_op jit(solution)/shard_map/ppermute | solution.py:25
  44.4 15.9 %collective-permute-start.2 = (bf16[304,128]{1,0:T(8,128)(2,1)S(1)}, bf16[304,128]{1,0:T(8,128)(2,1)S(1)}, u32[]{:S(2)}, u32[]{:S(2)}) collective-permute-start(bf16[304,128]{1,0:T(8,128)(2,1)S(1)} %get-tuple-element.24), channel_id=1, source_target_pairs={{0,3},{1,2},{2,1},{3,0},{4,7},{5,6},{6,5},{7,4},{8,11},{9,10},{10,... | collective-permute-start | bytes 233480 | tf_op jit(solution)/shard_map/ppermute | solution.py:25
  60.3 29.2 %copy-start.1 = (f32[4096]{0:T(1024)S(1)}, f32[4096]{0:T(1024)}, u32[]{:S(2)}) copy-start(f32[4096]{0:T(1024)} %param.9) | copy-start | bytes 49156
  62.2 1.2 %collective-permute-start.16 = (f32[1,4096]{1,0:T(1,128)S(1)}, f32[1,4096]{1,0:T(1,128)S(1)}, u32[]{:S(2)}, u32[]{:S(2)}) collective-permute-start(f32[1,4096]{1,0:T(1,128)S(1)} %gain_terms.1), channel_id=1, source_target_pairs={{0,4},{4,0},{8,12},{12,8},{16,20},{20,16},{24,28},{28,24},{1,5},{5... | collective-permute-start | bytes 49160 | tf_op jit(solution)/shard_map/ppermute | solution.py:25
  63.4 3.8 %collective-permute-start.17 = (f32[1,4096]{1,0:T(1,128)S(1)}, f32[1,4096]{1,0:T(1,128)S(1)}, u32[]{:S(2)}, u32[]{:S(2)}) collective-permute-start(f32[1,4096]{1,0:T(1,128)S(1)} %add.22), channel_id=1, source_target_pairs={{0,8},{4,12},{8,0},{12,4},{16,24},{20,28},{24,16},{28,20},{1,9},{5... | collective-permute-start | bytes 49160 | tf_op jit(solution)/shard_map/ppermute | solution.py:25
  67.3 4.7 %collective-permute-start.18 = (f32[1,4096]{1,0:T(1,128)S(1)}, f32[1,4096]{1,0:T(1,128)S(1)}, u32[]{:S(2)}, u32[]{:S(2)}) collective-permute-start(f32[1,4096]{1,0:T(1,128)S(1)} %add.23), channel_id=1, source_target_pairs={{0,16},{4,20},{8,24},{12,28},{16,0},{20,4},{24,8},{28,12},{1,17},{... | collective-permute-start | bytes 49160 | tf_op jit(solution)/shard_map/ppermute | solution.py:25
  72.0 4.7 %collective-permute-start.19 = (f32[1,4096]{1,0:T(1,128)S(1)}, f32[1,4096]{1,0:T(1,128)S(1)}, u32[]{:S(2)}, u32[]{:S(2)}) collective-permute-start(f32[1,4096]{1,0:T(1,128)S(1)} %add.24), channel_id=1, source_target_pairs={{0,3},{1,2},{2,1},{3,0},{4,5},{5,4},{6,7},{7,6},{8,11},{9,10},{10,... | collective-permute-start | bytes 49160 | tf_op jit(solution)/shard_map/ppermute | solution.py:322
  72.3 4.4 %collective-permute-start.20 = (f32[1,4096]{1,0:T(1,128)S(1)}, f32[1,4096]{1,0:T(1,128)S(1)}, u32[]{:S(2)}, u32[]{:S(2)}) collective-permute-start(f32[1,4096]{1,0:T(1,128)S(1)} %add.24), channel_id=1, source_target_pairs={{4,6},{5,7},{6,4},{7,5},{12,14},{13,15},{14,12},{15,13},{20,22},{2... | collective-permute-start | bytes 49160 | tf_op jit(solution)/shard_map/ppermute | solution.py:323
  76.7 3.6 %collective-permute-start.21 = (f32[1,4096]{1,0:T(1,128)S(1)}, f32[1,4096]{1,0:T(1,128)S(1)}, u32[]{:S(2)}, u32[]{:S(2)}) collective-permute-start(f32[1,4096]{1,0:T(1,128)S(1)} %fusion), channel_id=1, source_target_pairs={{0,4},{4,0},{8,12},{12,8},{16,20},{20,16},{24,28},{28,24},{1,5},{5... | collective-permute-start | bytes 49160 | tf_op jit(solution)/shard_map/ppermute | solution.py:25
  76.8 11.5 %collective-permute-start.10 = (bf16[24,4096]{1,0:T(8,128)(2,1)S(1)}, bf16[24,4096]{1,0:T(8,128)(2,1)S(1)}, u32[]{:S(2)}, u32[]{:S(2)}) collective-permute-start(bf16[24,4096]{1,0:T(8,128)(2,1)S(1)} %get-tuple-element.38.refs_2_), channel_id=1, source_target_pairs={{0,2},{1,3},{2,0},{3,1},{4,6},{5,7},{6,4},{7,5},{8,10},{9,11},{10,... | collective-permute-start | bytes 589832 | tf_op jit(solution)/shard_map/ppermute | solution.py:25
  77.4 11.0 %collective-permute-start.11 = (bf16[24,4096]{1,0:T(8,128)(2,1)S(1)}, bf16[24,4096]{1,0:T(8,128)(2,1)S(1)}, u32[]{:S(2)}, u32[]{:S(2)}) collective-permute-start(bf16[24,4096]{1,0:T(8,128)(2,1)S(1)} %get-tuple-element.39.refs_3_), channel_id=1, source_target_pairs={{0,3},{1,2},{2,1},{3,0},{4,7},{5,6},{6,5},{7,4},{8,11},{9,10},{10,... | collective-permute-start | bytes 589832 | tf_op jit(solution)/shard_map/ppermute | solution.py:25
  78.9 10.7 %collective-permute-start.9 = (bf16[24,4096]{1,0:T(8,128)(2,1)S(1)}, bf16[24,4096]{1,0:T(8,128)(2,1)S(1)}, u32[]{:S(2)}, u32[]{:S(2)}) collective-permute-start(bf16[24,4096]{1,0:T(8,128)(2,1)S(1)} %get-tuple-element.37.refs_1_), channel_id=1, source_target_pairs={{0,1},{1,0},{2,3},{3,2},{4,5},{5,4},{6,7},{7,6},{8,9},{9,8},{10,11... | collective-permute-start | bytes 589832 | tf_op jit(solution)/shard_map/ppermute | solution.py:25

commit v6 on v5

--- a/solution.py
+++ b/solution.py
@@ -239,7 +239,28 @@
     return rows
 
 
-def gain_terms(pieces, rows):
+def row_scales(rows):
+    whole = [j for j in sorted(rows) if len(rows[j]) == 1]
+    enc = rows[0][0][0].shape[1]
+
+    def kernel(*refs):
+        for n, j in enumerate(whole):
+            _, base, _, cols = rows[j][0]
+            x = refs[n][0, pl.ds(base, enc), :].astype(F32)
+            total = jnp.sum(x * x, axis=-1, keepdims=True)
+            scale = lax.rsqrt(total * (1.0 / cols) + 1e-06)
+            refs[-1][pl.ds(n * enc, enc), :] = jnp.broadcast_to(scale, (enc, LANES))
+
+    scales = pl.pallas_call(
+        kernel,
+        out_shape=jax.ShapeDtypeStruct((len(whole) * enc, LANES), F32),
+        compiler_params=pltpu.CompilerParams(vmem_limit_bytes=PACK_VMEM),
+        name="row_scales",
+    )(*[rows[j][0][0] for j in whole])
+    return whole, scales
+
+
+def gain_terms(pieces, rows, whole, scales):
     count = len(pieces)
     enc, width = pieces[0].shape
     arrays = []
@@ -256,9 +277,12 @@
     cuts = sorted({first for spots in places for _, _, first, _ in spots} | {width})
 
     def kernel(*refs):
-        piece_refs, row_refs, out_ref = refs[:count], refs[count:-1], refs[-1]
+        piece_refs, row_refs, scale_ref, out_ref = refs[:count], refs[count:-2], refs[-2], refs[-1]
         inv = []
-        for spots in places:
+        for j, spots in enumerate(places):
+            if j in whole:
+                inv.append(scale_ref[pl.ds(whole.index(j) * enc, enc), 0:1])
+                continue
             square = 0.0
             for n, base, _, cols in spots:
                 x = row_refs[n][0, pl.ds(base, enc), :].astype(F32)
@@ -279,7 +303,7 @@
         out_shape=jax.ShapeDtypeStruct((1, width), F32),
         compiler_params=pltpu.CompilerParams(vmem_limit_bytes=PACK_VMEM),
         name="gain_terms",
-    )(*pieces, *arrays)
+    )(*pieces, *arrays, scales)
 
 
 def finish(own, received, enc_final, norm_gain):
@@ -349,7 +373,8 @@
         outs = chunk_terms(gathered[index], weights[index], prior, dec, enc, index == len(chunks) - 1)
         prior = outs[0]
     received = [exchange(outs[j], "seq", seq, j) for j in range(1, seq)]
-    gain = gain_terms(outs, rows)
+    whole, scales = row_scales(rows)
+    gain = gain_terms(outs, rows, whole, scales)
     enc_grad = finish(outs[0], received, enc_final, norm_gain)
     for b in range(docs.bit_length() - 1):
         gain = gain + exchange(gain, "dp", docs, 1 << b)

time: 90.8 us -> 91 us (level)
  no operation moved by 1% of the time
where the time goes in v6:
time: 91 us; the launch traced here: 90.7 us
  waiting for transfers between devices  40.8 us (45%)
  starting transfers between devices  28 us (31%)
  Pallas kernels  20.3 us (22%)
    ppermute x20, waiting for transfers between devices, exchange(): return lax.ppermute(value, axis, xor_pairs(size, step))  37.1 us
    ppermute x20, starting transfers between devices, exchange(): return lax.ppermute(value, axis, xor_pairs(size, step))  27 us
    pallas_call x3, Pallas kernels, chunk_terms(): pl.pallas_call(kernel, out_shape=out_shape, in_specs=[vmem] * len(operand...  8.63 us
    pallas_call x1, Pallas kernels, load_weights(): pl.pallas_call(kernel, out_shape=[jax.ShapeDtypeStruct((width, 2 * chunk_...  5.89 us
    pallas_call x3, Pallas kernels, pack_chunk(): pl.pallas_call(kernel, out_shape=[jax.ShapeDtypeStruct((sum(rows), width)...  4.19 us
    ppermute x1, waiting for transfers between devices, add_peers(): first = lax.ppermute(value, ('dp', 'seq'), one)  3.69 us
  transfers between devices with their start and end apart: 22, of which 8 were waited for; matrix products, arithmetic and copies ran while one was open for 1% of the time, Pallas kernels for 19%

profile of v6, /device:TPU:0, one launch (start us, length us, event | category | flops | bytes accessed | tf_op | source)
XLA Modules:
  0.0 90.7 jit_solution(8710045934114207698)
XLA Ops:
  0.6 1.3 %shard_map.96 = (bf16[304,256]{1,0:T(8,128)(2,1)S(1)}, bf16[304,256]{1,0:T(8,128)(2,1)S(1)}, bf16[304,256]{1,0:T(8,128)(2,1)S(1)}, bf16[304,256]{1,0:T(8,128)(2,1)S(1)}) custom-call(bf16[2,1,128,2048]{3,2,1,0:T(8,128)(2,1)} %q_ref.5, bf16[2,1,128,2048]{3,2,1,0:T(8,128)(2,1)} %g_ref.5, bf16[2,1,24,2048]{3,2,1,0:T(8,128)(2,1)} %k_ref.5, ...), custom_call_target="tpu_custom_call" | custom-call | tf_op jit(solution)/shard_map/pallas_call | solution.py:83
  2.0 3.0 %collective-permute-start.3 = (bf16[304,256]{1,0:T(8,128)(2,1)S(1)}, bf16[304,256]{1,0:T(8,128)(2,1)S(1)}, u32[]{:S(2)}, u32[]{:S(2)}) collective-permute-start(bf16[304,256]{1,0:T(8,128)(2,1)S(1)} %get-tuple-element.27), channel_id=1, source_target_pairs={{0,1},{1,0},{2,3},{3,2},{4,5},{5,4},{6,7},{7,6},{8,9},{9,8},{10,11... | collective-permute-start | bytes 466952 | tf_op jit(solution)/shard_map/ppermute | solution.py:25
  5.0 1.8 %shard_map.97 = (bf16[304,640]{1,0:T(8,128)(2,1)S(1)}, bf16[304,640]{1,0:T(8,128)(2,1)S(1)}, bf16[304,640]{1,0:T(8,128)(2,1)S(1)}, bf16[304,640]{1,0:T(8,128)(2,1)S(1)}) custom-call(bf16[2,1,128,2048]{3,2,1,0:T(8,128)(2,1)} %q_ref.5, bf16[2,1,128,2048]{3,2,1,0:T(8,128)(2,1)} %g_ref.5, bf16[2,1,24,2048]{3,2,1,0:T(8,128)(2,1)} %k_ref.5, ...), custom_call_target="tpu_custom_call" | custom-call | tf_op jit(solution)/shard_map/pallas_call | solution.py:83
  6.8 0.1 collective-permute-start.6
  6.9 2.0 %collective-permute-start.7 = (bf16[304,640]{1,0:T(8,128)(2,1)S(1)}, bf16[304,640]{1,0:T(8,128)(2,1)S(1)}, u32[]{:S(2)}, u32[]{:S(2)}) collective-permute-start(bf16[304,640]{1,0:T(8,128)(2,1)S(1)} %get-tuple-element.33), channel_id=1, source_target_pairs={{0,2},{1,3},{2,0},{3,1},{4,6},{5,7},{6,4},{7,5},{8,10},{9,11},{10,... | collective-permute-start | bytes 1167368 | tf_op jit(solution)/shard_map/ppermute | solution.py:25
  8.9 1.4 %collective-permute-start.8 = (bf16[304,640]{1,0:T(8,128)(2,1)S(1)}, bf16[304,640]{1,0:T(8,128)(2,1)S(1)}, u32[]{:S(2)}, u32[]{:S(2)}) collective-permute-start(bf16[304,640]{1,0:T(8,128)(2,1)S(1)} %get-tuple-element.34), channel_id=1, source_target_pairs={{0,3},{1,2},{2,1},{3,0},{4,7},{5,6},{6,5},{7,4},{8,11},{9,10},{10,... | collective-permute-start | bytes 1167368 | tf_op jit(solution)/shard_map/ppermute | solution.py:25
  10.3 1.5 %collective-permute-start.4 = (bf16[304,256]{1,0:T(8,128)(2,1)S(1)}, bf16[304,256]{1,0:T(8,128)(2,1)S(1)}, u32[]{:S(2)}, u32[]{:S(2)}) collective-permute-start(bf16[304,256]{1,0:T(8,128)(2,1)S(1)} %get-tuple-element.28), channel_id=1, source_target_pairs={{0,2},{1,3},{2,0},{3,1},{4,6},{5,7},{6,4},{7,5},{8,10},{9,11},{10,... | collective-permute-start | bytes 466952 | tf_op jit(solution)/shard_map/ppermute | solution.py:25
  11.9 0.0 collective-permute-done.3.refs_1_
  11.9 0.5 collective-permute-start.12
  12.4 16.7 %collective-permute-done.4.refs_2_ = bf16[304,256]{1,0:T(8,128)(2,1)S(1)} collective-permute-done((bf16[304,256]{1,0:T(8,128)(2,1)S(1)}, bf16[304,256]{1,0:T(8,128)(2,1)S(1)}, u32[]{:S(2)}, u32[]{:S(2)}) %collective-permute-start.4) | collective-permute-done | bytes 155680 | tf_op jit(solution)/shard_map/ppermute | solution.py:25
  29.1 1.7 %collective-permute-start.13 = (bf16[1,24,4096]{2,1,0:T(8,128)(2,1)S(1)}, bf16[1,24,4096]{2,1,0:T(8,128)(2,1)S(1)}, u32[]{:S(2)}, u32[]{:S(2)}) collective-permute-start(bf16[1,24,4096]{2,1,0:T(8,128)(2,1)S(1)} %copy-done), channel_id=1, source_target_pairs={{0,2},{1,3},{2,0},{3,1},{4,6},{5,7},{6,4},{7,5},{8,10},{9,11},{10,... | collective-permute-start | bytes 589832 | tf_op jit(solution)/shard_map/ppermute | solution.py:25
  30.8 1.9 %collective-permute-start.5 = (bf16[304,256]{1,0:T(8,128)(2,1)S(1)}, bf16[304,256]{1,0:T(8,128)(2,1)S(1)}, u32[]{:S(2)}, u32[]{:S(2)}) collective-permute-start(bf16[304,256]{1,0:T(8,128)(2,1)S(1)} %get-tuple-element.29), channel_id=1, source_target_pairs={{0,3},{1,2},{2,1},{3,0},{4,7},{5,6},{6,5},{7,4},{8,11},{9,10},{10,... | collective-permute-start | bytes 466952 | tf_op jit(solution)/shard_map/ppermute | solution.py:25
  32.7 6.4 %collective-permute-done.13.refs_2_.refs_6_ = bf16[1,24,4096]{2,1,0:T(8,128)(2,1)S(1)} collective-permute-done((bf16[1,24,4096]{2,1,0:T(8,128)(2,1)S(1)}, bf16[1,24,4096]{2,1,0:T(8,128)(2,1)S(1)}, u32[]{:S(2)}, u32[]{:S(2)}) %collective-permute-start.13) | collective-permute-done | bytes 196640 | tf_op jit(solution)/shard_map/ppermute | solution.py:25
  39.1 1.7 %collective-permute-start.14 = (bf16[1,24,2304]{2,1,0:T(8,128)(2,1)S(1)}, bf16[1,24,2304]{2,1,0:T(8,128)(2,1)S(1)}, u32[]{:S(2)}, u32[]{:S(2)}) collective-permute-start(bf16[1,24,2304]{2,1,0:T(8,128)(2,1)S(1)} %slice.8), channel_id=1, source_target_pairs={{0,2},{1,3},{2,0},{3,1},{4,6},{5,7},{6,4},{7,5},{8,10},{9,11},{10,... | collective-permute-start | bytes 331784 | tf_op jit(solution)/shard_map/ppermute | solution.py:25
  40.8 0.0 collective-permute-done.5.refs_3_
  40.8 1.6 %collective-permute-start.15 = (bf16[1,24,1792]{2,1,0:T(8,128)(2,1)S(1)}, bf16[1,24,1792]{2,1,0:T(8,128)(2,1)S(1)}, u32[]{:S(2)}, u32[]{:S(2)}) collective-permute-start(bf16[1,24,1792]{2,1,0:T(8,128)(2,1)S(1)} %slice.9), channel_id=1, source_target_pairs={{0,1},{1,0},{2,3},{3,2},{4,5},{5,4},{6,7},{7,6},{8,9},{9,8},{10,11... | collective-permute-start | bytes 258056 | tf_op jit(solution)/shard_map/ppermute | solution.py:25
  42.4 1.1 %shard_map.95 = (bf16[304,128]{1,0:T(8,128)(2,1)S(1)}, bf16[304,128]{1,0:T(8,128)(2,1)S(1)}, bf16[304,128]{1,0:T(8,128)(2,1)S(1)}, bf16[304,128]{1,0:T(8,128)(2,1)S(1)}) custom-call(bf16[2,1,128,2048]{3,2,1,0:T(8,128)(2,1)} %q_ref.5, bf16[2,1,128,2048]{3,2,1,0:T(8,128)(2,1)} %g_ref.5, bf16[2,1,24,2048]{3,2,1,0:T(8,128)(2,1)} %k_ref.5, ...), custom_call_target="tpu_custom_call" | custom-call | tf_op jit(solution)/shard_map/pallas_call | solution.py:83
  43.5 0.0 collective-permute-done.6.refs_1_
  43.5 0.6 collective-permute-start
  44.1 0.0 collective-permute-done.7.refs_2_
  44.1 0.3 collective-permute-start.1
  44.4 0.0 collective-permute-done.8.refs_3_
  44.4 2.6 %collective-permute-start.2 = (bf16[304,128]{1,0:T(8,128)(2,1)S(1)}, bf16[304,128]{1,0:T(8,128)(2,1)S(1)}, u32[]{:S(2)}, u32[]{:S(2)}) collective-permute-start(bf16[304,128]{1,0:T(8,128)(2,1)S(1)} %get-tuple-element.24), channel_id=1, source_target_pairs={{0,3},{1,2},{2,1},{3,0},{4,7},{5,6},{6,5},{7,4},{8,11},{9,10},{10,... | collective-permute-start | bytes 233480 | tf_op jit(solution)/shard_map/ppermute | solution.py:25
  47.1 5.9 %load_weights.1 = (bf16[4096,1280]{1,0:T(8,128)(2,1)S(1)}, bf16[4096,512]{1,0:T(8,128)(2,1)S(1)}, bf16[4096,256]{1,0:T(8,128)(2,1)S(1)}) custom-call(bf16[2,4096,512]{2,1,0:T(8,128)(2,1)} %kw.1, bf16[2,4096,512]{2,1,0:T(8,128)(2,1)} %vw.1, bf16[304,128]{1,0:T(8,128)(2,1)S(1)} %get-tuple-element.21.after_ref.refs_0_), custom_call_target="tpu_custom_call" | custom-call | tf_op jit(solution)/shard_map/load_weights/pallas_call | solution.py:168
  53.0 0.2 row_scales.1.refs_9_
  53.2 5.2 %shard_map.98.refs_5_ = f32[96,4096]{1,0:T(8,128)S(1)} custom-call(bf16[304,640]{1,0:T(8,128)(2,1)S(1)} %get-tuple-element.31.refs_0_, bf16[304,640]{1,0:T(8,128)(2,1)S(1)} %collective-permute-done.6.refs_1_, bf16[304,640]{1,0:T(8,128)(2,1)S(1)} %collective-permute-done.7.refs_2_, bf16[304,640]{1,0:T(8,128)(2,1)S(1)} %collective-permute-done.8.refs_3_, ...), custom_call_target="tpu_custom_call" | custom-call | tf_op jit(solution)/shard_map/pallas_call | solution.py:207
  58.3 2.2 %shard_map.99.refs_5_ = f32[96,4096]{1,0:T(8,128)S(1)} custom-call(bf16[304,256]{1,0:T(8,128)(2,1)S(1)} %get-tuple-element.26.refs_0_, bf16[304,256]{1,0:T(8,128)(2,1)S(1)} %collective-permute-done.3.refs_1_, bf16[304,256]{1,0:T(8,128)(2,1)S(1)} %collective-permute-done.4.refs_2_, bf16[304,256]{1,0:T(8,128)(2,1)S(1)} %collective-permute-done.5.refs_3_, ...), custom_call_target="tpu_custom_call" | custom-call | tf_op jit(solution)/shard_map/pallas_call | solution.py:207
  60.5 0.0 copy-start.1
  60.6 0.0 collective-permute-done.refs_1_
  60.6 1.2 %shard_map.100 = (f32[24,4096]{1,0:T(8,128)S(1)}, bf16[24,4096]{1,0:T(8,128)(2,1)S(1)}, bf16[24,4096]{1,0:T(8,128)(2,1)S(1)}, bf16[24,4096]{1,0:T(8,128)(2,1)S(1)}) custom-call(bf16[304,128]{1,0:T(8,128)(2,1)S(1)} %get-tuple-element.21.after_ref.refs_0_, bf16[304,128]{1,0:T(8,128)(2,1)S(1)} %collective-permute-done.refs_1_, ...), custom_call_target="tpu_custom_call" | custom-call | tf_op jit(solution)/shard_map/pallas_call | solution.py:207
  61.9 0.4 gain_terms.1
  62.3 0.1 collective-permute-start.16
  62.4 1.2 %collective-permute-done.16 = f32[1,4096]{1,0:T(1,128)S(1)} collective-permute-done((f32[1,4096]{1,0:T(1,128)S(1)}, f32[1,4096]{1,0:T(1,128)S(1)}, u32[]{:S(2)}, u32[]{:S(2)}) %collective-permute-start.16) | collective-permute-done | bytes 16416 | tf_op jit(solution)/shard_map/ppermute | solution.py:25
  63.6 1.6 %collective-permute-start.17 = (f32[1,4096]{1,0:T(1,128)S(1)}, f32[1,4096]{1,0:T(1,128)S(1)}, u32[]{:S(2)}, u32[]{:S(2)}) collective-permute-start(f32[1,4096]{1,0:T(1,128)S(1)} %add.22), channel_id=1, source_target_pairs={{0,8},{4,12},{8,0},{12,4},{16,24},{20,28},{24,16},{28,20},{1,9},{5... | collective-permute-start | bytes 49160 | tf_op jit(solution)/shard_map/ppermute | solution.py:25
  65.2 2.2 %collective-permute-done.17 = f32[1,4096]{1,0:T(1,128)S(1)} collective-permute-done((f32[1,4096]{1,0:T(1,128)S(1)}, f32[1,4096]{1,0:T(1,128)S(1)}, u32[]{:S(2)}, u32[]{:S(2)}) %collective-permute-start.17) | collective-permute-done | bytes 16416 | tf_op jit(solution)/shard_map/ppermute | solution.py:25
  67.4 2.7 %collective-permute-start.18 = (f32[1,4096]{1,0:T(1,128)S(1)}, f32[1,4096]{1,0:T(1,128)S(1)}, u32[]{:S(2)}, u32[]{:S(2)}) collective-permute-start(f32[1,4096]{1,0:T(1,128)S(1)} %add.23), channel_id=1, source_target_pairs={{0,16},{4,20},{8,24},{12,28},{16,0},{20,4},{24,8},{28,12},{1,17},{... | collective-permute-start | bytes 49160 | tf_op jit(solution)/shard_map/ppermute | solution.py:25
  70.1 2.0 %collective-permute-done.18 = f32[1,4096]{1,0:T(1,128)S(1)} collective-permute-done((f32[1,4096]{1,0:T(1,128)S(1)}, f32[1,4096]{1,0:T(1,128)S(1)}, u32[]{:S(2)}, u32[]{:S(2)}) %collective-permute-start.18) | collective-permute-done | bytes 16416 | tf_op jit(solution)/shard_map/ppermute | solution.py:25
  72.1 0.3 collective-permute-start.19
  72.5 0.7 collective-permute-start.20
  73.1 3.7 %collective-permute-done.19 = f32[1,4096]{1,0:T(1,128)S(1)} collective-permute-done((f32[1,4096]{1,0:T(1,128)S(1)}, f32[1,4096]{1,0:T(1,128)S(1)}, u32[]{:S(2)}, u32[]{:S(2)}) %collective-permute-start.19) | collective-permute-done | bytes 16416 | tf_op jit(solution)/shard_map/ppermute | solution.py:346
  76.9 0.1 collective-permute-start.21
  76.9 0.6 collective-permute-start.10
  77.5 1.5 %collective-permute-start.11 = (bf16[24,4096]{1,0:T(8,128)(2,1)S(1)}, bf16[24,4096]{1,0:T(8,128)(2,1)S(1)}, u32[]{:S(2)}, u32[]{:S(2)}) collective-permute-start(bf16[24,4096]{1,0:T(8,128)(2,1)S(1)} %get-tuple-element.39.refs_3_), channel_id=1, source_target_pairs={{0,3},{1,2},{2,1},{3,0},{4,7},{5,6},{6,5},{7,4},{8,11},{9,10},{10,... | collective-permute-start | bytes 589832 | tf_op jit(solution)/shard_map/ppermute | solution.py:25
  79.0 1.5 %collective-permute-start.9 = (bf16[24,4096]{1,0:T(8,128)(2,1)S(1)}, bf16[24,4096]{1,0:T(8,128)(2,1)S(1)}, u32[]{:S(2)}, u32[]{:S(2)}) collective-permute-start(bf16[24,4096]{1,0:T(8,128)(2,1)S(1)} %get-tuple-element.37.refs_1_), channel_id=1, source_target_pairs={{0,1},{1,0},{2,3},{3,2},{4,5},{5,4},{6,7},{7,6},{8,9},{9,8},{10,11... | collective-permute-start | bytes 589832 | tf_op jit(solution)/shard_map/ppermute | solution.py:25
  80.5 0.6 add_multiply_fusion
  81.1 7.3 %collective-permute-done.10.refs_1_ = bf16[24,4096]{1,0:T(8,128)(2,1)S(1)} collective-permute-done((bf16[24,4096]{1,0:T(8,128)(2,1)S(1)}, bf16[24,4096]{1,0:T(8,128)(2,1)S(1)}, u32[]{:S(2)}, u32[]{:S(2)}) %collective-permute-start.10) | collective-permute-done | bytes 196640 | tf_op jit(solution)/shard_map/ppermute | solution.py:25
  88.5 1.2 %collective-permute-done.9.refs_0_ = bf16[24,4096]{1,0:T(8,128)(2,1)S(1)} collective-permute-done((bf16[24,4096]{1,0:T(8,128)(2,1)S(1)}, bf16[24,4096]{1,0:T(8,128)(2,1)S(1)}, u32[]{:S(2)}, u32[]{:S(2)}) %collective-permute-start.9) | collective-permute-done | bytes 196640 | tf_op jit(solution)/shard_map/ppermute | solution.py:25
  89.7 1.0 %finish.1 = bf16[1,24,4096]{2,1,0:T(8,128)(2,1)} custom-call(f32[24,4096]{1,0:T(8,128)S(1)} %get-tuple-element.36.own_ref.refs_0_, bf16[24,4096]{1,0:T(8,128)(2,1)S(1)} %collective-permute-done.9.refs_0_, bf16[24,4096]{1,0:T(8,128)(2,1)S(1)} %collective-permute-done.10.refs_1_, bf16[24,4096]{1,0:T(8,128)(2,1)S(1)} %collective-permute-done.11.refs_2_, ...), custom_call_target="tpu_custom_call" | custom-call | tf_op jit(solution)/shard_map/finish/pallas_call | solution.py:325
  (17 shorter events, 0.1 us)
Async XLA Ops:
  0.6 11.2 %copy-start = (bf16[1,24,4096]{2,1,0:T(8,128)(2,1)S(1)}, bf16[1,24,4096]{2,1,0:T(8,128)(2,1)}, u32[]{:S(2)}) copy-start(bf16[1,24,4096]{2,1,0:T(8,128)(2,1)} %refs_4_.1) | copy-start | bytes 589828
  2.0 9.9 %collective-permute-start.3 = (bf16[304,256]{1,0:T(8,128)(2,1)S(1)}, bf16[304,256]{1,0:T(8,128)(2,1)S(1)}, u32[]{:S(2)}, u32[]{:S(2)}) collective-permute-start(bf16[304,256]{1,0:T(8,128)(2,1)S(1)} %get-tuple-element.27), channel_id=1, source_target_pairs={{0,1},{1,0},{2,3},{3,2},{4,5},{5,4},{6,7},{7,6},{8,9},{9,8},{10,11... | collective-permute-start | bytes 466952 | tf_op jit(solution)/shard_map/ppermute | solution.py:25
  6.8 36.7 %collective-permute-start.6 = (bf16[304,640]{1,0:T(8,128)(2,1)S(1)}, bf16[304,640]{1,0:T(8,128)(2,1)S(1)}, u32[]{:S(2)}, u32[]{:S(2)}) collective-permute-start(bf16[304,640]{1,0:T(8,128)(2,1)S(1)} %get-tuple-element.32), channel_id=1, source_target_pairs={{0,1},{1,0},{2,3},{3,2},{4,5},{5,4},{6,7},{7,6},{8,9},{9,8},{10,11... | collective-permute-start | bytes 1167368 | tf_op jit(solution)/shard_map/ppermute | solution.py:25
  6.9 37.2 %collective-permute-start.7 = (bf16[304,640]{1,0:T(8,128)(2,1)S(1)}, bf16[304,640]{1,0:T(8,128)(2,1)S(1)}, u32[]{:S(2)}, u32[]{:S(2)}) collective-permute-start(bf16[304,640]{1,0:T(8,128)(2,1)S(1)} %get-tuple-element.33), channel_id=1, source_target_pairs={{0,2},{1,3},{2,0},{3,1},{4,6},{5,7},{6,4},{7,5},{8,10},{9,11},{10,... | collective-permute-start | bytes 1167368 | tf_op jit(solution)/shard_map/ppermute | solution.py:25
  8.9 35.5 %collective-permute-start.8 = (bf16[304,640]{1,0:T(8,128)(2,1)S(1)}, bf16[304,640]{1,0:T(8,128)(2,1)S(1)}, u32[]{:S(2)}, u32[]{:S(2)}) collective-permute-start(bf16[304,640]{1,0:T(8,128)(2,1)S(1)} %get-tuple-element.34), channel_id=1, source_target_pairs={{0,3},{1,2},{2,1},{3,0},{4,7},{5,6},{6,5},{7,4},{8,11},{9,10},{10,... | collective-permute-start | bytes 1167368 | tf_op jit(solution)/shard_map/ppermute | solution.py:25
  10.3 18.8 %collective-permute-start.4 = (bf16[304,256]{1,0:T(8,128)(2,1)S(1)}, bf16[304,256]{1,0:T(8,128)(2,1)S(1)}, u32[]{:S(2)}, u32[]{:S(2)}) collective-permute-start(bf16[304,256]{1,0:T(8,128)(2,1)S(1)} %get-tuple-element.28), channel_id=1, source_target_pairs={{0,2},{1,3},{2,0},{3,1},{4,6},{5,7},{6,4},{7,5},{8,10},{9,11},{10,... | collective-permute-start | bytes 466952 | tf_op jit(solution)/shard_map/ppermute | solution.py:25
  11.9 18.9 %collective-permute-start.12 = (bf16[1,24,4096]{2,1,0:T(8,128)(2,1)S(1)}, bf16[1,24,4096]{2,1,0:T(8,128)(2,1)S(1)}, u32[]{:S(2)}, u32[]{:S(2)}) collective-permute-start(bf16[1,24,4096]{2,1,0:T(8,128)(2,1)S(1)} %copy-done), channel_id=1, source_target_pairs={{0,1},{1,0},{2,3},{3,2},{4,5},{5,4},{6,7},{7,6},{8,9},{9,8},{10,11... | collective-permute-start | bytes 589832 | tf_op jit(solution)/shard_map/ppermute | solution.py:25
  29.1 10.0 %collective-permute-start.13 = (bf16[1,24,4096]{2,1,0:T(8,128)(2,1)S(1)}, bf16[1,24,4096]{2,1,0:T(8,128)(2,1)S(1)}, u32[]{:S(2)}, u32[]{:S(2)}) collective-permute-start(bf16[1,24,4096]{2,1,0:T(8,128)(2,1)S(1)} %copy-done), channel_id=1, source_target_pairs={{0,2},{1,3},{2,0},{3,1},{4,6},{5,7},{6,4},{7,5},{8,10},{9,11},{10,... | collective-permute-start | bytes 589832 | tf_op jit(solution)/shard_map/ppermute | solution.py:25
  30.8 10.0 %collective-permute-start.5 = (bf16[304,256]{1,0:T(8,128)(2,1)S(1)}, bf16[304,256]{1,0:T(8,128)(2,1)S(1)}, u32[]{:S(2)}, u32[]{:S(2)}) collective-permute-start(bf16[304,256]{1,0:T(8,128)(2,1)S(1)} %get-tuple-element.29), channel_id=1, source_target_pairs={{0,3},{1,2},{2,1},{3,0},{4,7},{5,6},{6,5},{7,4},{8,11},{9,10},{10,... | collective-permute-start | bytes 466952 | tf_op jit(solution)/shard_map/ppermute | solution.py:25
  39.1 22.7 %collective-permute-start.14 = (bf16[1,24,2304]{2,1,0:T(8,128)(2,1)S(1)}, bf16[1,24,2304]{2,1,0:T(8,128)(2,1)S(1)}, u32[]{:S(2)}, u32[]{:S(2)}) collective-permute-start(bf16[1,24,2304]{2,1,0:T(8,128)(2,1)S(1)} %slice.8), channel_id=1, source_target_pairs={{0,2},{1,3},{2,0},{3,1},{4,6},{5,7},{6,4},{7,5},{8,10},{9,11},{10,... | collective-permute-start | bytes 331784 | tf_op jit(solution)/shard_map/ppermute | solution.py:25
  40.8 21.0 %collective-permute-start.15 = (bf16[1,24,1792]{2,1,0:T(8,128)(2,1)S(1)}, bf16[1,24,1792]{2,1,0:T(8,128)(2,1)S(1)}, u32[]{:S(2)}, u32[]{:S(2)}) collective-permute-start(bf16[1,24,1792]{2,1,0:T(8,128)(2,1)S(1)} %slice.9), channel_id=1, source_target_pairs={{0,1},{1,0},{2,3},{3,2},{4,5},{5,4},{6,7},{7,6},{8,9},{9,8},{10,11... | collective-permute-start | bytes 258056 | tf_op jit(solution)/shard_map/ppermute | solution.py:25
  43.5 17.1 %collective-permute-start = (bf16[304,128]{1,0:T(8,128)(2,1)S(1)}, bf16[304,128]{1,0:T(8,128)(2,1)S(1)}, u32[]{:S(2)}, u32[]{:S(2)}) collective-permute-start(bf16[304,128]{1,0:T(8,128)(2,1)S(1)} %get-tuple-element.22), channel_id=1, source_target_pairs={{0,1},{1,0},{2,3},{3,2},{4,5},{5,4},{6,7},{7,6},{8,9},{9,8},{10,11... | collective-permute-start | bytes 233480 | tf_op jit(solution)/shard_map/ppermute | solution.py:25
  44.1 16.5 %collective-permute-start.1 = (bf16[304,128]{1,0:T(8,128)(2,1)S(1)}, bf16[304,128]{1,0:T(8,128)(2,1)S(1)}, u32[]{:S(2)}, u32[]{:S(2)}) collective-permute-start(bf16[304,128]{1,0:T(8,128)(2,1)S(1)} %get-tuple-element.23), channel_id=1, source_target_pairs={{0,2},{1,3},{2,0},{3,1},{4,6},{5,7},{6,4},{7,5},{8,10},{9,11},{10,... | collective-permute-start | bytes 233480 | tf_op jit(solution)/shard_map/ppermute | solution.py:25
  44.4 16.2 %collective-permute-start.2 = (bf16[304,128]{1,0:T(8,128)(2,1)S(1)}, bf16[304,128]{1,0:T(8,128)(2,1)S(1)}, u32[]{:S(2)}, u32[]{:S(2)}) collective-permute-start(bf16[304,128]{1,0:T(8,128)(2,1)S(1)} %get-tuple-element.24), channel_id=1, source_target_pairs={{0,3},{1,2},{2,1},{3,0},{4,7},{5,6},{6,5},{7,4},{8,11},{9,10},{10,... | collective-permute-start | bytes 233480 | tf_op jit(solution)/shard_map/ppermute | solution.py:25
  60.5 29.1 %copy-start.1 = (f32[4096]{0:T(1024)S(1)}, f32[4096]{0:T(1024)}, u32[]{:S(2)}) copy-start(f32[4096]{0:T(1024)} %param.9) | copy-start | bytes 49156
  62.3 1.2 %collective-permute-start.16 = (f32[1,4096]{1,0:T(1,128)S(1)}, f32[1,4096]{1,0:T(1,128)S(1)}, u32[]{:S(2)}, u32[]{:S(2)}) collective-permute-start(f32[1,4096]{1,0:T(1,128)S(1)} %gain_terms.1), channel_id=1, source_target_pairs={{0,4},{4,0},{8,12},{12,8},{16,20},{20,16},{24,28},{28,24},{1,5},{5... | collective-permute-start | bytes 49160 | tf_op jit(solution)/shard_map/ppermute | solution.py:25
  63.6 3.8 %collective-permute-start.17 = (f32[1,4096]{1,0:T(1,128)S(1)}, f32[1,4096]{1,0:T(1,128)S(1)}, u32[]{:S(2)}, u32[]{:S(2)}) collective-permute-start(f32[1,4096]{1,0:T(1,128)S(1)} %add.22), channel_id=1, source_target_pairs={{0,8},{4,12},{8,0},{12,4},{16,24},{20,28},{24,16},{28,20},{1,9},{5... | collective-permute-start | bytes 49160 | tf_op jit(solution)/shard_map/ppermute | solution.py:25
  67.4 4.7 %collective-permute-start.18 = (f32[1,4096]{1,0:T(1,128)S(1)}, f32[1,4096]{1,0:T(1,128)S(1)}, u32[]{:S(2)}, u32[]{:S(2)}) collective-permute-start(f32[1,4096]{1,0:T(1,128)S(1)} %add.23), channel_id=1, source_target_pairs={{0,16},{4,20},{8,24},{12,28},{16,0},{20,4},{24,8},{28,12},{1,17},{... | collective-permute-start | bytes 49160 | tf_op jit(solution)/shard_map/ppermute | solution.py:25
  72.1 4.7 %collective-permute-start.19 = (f32[1,4096]{1,0:T(1,128)S(1)}, f32[1,4096]{1,0:T(1,128)S(1)}, u32[]{:S(2)}, u32[]{:S(2)}) collective-permute-start(f32[1,4096]{1,0:T(1,128)S(1)} %add.24), channel_id=1, source_target_pairs={{0,3},{1,2},{2,1},{3,0},{4,5},{5,4},{6,7},{7,6},{8,11},{9,10},{10,... | collective-permute-start | bytes 49160 | tf_op jit(solution)/shard_map/ppermute | solution.py:346
  72.5 4.4 %collective-permute-start.20 = (f32[1,4096]{1,0:T(1,128)S(1)}, f32[1,4096]{1,0:T(1,128)S(1)}, u32[]{:S(2)}, u32[]{:S(2)}) collective-permute-start(f32[1,4096]{1,0:T(1,128)S(1)} %add.24), channel_id=1, source_target_pairs={{4,6},{5,7},{6,4},{7,5},{12,14},{13,15},{14,12},{15,13},{20,22},{2... | collective-permute-start | bytes 49160 | tf_op jit(solution)/shard_map/ppermute | solution.py:347
  76.9 3.6 %collective-permute-start.21 = (f32[1,4096]{1,0:T(1,128)S(1)}, f32[1,4096]{1,0:T(1,128)S(1)}, u32[]{:S(2)}, u32[]{:S(2)}) collective-permute-start(f32[1,4096]{1,0:T(1,128)S(1)} %fusion), channel_id=1, source_target_pairs={{0,4},{4,0},{8,12},{12,8},{16,20},{20,16},{24,28},{28,24},{1,5},{5... | collective-permute-start | bytes 49160 | tf_op jit(solution)/shard_map/ppermute | solution.py:25
  76.9 11.5 %collective-permute-start.10 = (bf16[24,4096]{1,0:T(8,128)(2,1)S(1)}, bf16[24,4096]{1,0:T(8,128)(2,1)S(1)}, u32[]{:S(2)}, u32[]{:S(2)}) collective-permute-start(bf16[24,4096]{1,0:T(8,128)(2,1)S(1)} %get-tuple-element.38.refs_2_), channel_id=1, source_target_pairs={{0,2},{1,3},{2,0},{3,1},{4,6},{5,7},{6,4},{7,5},{8,10},{9,11},{10,... | collective-permute-start | bytes 589832 | tf_op jit(solution)/shard_map/ppermute | solution.py:25
  77.5 11.0 %collective-permute-start.11 = (bf16[24,4096]{1,0:T(8,128)(2,1)S(1)}, bf16[24,4096]{1,0:T(8,128)(2,1)S(1)}, u32[]{:S(2)}, u32[]{:S(2)}) collective-permute-start(bf16[24,4096]{1,0:T(8,128)(2,1)S(1)} %get-tuple-element.39.refs_3_), channel_id=1, source_target_pairs={{0,3},{1,2},{2,1},{3,0},{4,7},{5,6},{6,5},{7,4},{8,11},{9,10},{10,... | collective-permute-start | bytes 589832 | tf_op jit(solution)/shard_map/ppermute | solution.py:25
  79.0 10.7 %collective-permute-start.9 = (bf16[24,4096]{1,0:T(8,128)(2,1)S(1)}, bf16[24,4096]{1,0:T(8,128)(2,1)S(1)}, u32[]{:S(2)}, u32[]{:S(2)}) collective-permute-start(bf16[24,4096]{1,0:T(8,128)(2,1)S(1)} %get-tuple-element.37.refs_1_), channel_id=1, source_target_pairs={{0,1},{1,0},{2,3},{3,2},{4,5},{5,4},{6,7},{7,6},{8,9},{9,8},{10,11... | collective-permute-start | bytes 589832 | tf_op jit(solution)/shard_map/ppermute | solution.py:25
